TPU v7x, 32 devices: a whole 2x2x4 slice. The times are simulated.
32 devices in a mesh: seg: 4 (over y, core), dp: 8 (over z, x).
Axes of the slice: x: 2, y: 2, z: 4, core: 2. Of those that a mesh axis runs over, the one named last changes fastest.
Arguments:
- queries: bfloat16 [8, 512, 2048], P('dp', 'seg'), may hold values from -32 to 32
- keys: bfloat16 [8, 512, 2048], P('dp', 'seg'), may hold values from -6 to 6
- values: bfloat16 [8, 512, 2048], P('dp', 'seg'), may hold values from -6 to 6
- rel_keys: bfloat16 [256, 2048], replicated, may hold values from -6 to 6
- bias_u: float32 [2048], replicated, may hold values from -3 to 3
- bias_v: float32 [2048], replicated, may hold values from -3 to 3
- d_out: bfloat16 [8, 512, 2048], P('dp', 'seg'), may hold values from -6 to 6
Outputs:
- d_queries: bfloat16 [8, 512, 2048], P('dp', 'seg')
- d_keys: bfloat16 [8, 512, 2048], P('dp', 'seg')
- d_rel_keys: float32 [256, 2048], P('seg', 'dp')
- d_bias_u: float32 [2048], replicated
- d_bias_v: float32 [2048], replicated
All inputs are finite; a program needn't handle non-finite values.
Results may differ from a plain program's by a relative error of at most 0.0068.
Values may be sent and summed in bfloat16 or wider, within the bound.
No kernel may reach another device: no remote copies, remote signals or barrier semaphores. Data moves between devices by JAX's collectives and lax.ppermute only.
A program may use at most 64 MiB of HBM per device.

v0:
```python
import jax
import jax.numpy as jnp
from jax import lax
from jax.sharding import PartitionSpec as P

DH = 128


def from_behind(block, axis, distance):
    devices = range(lax.axis_size(axis))
    route = [(i - distance, i) for i in devices if i - distance in devices]
    return lax.ppermute(block, axis, route)


def product(form, left, right):
    return jnp.einsum(form, left, right, preferred_element_type=jnp.float32)


def shift_rel(raw_scores):
    head_count, seg_rows, key_count = raw_scores.shape
    padded = jnp.pad(raw_scores, ((0, 0), (0, 0), (1, 0)))
    folded = padded.reshape(head_count, key_count + 1, seg_rows)[:, 1:, :]
    return folded.reshape(head_count, seg_rows, key_count)


def local_grads(
    query_rows,
    key_local,
    value_local,
    key_memory,
    value_memory,
    rel_keys,
    bias_u,
    bias_v,
    d_out,
    mem_on,
):
    seg_rows = query_rows.shape[0]
    mem_len = key_memory.shape[0]
    key_count = seg_rows + mem_len
    head_count = query_rows.shape[1] // DH
    keys_all = jnp.concatenate([key_memory, key_local], 0).reshape(key_count, head_count, DH)
    values_all = jnp.concatenate([value_memory, value_local], 0).reshape(key_count, head_count, DH)
    rel_heads = rel_keys.reshape(key_count, head_count, DH)
    query_wide = query_rows.astype(jnp.float32)
    q_content = (query_wide + bias_u).astype(jnp.bfloat16).reshape(seg_rows, head_count, DH)
    q_position = (query_wide + bias_v).astype(jnp.bfloat16).reshape(seg_rows, head_count, DH)
    content = product("ihd,jhd->hij", q_content, keys_all)
    position = shift_rel(product("ihd,phd->hip", q_position, rel_heads))
    score_scale = DH ** (-0.5)
    row_index = jnp.arange(seg_rows, dtype=jnp.int32)[:, None]
    key_index = jnp.arange(key_count, dtype=jnp.int32)[None, :]
    allowed = (key_index <= row_index + mem_len) & ((key_index >= mem_len) | mem_on)
    scores = jnp.where(allowed[None], score_scale * (content + position), -1e30)
    row_max = jnp.max(scores, axis=-1, keepdims=True)
    raised = jnp.exp(scores - row_max)
    weights = raised / jnp.sum(raised, axis=-1, keepdims=True)
    d_heads = d_out.reshape(seg_rows, head_count, DH)
    d_weights = product("ihd,jhd->hij", d_heads, values_all)
    centred = d_weights - jnp.sum(weights * d_weights, axis=-1, keepdims=True)
    grad_scores = (score_scale * weights * centred).astype(jnp.bfloat16)
    d_content = product("hij,jhd->ihd", grad_scores, keys_all)
    d_keys = product("hij,ihd->jhd", grad_scores[:, :, mem_len:], q_content)
    zero_raw = jnp.zeros((head_count, seg_rows, key_count), jnp.bfloat16)
    unshift = jax.vjp(shift_rel, zero_raw)[1]
    grad_rel = unshift(grad_scores)[0]
    d_position = product("hip,phd->ihd", grad_rel, rel_heads)
    d_rel = product("hip,ihd->phd", grad_rel, q_position).reshape(key_count, head_count * DH)
    d_query = (d_content + d_position).reshape(seg_rows, head_count * DH).astype(jnp.bfloat16)
    d_key = d_keys.reshape(seg_rows, head_count * DH).astype(jnp.bfloat16)
    return (
        d_query,
        d_key,
        d_rel,
        jnp.sum(d_content, 0).reshape(-1),
        jnp.sum(d_position, 0).reshape(-1),
    )


def shards(queries, keys, values, rel_keys, bias_u, bias_v, d_out):
    seg_rows = queries.shape[1]
    mem_len = rel_keys.shape[0] - seg_rows
    memory = from_behind((keys[0, seg_rows - mem_len :], values[0, seg_rows - mem_len :]), "seg", 1)
    mem_on = lax.axis_index("seg") > 0
    d_query, d_key, d_rel, d_content, d_position = local_grads(
        queries[0],
        keys[0],
        values[0],
        memory[0],
        memory[1],
        rel_keys,
        bias_u,
        bias_v,
        d_out[0],
        mem_on,
    )
    bias_grads = lax.psum((d_content, d_position), ("seg", "dp"))
    shared = lax.psum_scatter(d_rel, "seg", scatter_dimension=0, tiled=True)
    shared = lax.psum_scatter(shared, "dp", scatter_dimension=1, tiled=True)
    return (d_query[None], d_key[None], shared, bias_grads[0], bias_grads[1])


def solution(mesh):
    placed = (
        P("dp", "seg", None),
        P("dp", "seg", None),
        P("dp", "seg", None),
        P(),
        P(),
        P(),
        P("dp", "seg", None),
    )
    return jax.shard_map(
        shards,
        mesh=mesh,
        in_specs=placed,
        out_specs=(P("dp", "seg", None), P("dp", "seg", None), P("seg", "dp"), P(), P()),
        check_vma=False,
    )
```

profile of v0, /device:TPU:0, one launch (start us, length us, event | category | flops | bytes accessed | tf_op | source)
XLA Modules:
  0.0 174.5 jit_solution(12217957348637252360)
XLA Ops:
  7.2 0.0 copy-start.2
  7.2 0.0 copy-start.1
  7.2 0.0 reduce-scatter.3.cloned.1.call-start
  7.2 2.1 %copy.33 = bf16[1,128,2048]{1,2,0:T(8,128)(2,1)} copy(bf16[1,128,2048]{2,1,0:T(8,128)(2,1)} %param.9) | data formatting | bytes 1048576 | tf_op args[2]
  9.4 3.2 %collective-permute-start.1 = (bf16[128,2048]{0,1:T(8,128)(2,1)}, bf16[128,2048]{0,1:T(8,128)(2,1)}, u32[]{:S(2)}, u32[]{:S(2)}) collective-permute-start(bf16[128,2048]{0,1:T(8,128)(2,1)} %bitcast.5), channel_id=1, source_target_pairs={{0,8},{8,16},{16,24},{1,9},{9,17},{17,25},{2,10},{10,18},{18,26},{... | collective-permute-start | bytes 1572872 | tf_op jit(solution)/shard_map/ppermute | solution.py:12
  12.5 2.0 %copy.24 = bf16[1,128,2048]{1,2,0:T(8,128)(2,1)} copy(bf16[1,128,2048]{2,1,0:T(8,128)(2,1)} %param.8) | data formatting | bytes 1048576 | tf_op args[1]
  14.6 0.0 copy-start.3
  14.6 4.7 %collective-permute-start = (bf16[128,2048]{0,1:T(8,128)(2,1)}, bf16[128,2048]{0,1:T(8,128)(2,1)}, u32[]{:S(2)}, u32[]{:S(2)}) collective-permute-start(bf16[128,2048]{0,1:T(8,128)(2,1)} %bitcast), channel_id=1, source_target_pairs={{0,8},{8,16},{16,24},{1,9},{9,17},{17,25},{2,10},{10,18},{18,26},{... | collective-permute-start | bytes 1572872 | tf_op jit(solution)/shard_map/ppermute | solution.py:12
  19.3 0.0 copy-done.2
  19.3 0.2 copy.48
  19.5 0.0 copy-done.1
  19.5 0.5 copy.49
  20.0 0.0 copy-done.3
  20.0 0.8 fusion.15
  20.9 2.6 %pad.12 = f32[16,128,257]{2,1,0:T(8,128)} pad(f32[16,128,256]{2,1,0:T(8,128)S(1)} %fusion.15, f32[]{:T(128)} %constant.4.clone.1), padding=0_0x0_0x1_0 | pad | bytes 4202500 | tf_op jit(solution)/shard_map/jit(_pad)/pad | solution.py:21
  23.4 4.7 %reshape.134 = f32[16,257,128]{2,1,0:T(8,128)} reshape(f32[16,128,257]{2,1,0:T(8,128)} %pad.12) | data formatting | bytes 4210688 | tf_op jit(solution)/shard_map/reshape | solution.py:22
  28.1 3.2 %slice.9 = f32[16,256,128]{2,1,0:T(8,128)} slice(f32[16,257,128]{2,1,0:T(8,128)} %reshape.134), slice={[0:16], [1:257], [0:128]} | slice | bytes 4194304 | tf_op jit(solution)/shard_map/slice | solution.py:22
  31.3 2.9 %reshape.135 = f32[16,128,256]{2,1,0:T(8,128)} reshape(f32[16,256,128]{2,1,0:T(8,128)} %slice.9) | data formatting | bytes 4194304 | tf_op jit(solution)/shard_map/reshape | solution.py:23
  34.2 1.3 copy.36
  35.5 1.1 copy.50
  36.6 2.0 %copy.27 = bf16[128,16,128]{2,0,1:T(8,128)(2,1)} copy(bf16[128,16,128]{0,2,1:T(8,128)(2,1)} %bitcast.2) | data formatting | bytes 1048576 | tf_op jit(solution)/shard_map/concatenate | solution.py:42
  38.7 0.1 fusion.16
  38.8 0.0 collective-permute-done.1
  38.8 2.0 %copy.35 = bf16[128,16,128]{2,0,1:T(8,128)(2,1)} copy(bf16[128,16,128]{0,2,1:T(8,128)(2,1)} %bitcast.6) | data formatting | bytes 1048576 | tf_op jit(solution)/shard_map/concatenate | solution.py:43
  40.8 0.0 collective-permute-done
  40.9 2.0 %copy.26 = bf16[128,16,128]{2,0,1:T(8,128)(2,1)} copy(bf16[128,16,128]{0,2,1:T(8,128)(2,1)} %bitcast.1) | data formatting | bytes 1048576 | tf_op jit(solution)/shard_map/concatenate | solution.py:42
  42.9 0.0 copy-start.4
  42.9 2.8 %fusion.6 = f32[16,256,128]{1,2,0:T(8,128)} fusion(bf16[128,16,128]{2,0,1:T(8,128)(2,1)S(1)} %copy.36, bf16[128,16,128]{2,0,1:T(8,128)(2,1)} %copy.35, bf16[128,16,128]{2,1,0:T(8,128)(2,1)S(1)} %bitcast.45), kind=kOutput, calls=%fused_computation.14 | convolution fusion | flops 136314880 | bytes 3670016 | tf_op jit(solution)/shard_map/ihd,jhd->hij/dot_general | solution.py:16
  45.7 0.0 copy-done.4
  45.7 5.4 %fusion.2 = (f32[16,128]{1,0:T(8,128)S(1)}, f32[16,128,256]{2,1,0:T(8,128)}) fusion(f32[16,256,128]{1,2,0:T(8,128)} %fusion.6, f32[16,128,256]{2,1,0:T(8,128)} %reshape.135, pred[128,256]{1,0:T(8,128)(4,1)S(1)} %fusion.16, bf16[128,16,128]{2,0,1:T(8,128)(2,1)} %copy.27, bf16[128,16,128]{2,0,1:T(8,128)(2,1)} %copy.26, f32[128,16,128]{0,2,1:T(8,128)S(1)} %bitcast.39, ...), kind=kOutput, calls=%fused_computation.4 | convolution fusion | flops 140511744 | bytes 8437760 | tf_op jit(solution)/shard_map/div | solution.py:57
  51.2 2.6 %fusion.4 = bf16[16,128,256]{2,1,0:T(8,128)(2,1)S(1)} fusion(f32[16,256,128]{1,2,0:T(8,128)} %fusion.6, f32[16,128,256]{2,1,0:T(8,128)} %get-tuple-element.21, f32[16,128]{1,0:T(8,128)S(1)} %get-tuple-element.20), kind=kLoop, calls=%fused_computation.6 | loop fusion | flops 2097152 | bytes 5251072 | tf_op jit(solution)/shard_map/convert_element_type | solution.py:61
  53.7 1.2 reshape.136
  54.9 2.5 %pad.13 = bf16[16,257,128]{2,1,0:T(8,128)(2,1)} pad(bf16[16,256,128]{2,1,0:T(8,128)(2,1)} %reshape.136, bf16[]{:T(256)} %constant.22.clone.1), padding=0_0x1_0x0_0 | pad | bytes 2101250 | tf_op jit(solution)/shard_map/transpose(jvp())/pad | solution.py:22
  57.4 5.0 %reshape.137 = bf16[16,128,257]{2,1,0:T(8,128)(2,1)} reshape(bf16[16,257,128]{2,1,0:T(8,128)(2,1)} %pad.13) | data formatting | bytes 2105344 | tf_op jit(solution)/shard_map/transpose(jvp())/reshape | solution.py:22
  62.5 3.6 %fusion.10 = f32[16,128,256]{2,1,0:T(8,128)} fusion(bf16[16,128,257]{2,1,0:T(8,128)(2,1)} %reshape.137, f32[128,16,128]{0,2,1:T(8,128)S(1)} %bitcast.40, f32[16,128]{1,0:T(8,128)S(1)} %bitcast.50), kind=kOutput, calls=%fused_computation.21 | convolution fusion | flops 134742016 | bytes 4202496 | tf_op jit(solution)/shard_map/hip,ihd->phd/dot_general | solution.py:16
  66.1 2.9 %copy.41 = f32[256,2048]{1,0:T(8,128)} copy(f32[256,2048]{0,1:T(8,128)} %bitcast.44) | data formatting | bytes 4194304 | tf_op jit(solution)/shard_map/reshape | solution.py:68
  68.9 0.0 reduce-scatter.3.cloned.1.call-update
  69.0 0.2 reduce-scatter.5.cloned.1.call-start
  69.2 31.7 %reduce-scatter.3.cloned.1.call-done = f32[64,2048]{1,0:T(8,128)} async-done(((f32[256,2048]{1,0:T(8,128)}), f32[64,2048]{1,0:T(8,128)}) %reduce-scatter.3.cloned.1.call-update) | async-done | bytes 524304 | tf_op jit(solution)/shard_map/reduce_scatter | solution.py:98
  100.8 0.0 reduce-scatter.5.cloned.1.call-update
  100.9 0.0 copy-start
  100.9 1.8 %convolution_bitcast_fusion.1 = f32[128,16,128]{0,2,1:T(8,128)S(1)} fusion(bf16[16,128,256]{2,1,0:T(8,128)(2,1)S(1)} %fusion.4, bf16[128,16,128]{2,0,1:T(8,128)(2,1)} %copy.27, bf16[128,16,128]{2,0,1:T(8,128)(2,1)} %copy.26), kind=kOutput, calls=%fused_computation.11 | convolution fusion | flops 136314880 | bytes 3145728 | tf_op jit(solution)/shard_map/hij,jhd->ihd/dot_general | solution.py:16
  102.7 0.0 copy-done
  102.7 1.4 fusion.21
  104.0 2.0 %copy.42 = bf16[1,128,2048]{2,1,0:T(8,128)(2,1)} copy(bf16[1,128,2048]{1,2,0:T(8,128)(2,1)} %bitcast.46) | data formatting | bytes 1048576
  106.1 0.5 convolution_convert_fusion
  106.5 1.0 copy.43
  107.6 39.6 %all-reduce.2 = (f32[2048]{0:T(1024)}, f32[2048]{0:T(1024)}) all-reduce(f32[2048]{0:T(1024)S(1)} %bitcast.52, f32[2048]{0:T(1024)S(1)} %bitcast.51), channel_id=1, replica_groups=mesh['seg'=4,'dp'=8] {'seg','dp'}, use_global_device_ids=true, to_apply=%region_6.7 | all-reduce | flops 4096 | bytes 32768 | tf_op jit(solution)/shard_map/psum | solution.py:97
  147.2 20.5 %reduce-scatter.5.cloned.1.call-done = f32[64,256]{1,0:T(8,128)} async-done(((f32[64,2048]{1,0:T(8,128)}), f32[64,256]{1,0:T(8,128)}) %reduce-scatter.5.cloned.1.call-update) | async-done | bytes 65552 | tf_op jit(solution)/shard_map/reduce_scatter | solution.py:99
  (2 shorter events, 0.0 us)
Async XLA Ops:
  7.2 12.1 %copy-start.2 = (bf16[1,128,2048]{2,1,0:T(8,128)(2,1)S(1)}, bf16[1,128,2048]{2,1,0:T(8,128)(2,1)}, u32[]{:S(2)}) copy-start(bf16[1,128,2048]{2,1,0:T(8,128)(2,1)} %param.7) | copy-start | bytes 1572868
  7.2 12.3 %copy-start.1 = (bf16[256,2048]{1,0:T(8,128)(2,1)S(1)}, bf16[256,2048]{1,0:T(8,128)(2,1)}, u32[]{:S(2)}) copy-start(bf16[256,2048]{1,0:T(8,128)(2,1)} %param.10) | copy-start | bytes 3145732
  7.2 93.7 %reduce-scatter.3.cloned.1.call-start = ((), (), s32[]{:S(2)}) async-start(), calls=%async_computation.2 | async-start | bytes 2621440 | tf_op jit(solution)/shard_map/reduce_scatter | solution.py:98
  9.4 29.4 %collective-permute-start.1 = (bf16[128,2048]{0,1:T(8,128)(2,1)}, bf16[128,2048]{0,1:T(8,128)(2,1)}, u32[]{:S(2)}, u32[]{:S(2)}) collective-permute-start(bf16[128,2048]{0,1:T(8,128)(2,1)} %bitcast.5), channel_id=1, source_target_pairs={{0,8},{8,16},{16,24},{1,9},{9,17},{17,25},{2,10},{10,18},{18,26},{... | collective-permute-start | bytes 1572872 | tf_op jit(solution)/shard_map/ppermute | solution.py:12
  14.6 5.4 %copy-start.3 = (f32[2048]{0:T(1024)S(1)}, f32[2048]{0:T(1024)}, u32[]{:S(2)}) copy-start(f32[2048]{0:T(1024)} %param.12) | copy-start | bytes 24580
  14.6 26.3 %collective-permute-start = (bf16[128,2048]{0,1:T(8,128)(2,1)}, bf16[128,2048]{0,1:T(8,128)(2,1)}, u32[]{:S(2)}, u32[]{:S(2)}) collective-permute-start(bf16[128,2048]{0,1:T(8,128)(2,1)} %bitcast), channel_id=1, source_target_pairs={{0,8},{8,16},{16,24},{1,9},{9,17},{17,25},{2,10},{10,18},{18,26},{... | collective-permute-start | bytes 1572872 | tf_op jit(solution)/shard_map/ppermute | solution.py:12
  42.9 2.8 %copy-start.4 = (f32[2048]{0:T(1024)S(1)}, f32[2048]{0:T(1024)}, u32[]{:S(2)}) copy-start(f32[2048]{0:T(1024)} %param.11) | copy-start | bytes 24580
  69.0 98.7 %reduce-scatter.5.cloned.1.call-start = ((), (), s32[]{:S(2)}) async-start(), calls=%async_computation.3 | async-start | bytes 589824 | tf_op jit(solution)/shard_map/reduce_scatter | solution.py:99
  100.9 1.8 %copy-start = (bf16[16,128,257]{2,1,0:T(8,128)(2,1)S(1)}, bf16[16,128,257]{2,1,0:T(8,128)(2,1)}, u32[]{:S(2)}) copy-start(bf16[16,128,257]{2,1,0:T(8,128)(2,1)} %reshape.137) | copy-start | bytes 3158020
Sparse Core Ops, SparseCore 0:
  69.1 31.7 reduce-scatter.2
  105.1 62.5 reduce-scatter.4
where the time goes:
time: 175 us
  waiting for transfers between devices  52.2 us (30%)
  local copies, waits for them, and re-layouts  41.5 us (24%)
  blocking collectives  39.6 us (23%)
  matrix products  16.3 us (9%)
  between operations  14.2 us (8%)
  starting transfers between devices  8.1 us (5%)
  other arithmetic  2.66 us (2%)
    psum x1, blocking collectives, shards(): bias_grads = lax.psum((d_content, d_position), ('seg', 'dp'))  39.6 us
    reduce_scatter x1, waiting for transfers between devices, shards(): shared = lax.psum_scatter(d_rel, 'seg', scatter_dimension=0, tiled=True)  31.7 us
    reduce_scatter x1, waiting for transfers between devices, shards(): shared = lax.psum_scatter(shared, 'dp', scatter_dimension=1, tiled=True)  20.5 us
    dot_general x6, matrix products, product(): return jnp.einsum(form, left, right, preferred_element_type=jnp.float32)  10.9 us
    reshape x2, local copies, waits for them, and re-layouts, shift_rel(): folded = padded.reshape(head_count, key_count + 1, seg_rows)[:, 1:, :]  9.72 us
    unnamed x15, local copies, waits for them, and re-layouts  8.4 us
    ppermute x2, starting transfers between devices, from_behind(): return lax.ppermute(block, axis, route)  7.84 us
    div x1, matrix products, local_grads(): weights = raised / jnp.sum(raised, axis=-1, keepdims=True)  5.43 us
  transfers between devices with their start and end apart: 4, of which 2 were waited for; matrix products, arithmetic and copies ran while one was open for 17% of the time, Pallas kernels for 0%

commit v1 on v0

v1 whole, which is shorter than its diff:
```python
import jax
import jax.numpy as jnp
from jax import lax
from jax.experimental import pallas as pl
from jax.experimental.pallas import tpu as pltpu
from jax.sharding import PartitionSpec as P

DH = 128
HEADS_PER_STEP = 4
BIAS_ROWS = 16
DIRECT_PEERS = 8


def contract(left, right, left_dim, right_dim):
    return lax.dot_general(
        left,
        right,
        (((left_dim,), (right_dim,)), ((), ())),
        preferred_element_type=jnp.float32,
    )


def attention_kernel(
    q_ref,
    k_ref,
    v_ref,
    k_mem_ref,
    v_mem_ref,
    rel_ref,
    bias_u_ref,
    bias_v_ref,
    d_out_ref,
    d_q_ref,
    d_k_ref,
    keep_ref,
    send_ref,
    bias_ref,
):
    seg_rows = q_ref.shape[0]
    mem_len = k_mem_ref.shape[0]
    key_count = seg_rows + mem_len
    pair_count, part_rows, _ = keep_ref.shape
    seg_index = lax.axis_index("seg")
    first_key = jnp.where(seg_index > 0, 0, mem_len)
    odd = jnp.bitwise_and(seg_index, 1) == 1
    row_index = lax.broadcasted_iota(jnp.int32, (seg_rows, key_count), 0)
    key_index = lax.broadcasted_iota(jnp.int32, (seg_rows, key_count), 1)
    allowed = (key_index <= row_index + mem_len) & (key_index >= first_key)
    mirror_row = lax.broadcasted_iota(jnp.int32, (key_count, key_count), 0)
    mirror_col = lax.broadcasted_iota(jnp.int32, (key_count, key_count), 1)
    mirror = (mirror_row + mirror_col == key_count - 1).astype(jnp.bfloat16)
    score_scale = DH ** (-0.5)
    for head in range(q_ref.shape[1] // DH):
        cols = slice(head * DH, (head + 1) * DH)
        query_wide = q_ref[:, cols].astype(jnp.float32)
        q_content = (query_wide + bias_u_ref[:, cols]).astype(jnp.bfloat16)
        q_position = (query_wide + bias_v_ref[:, cols]).astype(jnp.bfloat16)
        keys_all = jnp.concatenate([k_mem_ref[:, cols], k_ref[:, cols]], 0)
        values_all = jnp.concatenate([v_mem_ref[:, cols], v_ref[:, cols]], 0)
        rel = rel_ref[:, cols]
        content = contract(q_content, keys_all, 1, 1)
        by_distance = contract(q_position, rel, 1, 1)
        position = pltpu.roll(by_distance, key_count - seg_rows + 1, 1, stride=1, stride_axis=0)
        scores = jnp.where(allowed, score_scale * (content + position), -1e30)
        raised = jnp.exp(scores - jnp.max(scores, axis=1, keepdims=True))
        weights = raised / jnp.sum(raised, axis=1, keepdims=True)
        d_weights = contract(d_out_ref[:, cols], values_all, 1, 1)
        centred = d_weights - jnp.sum(weights * d_weights, axis=1, keepdims=True)
        grad_scores = (score_scale * weights * centred).astype(jnp.bfloat16)
        mirrored = pltpu.roll(
            contract(grad_scores, mirror, 1, 0), key_count - seg_rows + 1, 1, stride=1, stride_axis=0
        )
        grad_rel = contract(mirrored.astype(jnp.bfloat16), mirror, 1, 0).astype(jnp.bfloat16)
        d_content = contract(grad_scores, keys_all, 1, 0)
        d_position = contract(grad_rel, rel, 1, 0)
        d_q_ref[:, cols] = (d_content + d_position).astype(jnp.bfloat16)
        d_k_ref[:, cols] = contract(grad_scores[:, mem_len:], q_content, 0, 0).astype(jnp.bfloat16)
        d_rel = contract(grad_rel, q_position, 0, 0)
        sums = jnp.concatenate(
            [jnp.sum(d_content, 0, keepdims=True), jnp.sum(d_position, 0, keepdims=True)], 0
        )
        bias_ref[:, cols] = sums
        high = sums.astype(jnp.bfloat16)
        low = (sums - high.astype(jnp.float32)).astype(jnp.bfloat16)
        fill = jnp.zeros((BIAS_ROWS - 4, DH), jnp.bfloat16)
        for pair in range(pair_count):
            start = 2 * pair * part_rows
            even_part = d_rel[start : start + part_rows]
            odd_part = d_rel[start + part_rows : start + 2 * part_rows]
            keep_ref[pair, :, cols] = jnp.where(odd, odd_part, even_part)
            send_ref[pair * part_rows : (pair + 1) * part_rows, cols] = jnp.where(
                odd, even_part, odd_part
            ).astype(jnp.bfloat16)
        send_ref[pair_count * part_rows :, cols] = jnp.concatenate([high, low, fill], 0)


def attention(queries, keys, values, key_memory, value_memory, rel_keys, bias_u, bias_v, d_out):
    seg_rows, width = queries.shape
    key_count = rel_keys.shape[0]
    seg_count = lax.axis_size("seg")
    pair_count = seg_count // 2
    part_rows = key_count // seg_count
    span = HEADS_PER_STEP * DH

    def block(rows):
        return pl.BlockSpec((rows, span), lambda step: (0, step))

    rows_in = [seg_rows] * 3 + [key_count - seg_rows] * 2 + [key_count, 1, 1, seg_rows]
    send_rows = pair_count * part_rows + BIAS_ROWS
    return pl.pallas_call(
        attention_kernel,
        name="attention_grads",
        grid=(width // span,),
        in_specs=[block(rows) for rows in rows_in],
        out_specs=[
            block(seg_rows),
            block(seg_rows),
            pl.BlockSpec((pair_count, part_rows, span), lambda step: (0, 0, step)),
            block(send_rows),
            block(2),
        ],
        out_shape=[
            jax.ShapeDtypeStruct((seg_rows, width), jnp.bfloat16),
            jax.ShapeDtypeStruct((seg_rows, width), jnp.bfloat16),
            jax.ShapeDtypeStruct((pair_count, part_rows, width), jnp.float32),
            jax.ShapeDtypeStruct((send_rows, width), jnp.bfloat16),
            jax.ShapeDtypeStruct((2, width), jnp.float32),
        ],
        compiler_params=pltpu.CompilerParams(
            dimension_semantics=("arbitrary",), vmem_limit_bytes=48 * 1024 * 1024
        ),
    )(
        queries,
        keys,
        values,
        key_memory,
        value_memory,
        rel_keys,
        bias_u[None],
        bias_v[None],
        d_out,
    )


def from_behind(block, axis, distance):
    devices = range(lax.axis_size(axis))
    route = [(i - distance, i) for i in devices if i - distance in devices]
    return lax.ppermute(block, axis, route)


def swap(block, axis, flip):
    return lax.ppermute(block, axis, [(i, i ^ flip) for i in range(lax.axis_size(axis))])


def bit_of(axis, flip):
    return (lax.axis_index(axis) // flip) % 2


def split_bias(sums):
    high = sums.astype(jnp.bfloat16)
    return high, (sums - high.astype(jnp.float32)).astype(jnp.bfloat16)


def add_packed(keep, sums, packed):
    rows = keep.shape[0] * keep.shape[1]
    partial = packed[:rows].astype(jnp.float32).reshape(keep.shape)
    halves = packed[rows : rows + 4].astype(jnp.float32)
    return keep + partial, sums + (halves[:2] + halves[2:])


def reduce_rel(keep, packed, sums):
    seg_count = lax.axis_size("seg")
    width = keep.shape[2]
    part_rows = keep.shape[1]
    partial, sums = add_packed(keep, sums, swap(packed, "seg", 1))
    flip = 2
    while flip < seg_count:
        parts = partial.reshape(partial.shape[0] // 2, 2, part_rows, width)
        mine = bit_of("seg", flip)
        keep = lax.dynamic_index_in_dim(parts, mine, 1, keepdims=False)
        other = lax.dynamic_index_in_dim(parts, 1 - mine, 1, keepdims=False)
        high, low = split_bias(sums)
        fill = jnp.zeros((BIAS_ROWS - 4, width), jnp.bfloat16)
        packed = jnp.concatenate(
            [other.astype(jnp.bfloat16).reshape(-1, width), high, low, fill], 0
        )
        partial, sums = add_packed(keep, sums, swap(packed, "seg", flip))
        flip *= 2
    partial = partial[0]
    dp_count = lax.axis_size("dp")
    flip = dp_count // 2
    while 2 * flip > DIRECT_PEERS:
        half = partial.shape[1] // 2
        mine = bit_of("dp", flip)
        keep = lax.dynamic_slice_in_dim(partial, mine * half, half, 1)
        other = lax.dynamic_slice_in_dim(partial, (1 - mine) * half, half, 1)
        partial = keep + swap(other.astype(jnp.bfloat16), "dp", flip).astype(jnp.float32)
        sums = sums + swap(sums, "dp", flip)
        flip //= 2
    peers = 2 * flip
    place = lax.axis_index("dp") % peers
    cols = partial.shape[1] // peers
    high, low = split_bias(sums)
    tail = jnp.concatenate([high.reshape(-1, cols), low.reshape(-1, cols)], 0)
    total = lax.dynamic_slice_in_dim(partial, place * cols, cols, 1)
    for distance in range(1, peers):
        other = lax.dynamic_slice_in_dim(partial, (place ^ distance) * cols, cols, 1)
        packed = jnp.concatenate([other.astype(jnp.bfloat16), tail], 0)
        packed = swap(packed, "dp", distance).astype(jnp.float32)
        total = total + packed[:part_rows]
        halves = packed[part_rows:].reshape(2, 2, width)
        sums = sums + (halves[0] + halves[1])
    return total, sums


def shards(queries, keys, values, rel_keys, bias_u, bias_v, d_out):
    seg_rows = queries.shape[1]
    mem_len = rel_keys.shape[0] - seg_rows
    key_memory = from_behind(keys[0, seg_rows - mem_len :], "seg", 1)
    value_memory = from_behind(values[0, seg_rows - mem_len :], "seg", 1)
    d_query, d_key, keep, packed, sums = attention(
        queries[0],
        keys[0],
        values[0],
        key_memory,
        value_memory,
        rel_keys,
        bias_u,
        bias_v,
        d_out[0],
    )
    total, sums = reduce_rel(keep, packed, sums)
    return (d_query[None], d_key[None], total, sums[0], sums[1])


def solution(mesh):
    placed = (
        P("dp", "seg", None),
        P("dp", "seg", None),
        P("dp", "seg", None),
        P(),
        P(),
        P(),
        P("dp", "seg", None),
    )
    return jax.shard_map(
        shards,
        mesh=mesh,
        in_specs=placed,
        out_specs=(P("dp", "seg", None), P("dp", "seg", None), P("seg", "dp"), P(), P()),
        check_vma=False,
    )
```

time: 175 us -> 68.2 us (0.39)
  blocking collectives: 39.6 us -> 0 us
  waiting for transfers between devices: 52.2 us -> 14.7 us
  local copies, waits for them, and re-layouts: 41.5 us -> 7.05 us
  starting transfers between devices: 8.1 us -> 29.4 us
  matrix products: 16.3 us -> 0 us
  Pallas kernels: 0 us -> 14.6 us
  between operations: 14.2 us -> 0.89 us
    reduce_scatter x2 -> x0, waiting for transfers between devices: 52.2 us -> none  [the longest x1 31.7 us: shards(): shared = lax.psum_scatter(d_rel, 'seg', scatter_dimension=0, tiled=True)]
    psum x1 -> x0, blocking collectives: 39.6 us -> none  [shards(): bias_grads = lax.psum((d_content, d_position), ('seg', 'dp'))]
    ppermute x0 -> x9, starting transfers between devices: none -> 22.4 us  [swap(): lax.ppermute(block, axis, [(i, i ^ flip) for i in range(lax.axis_size(axi...]
    reshape x6 -> x3, local copies, waits for them, and re-layouts: 17.2 us -> 0.07 us  [the longest x1 0.04 us: reduce_rel(): other.astype(jnp.bfloat16).reshape(-1, width)]
    pallas_call x0 -> x1, Pallas kernels: none -> 14.6 us  [attention(): pl.pallas_call(attention_kernel, name='attention_grads', grid=(width // s...]
    ppermute x0 -> x9, waiting for transfers between devices: none -> 13 us  [swap(): lax.ppermute(block, axis, [(i, i ^ flip) for i in range(lax.axis_size(axi...]
    dot_general x6 -> x0, matrix products: 10.9 us -> none  [product(): return jnp.einsum(form, left, right, preferred_element_type=jnp.float32)]
    concatenate x4 -> x1, local copies, waits for them, and re-layouts: 7.43 us -> 0.08 us  [reduce_rel(): jnp.concatenate([other.astype(jnp.bfloat16).reshape(-1, width), high, low...]
  transfers between devices with their start and end apart: 4 -> 11, of which waited for: 2 -> 7; matrix products, arithmetic and copies ran while one was open for 17% -> 0% of each run, Pallas kernels for 0% -> 0%
where the time goes in v1:
time: 68.2 us; the launch traced here: 67.8 us
  starting transfers between devices  29.4 us (43%)
  waiting for transfers between devices  14.7 us (22%)
  Pallas kernels  14.6 us (21%)
  local copies, waits for them, and re-layouts  7.05 us (10%)
  other arithmetic  1.17 us (2%)
  between operations  0.89 us (1%)
    ppermute x9, starting transfers between devices, swap(): lax.ppermute(block, axis, [(i, i ^ flip) for i in range(lax.axis_size(axi...  22.4 us
    pallas_call x1, Pallas kernels, attention(): pl.pallas_call(attention_kernel, name='attention_grads', grid=(width // s...  14.6 us
    ppermute x9, waiting for transfers between devices, swap(): lax.ppermute(block, axis, [(i, i ^ flip) for i in range(lax.axis_size(axi...  13 us
    ppermute x2, starting transfers between devices, from_behind(): return lax.ppermute(block, axis, route)  6.93 us
    unnamed x14, local copies, waits for them, and re-layouts  6.09 us
    ppermute x2, waiting for transfers between devices, from_behind(): return lax.ppermute(block, axis, route)  1.69 us
  transfers between devices with their start and end apart: 11, of which 7 were waited for; matrix products, arithmetic and copies ran while one was open for 0% of the time, Pallas kernels for 0%

profile of v1, /device:TPU:0, one launch (start us, length us, event | category | flops | bytes accessed | tf_op | source)
XLA Modules:
  0.0 67.8 jit_solution(2959743934995870608)
XLA Ops:
  0.6 0.0 copy-start.5
  0.6 2.4 %collective-permute-start = (bf16[128,2048]{1,0:T(8,128)(2,1)}, bf16[128,2048]{1,0:T(8,128)(2,1)S(1)}, u32[]{:S(2)}, u32[]{:S(2)}) collective-permute-start(bf16[128,2048]{1,0:T(8,128)(2,1)} %bitcast.17), channel_id=1, source_target_pairs={{0,8},{8,16},{16,24},{1,9},{9,17},{17,25},{2,10},{10,18},{18,26},{... | collective-permute-start | bytes 1572872 | tf_op jit(solution)/shard_map/ppermute | solution.py:148
  3.0 4.5 %collective-permute-start.1 = (bf16[128,2048]{1,0:T(8,128)(2,1)}, bf16[128,2048]{1,0:T(8,128)(2,1)S(1)}, u32[]{:S(2)}, u32[]{:S(2)}) collective-permute-start(bf16[128,2048]{1,0:T(8,128)(2,1)} %bitcast.19), channel_id=1, source_target_pairs={{0,8},{8,16},{16,24},{1,9},{9,17},{17,25},{2,10},{10,18},{18,26},{... | collective-permute-start | bytes 1572872 | tf_op jit(solution)/shard_map/ppermute | solution.py:148
  7.6 0.0 collective-permute-done.k_mem_ref
  7.6 1.7 %collective-permute-done.1.v_mem_ref = bf16[128,2048]{1,0:T(8,128)(2,1)S(1)} collective-permute-done((bf16[128,2048]{1,0:T(8,128)(2,1)}, bf16[128,2048]{1,0:T(8,128)(2,1)S(1)}, u32[]{:S(2)}, u32[]{:S(2)}) %collective-permute-start.1) | collective-permute-done | bytes 524320 | tf_op jit(solution)/shard_map/ppermute | solution.py:148
  9.3 0.0 copy-done.5
  9.3 0.0 copy-start
  9.3 1.2 %copy-done = bf16[256,2048]{1,0:T(8,128)(2,1)S(1)} copy-done((bf16[256,2048]{1,0:T(8,128)(2,1)S(1)}, bf16[256,2048]{1,0:T(8,128)(2,1)}, u32[]{:S(2)}) %copy-start) | copy-done | bytes 1048600
  10.5 0.0 copy-start.1
  10.5 1.0 %copy-done.1 = bf16[1,128,2048]{2,1,0:T(8,128)(2,1)S(1)} copy-done((bf16[1,128,2048]{2,1,0:T(8,128)(2,1)S(1)}, bf16[1,128,2048]{2,1,0:T(8,128)(2,1)}, u32[]{:S(2)}) %copy-start.1) | copy-done | bytes 524312
  11.6 0.0 copy-start.2
  11.6 1.0 %copy-done.2 = bf16[1,128,2048]{2,1,0:T(8,128)(2,1)S(1)} copy-done((bf16[1,128,2048]{2,1,0:T(8,128)(2,1)S(1)}, bf16[1,128,2048]{2,1,0:T(8,128)(2,1)}, u32[]{:S(2)}) %copy-start.2) | copy-done | bytes 524312
  12.6 0.0 copy-start.3
  12.6 1.0 %copy-done.3 = bf16[1,128,2048]{2,1,0:T(8,128)(2,1)S(1)} copy-done((bf16[1,128,2048]{2,1,0:T(8,128)(2,1)S(1)}, bf16[1,128,2048]{2,1,0:T(8,128)(2,1)}, u32[]{:S(2)}) %copy-start.3) | copy-done | bytes 524312
  13.6 0.0 copy-start.4
  13.6 1.0 %copy-done.4 = bf16[1,128,2048]{2,1,0:T(8,128)(2,1)S(1)} copy-done((bf16[1,128,2048]{2,1,0:T(8,128)(2,1)S(1)}, bf16[1,128,2048]{2,1,0:T(8,128)(2,1)}, u32[]{:S(2)}) %copy-start.4) | copy-done | bytes 524312
  14.7 0.0 copy-start.6
  14.7 0.7 %copy-done.6 = f32[2048]{0:T(1024)S(1)} copy-done((f32[2048]{0:T(1024)S(1)}, f32[2048]{0:T(1024)}, u32[]{:S(2)}) %copy-start.6) | copy-done | bytes 8216
  15.4 14.6 %attention_grads.1 = (bf16[128,2048]{1,0:T(8,128)(2,1)}, bf16[128,2048]{1,0:T(8,128)(2,1)}, f32[2,64,2048]{2,1,0:T(8,128)S(1)}, bf16[144,2048]{1,0:T(8,128)(2,1)S(1)}, f32[2,2048]{1,0:T(2,128)S(1)}) custom-call(bf16[128,2048]{1,0:T(8,128)(2,1)S(1)} %bitcast.16, bf16[128,2048]{1,0:T(8,128)(2,1)S(1)} %bitcast.18, bf16[128,2048]{1,0:T(8,128)(2,1)S(1)} %bitcast.20, ...), custom_call_target="tpu_custom_call" | custom-call | tf_op jit(solution)/shard_map/attention_grads/pallas_call | solution.py:110
  30.0 8.4 %collective-permute-start.2 = (bf16[144,2048]{1,0:T(8,128)(2,1)S(1)}, bf16[144,2048]{1,0:T(8,128)(2,1)S(1)}, u32[]{:S(2)}, u32[]{:S(2)}) collective-permute-start(bf16[144,2048]{1,0:T(8,128)(2,1)S(1)} %get-tuple-element.13), channel_id=1, source_target_pairs={{0,8},{8,0},{16,24},{24,16},{1,9},{9,1},{17,25},{25,17},{2,10},{10... | collective-permute-start | bytes 1769480 | tf_op jit(solution)/shard_map/ppermute | solution.py:152
  38.4 0.1 pad.24.clone
  38.5 1.5 %collective-permute-done.2 = bf16[144,2048]{1,0:T(8,128)(2,1)S(1)} collective-permute-done((bf16[144,2048]{1,0:T(8,128)(2,1)S(1)}, bf16[144,2048]{1,0:T(8,128)(2,1)S(1)}, u32[]{:S(2)}, u32[]{:S(2)}) %collective-permute-start.2) | collective-permute-done | bytes 589856 | tf_op jit(solution)/shard_map/ppermute | solution.py:152
  40.1 0.1 convert_add_fusion
  40.3 0.1 maximum_maximum_fusion
  40.4 2.7 %collective-permute-start.3 = (bf16[80,2048]{1,0:T(8,128)(2,1)S(1)}, bf16[80,2048]{1,0:T(8,128)(2,1)S(1)}, u32[]{:S(2)}, u32[]{:S(2)}) collective-permute-start(bf16[80,2048]{1,0:T(8,128)(2,1)S(1)} %maximum_maximum_fusion), channel_id=1, source_target_pairs={{0,16},{8,24},{16,0},{24,8},{1,17},{9,25},{17,1},{25,9},{2,18},{10... | collective-permute-start | bytes 983048 | tf_op jit(solution)/shard_map/ppermute | solution.py:152
  43.1 8.0 %collective-permute-done.3 = bf16[80,2048]{1,0:T(8,128)(2,1)S(1)} collective-permute-done((bf16[80,2048]{1,0:T(8,128)(2,1)S(1)}, bf16[80,2048]{1,0:T(8,128)(2,1)S(1)}, u32[]{:S(2)}, u32[]{:S(2)}) %collective-permute-start.3) | collective-permute-done | bytes 327712 | tf_op jit(solution)/shard_map/ppermute | solution.py:152
  51.2 0.1 bitcast_add_fusion
  51.2 0.1 dynamic-slice_convert_fusion.7
  51.3 4.6 %collective-permute-start.10 = (bf16[96,256]{1,0:T(8,128)(2,1)S(1)}, bf16[96,256]{1,0:T(8,128)(2,1)S(1)}, u32[]{:S(2)}, u32[]{:S(2)}) collective-permute-start(bf16[96,256]{1,0:T(8,128)(2,1)S(1)} %pad_maximum_fusion), channel_id=1, source_target_pairs={{0,7},{1,6},{2,5},{3,4},{4,3},{5,2},{6,1},{7,0},{8,15},{9,14},{10,... | collective-permute-start | bytes 147464 | tf_op jit(solution)/shard_map/ppermute | solution.py:152
  55.9 0.3 collective-permute-start.9
  56.2 0.8 %collective-permute-start.8 = (bf16[96,256]{1,0:T(8,128)(2,1)S(1)}, bf16[96,256]{1,0:T(8,128)(2,1)S(1)}, u32[]{:S(2)}, u32[]{:S(2)}) collective-permute-start(bf16[96,256]{1,0:T(8,128)(2,1)S(1)} %get-tuple-element.34), channel_id=1, source_target_pairs={{0,5},{1,4},{2,7},{3,6},{4,1},{5,0},{6,3},{7,2},{8,13},{9,12},{10,... | collective-permute-start | bytes 147464 | tf_op jit(solution)/shard_map/ppermute | solution.py:152
  57.0 2.1 %collective-permute-start.7 = (bf16[96,256]{1,0:T(8,128)(2,1)S(1)}, bf16[96,256]{1,0:T(8,128)(2,1)S(1)}, u32[]{:S(2)}, u32[]{:S(2)}) collective-permute-start(bf16[96,256]{1,0:T(8,128)(2,1)S(1)} %get-tuple-element.33), channel_id=1, source_target_pairs={{0,4},{1,5},{2,6},{3,7},{4,0},{5,1},{6,2},{7,3},{8,12},{9,13},{10,... | collective-permute-start | bytes 147464 | tf_op jit(solution)/shard_map/ppermute | solution.py:152
  59.1 2.2 %collective-permute-start.6 = (bf16[96,256]{1,0:T(8,128)(2,1)S(1)}, bf16[96,256]{1,0:T(8,128)(2,1)S(1)}, u32[]{:S(2)}, u32[]{:S(2)}) collective-permute-start(bf16[96,256]{1,0:T(8,128)(2,1)S(1)} %get-tuple-element.32), channel_id=1, source_target_pairs={{0,3},{1,2},{2,1},{3,0},{4,7},{5,6},{6,5},{7,4},{8,11},{9,10},{10,... | collective-permute-start | bytes 147464 | tf_op jit(solution)/shard_map/ppermute | solution.py:152
  61.3 0.0 collective-permute-done.10
  61.3 0.8 %collective-permute-start.5 = (bf16[96,256]{1,0:T(8,128)(2,1)S(1)}, bf16[96,256]{1,0:T(8,128)(2,1)S(1)}, u32[]{:S(2)}, u32[]{:S(2)}) collective-permute-start(bf16[96,256]{1,0:T(8,128)(2,1)S(1)} %get-tuple-element.31), channel_id=1, source_target_pairs={{0,2},{1,3},{2,0},{3,1},{4,6},{5,7},{6,4},{7,5},{8,10},{9,11},{10,... | collective-permute-start | bytes 147464 | tf_op jit(solution)/shard_map/ppermute | solution.py:152
  62.1 0.0 collective-permute-done.9
  62.1 0.6 collective-permute-start.4
  62.7 1.2 %collective-permute-done.8 = bf16[96,256]{1,0:T(8,128)(2,1)S(1)} collective-permute-done((bf16[96,256]{1,0:T(8,128)(2,1)S(1)}, bf16[96,256]{1,0:T(8,128)(2,1)S(1)}, u32[]{:S(2)}, u32[]{:S(2)}) %collective-permute-start.8) | collective-permute-done | bytes 49184 | tf_op jit(solution)/shard_map/ppermute | solution.py:152
  63.9 0.0 collective-permute-done.7
  64.0 1.0 %collective-permute-done.6 = bf16[96,256]{1,0:T(8,128)(2,1)S(1)} collective-permute-done((bf16[96,256]{1,0:T(8,128)(2,1)S(1)}, bf16[96,256]{1,0:T(8,128)(2,1)S(1)}, u32[]{:S(2)}, u32[]{:S(2)}) %collective-permute-start.6) | collective-permute-done | bytes 49184 | tf_op jit(solution)/shard_map/ppermute | solution.py:152
  65.0 0.4 collective-permute-done.5
  65.4 0.9 %collective-permute-done.4 = bf16[96,256]{1,0:T(8,128)(2,1)S(1)} collective-permute-done((bf16[96,256]{1,0:T(8,128)(2,1)S(1)}, bf16[96,256]{1,0:T(8,128)(2,1)S(1)}, u32[]{:S(2)}, u32[]{:S(2)}) %collective-permute-start.4) | collective-permute-done | bytes 49184 | tf_op jit(solution)/shard_map/ppermute | solution.py:152
  66.3 0.7 slice_add_fusion
  67.2 0.6 fusion.5
  (33 shorter events, 0.4 us)
Async XLA Ops:
  0.6 8.7 %copy-start.5 = (f32[2048]{0:T(1024)S(1)}, f32[2048]{0:T(1024)}, u32[]{:S(2)}) copy-start(f32[2048]{0:T(1024)} %param.11) | copy-start | bytes 24580
  0.6 6.9 %collective-permute-start = (bf16[128,2048]{1,0:T(8,128)(2,1)}, bf16[128,2048]{1,0:T(8,128)(2,1)S(1)}, u32[]{:S(2)}, u32[]{:S(2)}) collective-permute-start(bf16[128,2048]{1,0:T(8,128)(2,1)} %bitcast.17), channel_id=1, source_target_pairs={{0,8},{8,16},{16,24},{1,9},{9,17},{17,25},{2,10},{10,18},{18,26},{... | collective-permute-start | bytes 1572872 | tf_op jit(solution)/shard_map/ppermute | solution.py:148
  3.0 6.2 %collective-permute-start.1 = (bf16[128,2048]{1,0:T(8,128)(2,1)}, bf16[128,2048]{1,0:T(8,128)(2,1)S(1)}, u32[]{:S(2)}, u32[]{:S(2)}) collective-permute-start(bf16[128,2048]{1,0:T(8,128)(2,1)} %bitcast.19), channel_id=1, source_target_pairs={{0,8},{8,16},{16,24},{1,9},{9,17},{17,25},{2,10},{10,18},{18,26},{... | collective-permute-start | bytes 1572872 | tf_op jit(solution)/shard_map/ppermute | solution.py:148
  9.3 1.2 %copy-start = (bf16[256,2048]{1,0:T(8,128)(2,1)S(1)}, bf16[256,2048]{1,0:T(8,128)(2,1)}, u32[]{:S(2)}) copy-start(bf16[256,2048]{1,0:T(8,128)(2,1)} %rel_ref.1) | copy-start | bytes 3145732
  10.5 1.0 %copy-start.1 = (bf16[1,128,2048]{2,1,0:T(8,128)(2,1)S(1)}, bf16[1,128,2048]{2,1,0:T(8,128)(2,1)}, u32[]{:S(2)}) copy-start(bf16[1,128,2048]{2,1,0:T(8,128)(2,1)} %param.7) | copy-start | bytes 1572868
  11.6 1.0 %copy-start.2 = (bf16[1,128,2048]{2,1,0:T(8,128)(2,1)S(1)}, bf16[1,128,2048]{2,1,0:T(8,128)(2,1)}, u32[]{:S(2)}) copy-start(bf16[1,128,2048]{2,1,0:T(8,128)(2,1)} %param.8) | copy-start | bytes 1572868
  12.6 1.0 %copy-start.3 = (bf16[1,128,2048]{2,1,0:T(8,128)(2,1)S(1)}, bf16[1,128,2048]{2,1,0:T(8,128)(2,1)}, u32[]{:S(2)}) copy-start(bf16[1,128,2048]{2,1,0:T(8,128)(2,1)} %param.9) | copy-start | bytes 1572868
  13.6 1.0 %copy-start.4 = (bf16[1,128,2048]{2,1,0:T(8,128)(2,1)S(1)}, bf16[1,128,2048]{2,1,0:T(8,128)(2,1)}, u32[]{:S(2)}) copy-start(bf16[1,128,2048]{2,1,0:T(8,128)(2,1)} %param.13) | copy-start | bytes 1572868
  14.7 0.7 %copy-start.6 = (f32[2048]{0:T(1024)S(1)}, f32[2048]{0:T(1024)}, u32[]{:S(2)}) copy-start(f32[2048]{0:T(1024)} %param.12) | copy-start | bytes 24580
  30.0 10.0 %collective-permute-start.2 = (bf16[144,2048]{1,0:T(8,128)(2,1)S(1)}, bf16[144,2048]{1,0:T(8,128)(2,1)S(1)}, u32[]{:S(2)}, u32[]{:S(2)}) collective-permute-start(bf16[144,2048]{1,0:T(8,128)(2,1)S(1)} %get-tuple-element.13), channel_id=1, source_target_pairs={{0,8},{8,0},{16,24},{24,16},{1,9},{9,1},{17,25},{25,17},{2,10},{10... | collective-permute-start | bytes 1769480 | tf_op jit(solution)/shard_map/ppermute | solution.py:152
  40.4 10.7 %collective-permute-start.3 = (bf16[80,2048]{1,0:T(8,128)(2,1)S(1)}, bf16[80,2048]{1,0:T(8,128)(2,1)S(1)}, u32[]{:S(2)}, u32[]{:S(2)}) collective-permute-start(bf16[80,2048]{1,0:T(8,128)(2,1)S(1)} %maximum_maximum_fusion), channel_id=1, source_target_pairs={{0,16},{8,24},{16,0},{24,8},{1,17},{9,25},{17,1},{25,9},{2,18},{10... | collective-permute-start | bytes 983048 | tf_op jit(solution)/shard_map/ppermute | solution.py:152
  51.3 10.0 %collective-permute-start.10 = (bf16[96,256]{1,0:T(8,128)(2,1)S(1)}, bf16[96,256]{1,0:T(8,128)(2,1)S(1)}, u32[]{:S(2)}, u32[]{:S(2)}) collective-permute-start(bf16[96,256]{1,0:T(8,128)(2,1)S(1)} %pad_maximum_fusion), channel_id=1, source_target_pairs={{0,7},{1,6},{2,5},{3,4},{4,3},{5,2},{6,1},{7,0},{8,15},{9,14},{10,... | collective-permute-start | bytes 147464 | tf_op jit(solution)/shard_map/ppermute | solution.py:152
  55.9 6.2 %collective-permute-start.9 = (bf16[96,256]{1,0:T(8,128)(2,1)S(1)}, bf16[96,256]{1,0:T(8,128)(2,1)S(1)}, u32[]{:S(2)}, u32[]{:S(2)}) collective-permute-start(bf16[96,256]{1,0:T(8,128)(2,1)S(1)} %get-tuple-element.35), channel_id=1, source_target_pairs={{0,6},{1,7},{2,4},{3,5},{4,2},{5,3},{6,0},{7,1},{8,14},{9,15},{10,... | collective-permute-start | bytes 147464 | tf_op jit(solution)/shard_map/ppermute | solution.py:152
  56.2 7.7 %collective-permute-start.8 = (bf16[96,256]{1,0:T(8,128)(2,1)S(1)}, bf16[96,256]{1,0:T(8,128)(2,1)S(1)}, u32[]{:S(2)}, u32[]{:S(2)}) collective-permute-start(bf16[96,256]{1,0:T(8,128)(2,1)S(1)} %get-tuple-element.34), channel_id=1, source_target_pairs={{0,5},{1,4},{2,7},{3,6},{4,1},{5,0},{6,3},{7,2},{8,13},{9,12},{10,... | collective-permute-start | bytes 147464 | tf_op jit(solution)/shard_map/ppermute | solution.py:152
  57.0 7.0 %collective-permute-start.7 = (bf16[96,256]{1,0:T(8,128)(2,1)S(1)}, bf16[96,256]{1,0:T(8,128)(2,1)S(1)}, u32[]{:S(2)}, u32[]{:S(2)}) collective-permute-start(bf16[96,256]{1,0:T(8,128)(2,1)S(1)} %get-tuple-element.33), channel_id=1, source_target_pairs={{0,4},{1,5},{2,6},{3,7},{4,0},{5,1},{6,2},{7,3},{8,12},{9,13},{10,... | collective-permute-start | bytes 147464 | tf_op jit(solution)/shard_map/ppermute | solution.py:152
  59.1 5.9 %collective-permute-start.6 = (bf16[96,256]{1,0:T(8,128)(2,1)S(1)}, bf16[96,256]{1,0:T(8,128)(2,1)S(1)}, u32[]{:S(2)}, u32[]{:S(2)}) collective-permute-start(bf16[96,256]{1,0:T(8,128)(2,1)S(1)} %get-tuple-element.32), channel_id=1, source_target_pairs={{0,3},{1,2},{2,1},{3,0},{4,7},{5,6},{6,5},{7,4},{8,11},{9,10},{10,... | collective-permute-start | bytes 147464 | tf_op jit(solution)/shard_map/ppermute | solution.py:152
  61.3 4.1 %collective-permute-start.5 = (bf16[96,256]{1,0:T(8,128)(2,1)S(1)}, bf16[96,256]{1,0:T(8,128)(2,1)S(1)}, u32[]{:S(2)}, u32[]{:S(2)}) collective-permute-start(bf16[96,256]{1,0:T(8,128)(2,1)S(1)} %get-tuple-element.31), channel_id=1, source_target_pairs={{0,2},{1,3},{2,0},{3,1},{4,6},{5,7},{6,4},{7,5},{8,10},{9,11},{10,... | collective-permute-start | bytes 147464 | tf_op jit(solution)/shard_map/ppermute | solution.py:152
  62.1 4.2 %collective-permute-start.4 = (bf16[96,256]{1,0:T(8,128)(2,1)S(1)}, bf16[96,256]{1,0:T(8,128)(2,1)S(1)}, u32[]{:S(2)}, u32[]{:S(2)}) collective-permute-start(bf16[96,256]{1,0:T(8,128)(2,1)S(1)} %get-tuple-element.30), channel_id=1, source_target_pairs={{0,1},{1,0},{2,3},{3,2},{4,5},{5,4},{6,7},{7,6},{8,9},{9,8},{10,11... | collective-permute-start | bytes 147464 | tf_op jit(solution)/shard_map/ppermute | solution.py:152

commit v2 on v1

v2 whole, which is shorter than its diff:
```python
import functools

import jax
import jax.numpy as jnp
from jax import lax
from jax.experimental import pallas as pl
from jax.experimental.pallas import tpu as pltpu
from jax.sharding import PartitionSpec as P

DH = 128
LOG2_E = 1.4426950408889634
GROUP = 4
CHUNKS = (1024, 1024)
BIAS_ROWS = 8
DIRECT_PEERS = 8


def contract(left, right, left_dim, right_dim):
    return lax.dot_general(
        left,
        right,
        (((left_dim,), (right_dim,)), ((), ())),
        preferred_element_type=jnp.float32,
    )


def attention_kernel(
    aliased,
    q_ref,
    k_ref,
    v_ref,
    k_mem_ref,
    v_mem_ref,
    rel_ref,
    bias_u_ref,
    bias_v_ref,
    d_out_ref,
    *out_refs,
):
    d_q_ref, d_k_ref, keep_ref, send_ref, bias_ref = out_refs[aliased:]

    seg_rows = q_ref.shape[0]
    mem_len = k_mem_ref.shape[0]
    key_count = seg_rows + mem_len
    pair_count, part_rows, _ = keep_ref.shape
    seg_index = lax.axis_index("seg")
    first_key = jnp.where(seg_index > 0, 0, mem_len)
    odd = jnp.bitwise_and(seg_index, 1) == 1
    row_index = lax.broadcasted_iota(jnp.int32, (seg_rows, key_count), 0)
    key_index = lax.broadcasted_iota(jnp.int32, (seg_rows, key_count), 1)
    allowed = (key_index <= row_index + mem_len) & (key_index >= first_key)

    flip_row = lax.broadcasted_iota(jnp.int32, (seg_rows, seg_rows), 0)
    flip_col = lax.broadcasted_iota(jnp.int32, (seg_rows, seg_rows), 1)
    flip = (flip_row + flip_col == seg_rows - 1).astype(jnp.bfloat16)
    score_scale = DH ** (-0.5)
    heads = range(q_ref.shape[1] // DH)
    def group_grads(group):
        cols = [slice(h * DH, (h + 1) * DH) for h in group]
        n = range(len(group))
        q_wide = [q_ref[:, c].astype(jnp.float32) for c in cols]
        q_content = [(q_wide[t] + bias_u_ref[:, cols[t]]).astype(jnp.bfloat16) for t in n]
        q_position = [(q_wide[t] + bias_v_ref[:, cols[t]]).astype(jnp.bfloat16) for t in n]
        by_distance = [contract(q_position[t], rel_ref[:, cols[t]], 1, 1) for t in n]
        keys_all = [jnp.concatenate([k_mem_ref[:, c], k_ref[:, c]], 0) for c in cols]
        content = [contract(q_content[t], keys_all[t], 1, 1) for t in n]
        position = [pltpu.roll(by_distance[t], key_count - seg_rows + 1, 1, stride=1, stride_axis=0) for t in n]
        values_all = [jnp.concatenate([v_mem_ref[:, c], v_ref[:, c]], 0) for c in cols]
        d_weights = [contract(d_out_ref[:, cols[t]], values_all[t], 1, 1) for t in n]
        scores = [jnp.where(allowed, (score_scale * LOG2_E) * (content[t] + position[t]), -1e30) for t in n]
        top = [jnp.max(s, axis=1, keepdims=True) for s in scores]
        raised = [jnp.exp2(scores[t] - top[t]) for t in n]
        total = [jnp.sum(r, axis=1, keepdims=True) for r in raised]
        cross = [jnp.sum(raised[t] * d_weights[t], axis=1, keepdims=True) for t in n]
        inverse = [1.0 / s for s in total]
        grad_scores = [((raised[t] * (score_scale * inverse[t])) * (d_weights[t] - cross[t] * inverse[t])).astype(jnp.bfloat16) for t in n]
        flipped = [contract(flip, g, 1, 0) for g in grad_scores]
        grad_rel = [pltpu.roll(f, 0, 1, stride=1, stride_axis=0).astype(jnp.bfloat16) for f in flipped]
        d_content = [contract(grad_scores[t], keys_all[t], 1, 0) for t in n]
        for t in n:
            d_k_ref[:, cols[t]] = contract(grad_scores[t][:, mem_len:], q_content[t], 0, 0).astype(jnp.bfloat16)
        q_flip = [contract(flip, q_ref[:, c], 1, 0) for c in cols]
        q_flip = [(q_flip[t] + bias_v_ref[:, cols[t]]).astype(jnp.bfloat16) for t in n]
        grad_back = [contract(flip, g, 1, 0).astype(jnp.bfloat16) for g in grad_rel]
        d_position = [contract(grad_back[t], rel_ref[:, cols[t]], 1, 0) for t in n]
        d_rel_all = [contract(grad_rel[t], q_flip[t], 0, 0) for t in n]
        for t in n:
            c = cols[t]
            d_q_ref[:, c] = (d_content[t] + d_position[t]).astype(jnp.bfloat16)
            sums = jnp.concatenate(
                [jnp.sum(d_content[t], 0, keepdims=True), jnp.sum(d_position[t], 0, keepdims=True)], 0
            )
            bias_ref[:, c] = sums
            high = sums.astype(jnp.bfloat16)
            low = (sums - high.astype(jnp.float32)).astype(jnp.bfloat16)
            fill = jnp.zeros((BIAS_ROWS - 4, DH), jnp.bfloat16)
            d_rel = d_rel_all[t]
            for pair in range(pair_count):
                start = 2 * pair * part_rows
                even_part = d_rel[start : start + part_rows]
                odd_part = d_rel[start + part_rows : start + 2 * part_rows]
                keep_ref[pair, :, c] = jnp.where(odd, odd_part, even_part)
                send_ref[pair * part_rows : (pair + 1) * part_rows, c] = jnp.where(
                    odd, even_part, odd_part
                ).astype(jnp.bfloat16)
            send_ref[pair_count * part_rows :, c] = jnp.concatenate([high, low, fill], 0)

    for first in range(0, len(heads), GROUP):
        group_grads(heads[first:first+GROUP])


def attention(start, span, grads, queries, keys, values, key_memory, value_memory, rest):
    rel_keys, bias_u, bias_v, d_out = rest
    seg_rows, width = queries.shape
    key_count = rel_keys.shape[0]
    seg_count = lax.axis_size("seg")
    pair_count = seg_count // 2
    part_rows = key_count // seg_count
    step_cols = GROUP * DH
    first = start // step_cols

    def block(rows):
        return pl.BlockSpec((rows, step_cols), lambda step: (0, first + step))

    def own(rows):
        return pl.BlockSpec((rows, step_cols), lambda step: (0, step))

    mem_len = key_count - seg_rows
    send_rows = pair_count * part_rows + BIAS_ROWS
    in_place = pl.BlockSpec(memory_space=pl.ANY)
    return pl.pallas_call(
        functools.partial(attention_kernel, len(grads)),
        name="attention_grads",
        grid=(span // step_cols,),
        in_specs=[block(seg_rows)] * 3
        + [own(mem_len)] * 2
        + [block(key_count), block(1), block(1), block(seg_rows)]
        + [in_place] * len(grads),
        out_specs=[
            block(seg_rows),
            block(seg_rows),
            pl.BlockSpec((pair_count, part_rows, step_cols), lambda step: (0, 0, step)),
            own(send_rows),
            own(2),
        ],
        out_shape=[
            jax.ShapeDtypeStruct((seg_rows, width), jnp.bfloat16),
            jax.ShapeDtypeStruct((seg_rows, width), jnp.bfloat16),
            jax.ShapeDtypeStruct((pair_count, part_rows, span), jnp.float32),
            jax.ShapeDtypeStruct((send_rows, span), jnp.bfloat16),
            jax.ShapeDtypeStruct((2, span), jnp.float32),
        ],
        input_output_aliases={9 + n: n for n in range(len(grads))},
        compiler_params=pltpu.CompilerParams(
            dimension_semantics=("arbitrary",), vmem_limit_bytes=48 * 1024 * 1024
        ),
    )(
        *(in_hbm(block) for block in (queries, keys, values)),
        key_memory,
        value_memory,
        in_hbm(rel_keys),
        bias_u[None],
        bias_v[None],
        in_hbm(d_out),
        *grads,
    )


def in_hbm(block):
    return pltpu.with_memory_space_constraint(block, pltpu.HBM)


def from_behind(block, axis, distance):
    devices = range(lax.axis_size(axis))
    route = [(i - distance, i) for i in devices if i - distance in devices]
    return lax.ppermute(block, axis, route)


def swap(block, axis, flip):
    return lax.ppermute(block, axis, [(i, i ^ flip) for i in range(lax.axis_size(axis))])


def bit_of(axis, flip):
    return (lax.axis_index(axis) // flip) % 2


def split_bias(sums):
    high = sums.astype(jnp.bfloat16)
    return high, (sums - high.astype(jnp.float32)).astype(jnp.bfloat16)


def add_packed(keep, sums, packed):
    rows = keep.shape[0] * keep.shape[1]
    partial = packed[:rows].astype(jnp.float32).reshape(keep.shape)
    halves = packed[rows : rows + 4].astype(jnp.float32)
    return keep + partial, sums + (halves[:2] + halves[2:])


def reduce_by_halves(keeps, sends, sums):
    seg_count = lax.axis_size("seg")
    got = [swap(send, "seg", 1) for send in sends]
    added = [add_packed(*part) for part in zip(keeps, sums, got)]
    partial = jnp.concatenate([part for part, _ in added], 2)
    sums = jnp.concatenate([part for _, part in added], 1)
    part_rows, width = partial.shape[1:]
    flip = 2
    while flip < seg_count:
        parts = partial.reshape(partial.shape[0] // 2, 2, part_rows, width)
        mine = bit_of("seg", flip)
        keep = lax.dynamic_index_in_dim(parts, mine, 1, keepdims=False)
        other = lax.dynamic_index_in_dim(parts, 1 - mine, 1, keepdims=False)
        high, low = split_bias(sums)
        fill = jnp.zeros((BIAS_ROWS - 4, width), jnp.bfloat16)
        packed = jnp.concatenate(
            [other.astype(jnp.bfloat16).reshape(-1, width), high, low, fill], 0
        )
        partial, sums = add_packed(keep, sums, swap(packed, "seg", flip))
        flip *= 2
    partial = partial[0]
    dp_count = lax.axis_size("dp")
    flip = dp_count // 2
    while 2 * flip > DIRECT_PEERS:
        half = partial.shape[1] // 2
        mine = bit_of("dp", flip)
        keep = lax.dynamic_slice_in_dim(partial, mine * half, half, 1)
        other = lax.dynamic_slice_in_dim(partial, (1 - mine) * half, half, 1)
        partial = keep + swap(other.astype(jnp.bfloat16), "dp", flip).astype(jnp.float32)
        sums = sums + swap(sums, "dp", flip)
        flip //= 2
    peers = 2 * flip
    place = lax.axis_index("dp") % peers
    cols = partial.shape[1] // peers
    high, low = split_bias(sums)
    tail = jnp.concatenate([high.reshape(-1, cols), low.reshape(-1, cols)], 0)
    total = lax.dynamic_slice_in_dim(partial, place * cols, cols, 1)
    for distance in range(1, peers):
        other = lax.dynamic_slice_in_dim(partial, (place ^ distance) * cols, cols, 1)
        packed = jnp.concatenate([other.astype(jnp.bfloat16), tail], 0)
        packed = swap(packed, "dp", distance).astype(jnp.float32)
        total = total + packed[:part_rows]
        halves = packed[part_rows:].reshape(2, 2, width)
        sums = sums + (halves[0] + halves[1])
    return total, sums


def split_rows(sums, width):
    rows = [
        sums[row : row + 1, col : col + width]
        for row in range(sums.shape[0])
        for col in range(0, sums.shape[1], width)
    ]
    rows = jnp.concatenate(rows, 0)
    high = rows.astype(jnp.bfloat16).astype(jnp.float32)
    return rows, jnp.concatenate([high, rows - high], 0)


def plane_kernel(chunk_count, *refs):
    keep_refs, got_refs, sum_refs = (refs[n * chunk_count : (n + 1) * chunk_count] for n in range(3))
    own_ref, sums_ref, send_y_ref, send_x_ref, send_xy_ref = refs[3 * chunk_count :]
    part_rows, width = own_ref.shape
    upper = lax.axis_index("seg") // 2 == 1
    right = lax.axis_index("dp") % 2 == 1
    cols = 2 * width // lax.axis_size("dp")
    starts = [sum(ref.shape[1] for ref in sum_refs[:n]) for n in range(chunk_count)]

    def columns(start):
        chunk = max(n for n in range(chunk_count) if starts[n] <= start)
        at = slice(start - starts[chunk], start - starts[chunk] + cols)
        parts = []
        for part in range(2):
            rows = slice(part * part_rows, (part + 1) * part_rows)
            parts.append(keep_refs[chunk][part, :, at] + got_refs[chunk][rows, at].astype(jnp.float32))
        return jnp.where(upper, parts[1], parts[0]), jnp.where(upper, parts[0], parts[1])

    for pair in range(lax.axis_size("dp") // 2):
        mine_left, other_left = columns(2 * pair * cols)
        mine_right, other_right = columns((2 * pair + 1) * cols)
        at = slice(pair * cols, (pair + 1) * cols)
        rows = slice(0, part_rows)
        own_ref[:, at] = jnp.where(right, mine_right, mine_left)
        send_x_ref[rows, at] = jnp.where(right, mine_left, mine_right).astype(jnp.bfloat16)
        send_y_ref[rows, at] = jnp.where(right, other_right, other_left).astype(jnp.bfloat16)
        send_xy_ref[rows, at] = jnp.where(right, other_left, other_right).astype(jnp.bfloat16)
    halves = [ref[2 * part_rows : 2 * part_rows + 4].astype(jnp.float32) for ref in got_refs]
    sums = [ref[...] + (half[:2] + half[2:]) for ref, half in zip(sum_refs, halves)]
    sums, tail = split_rows(jnp.concatenate(sums, 1), width)
    sums_ref[...] = sums
    for ref in (send_y_ref, send_x_ref, send_xy_ref):
        ref[part_rows:, :] = tail.astype(jnp.bfloat16)


def line_kernel(own_ref, sums_ref, *refs):
    got_refs, (total_ref, rows_ref, *send_refs) = refs[:3], refs[3:]
    part_rows, cols = total_ref.shape
    place = lax.axis_index("dp") // 2
    count = own_ref.shape[1] // cols
    blocks = []
    for n in range(count):
        at = slice(n * cols, (n + 1) * cols)
        block = own_ref[:, at]
        for ref in got_refs:
            block = block + ref[:part_rows, at].astype(jnp.float32)
        blocks.append(block)
    sums = sums_ref[...]
    for ref in got_refs:
        halves = ref[part_rows:, :].astype(jnp.float32)
        sums = sums + (halves[: sums.shape[0]] + halves[sums.shape[0] :])
    rows, tail = split_rows(sums, cols)
    rows_ref[...] = rows
    for distance, ref in zip(range(count), (total_ref, *send_refs)):
        block = blocks[distance]
        for n in range(1, count):
            block = jnp.where(place == n, blocks[n ^ distance], block)
        if distance == 0:
            ref[...] = block
        else:
            ref[:part_rows, :] = block.astype(jnp.bfloat16)
            ref[part_rows:, :] = tail.astype(jnp.bfloat16)


def whole_call(kernel, name, out_shape, *operands):
    return pl.pallas_call(
        kernel,
        name=name,
        out_shape=[jax.ShapeDtypeStruct(*shape) for shape in out_shape],
        compiler_params=pltpu.CompilerParams(vmem_limit_bytes=48 * 1024 * 1024),
    )(*operands)


def reduce_by_planes(keeps, sends, sums):
    dp_count = lax.axis_size("dp")
    got = [swap(send, "seg", 1) for send in sends]
    part_rows = keeps[0].shape[1]
    width = sum(keep.shape[2] for keep in keeps)
    half = width // 2
    tail = 2 * 2 * width // half
    send = ((part_rows + tail, half), jnp.bfloat16)
    own, plane_sums, *sends = whole_call(
        functools.partial(plane_kernel, len(keeps)),
        "plane_parts",
        [((part_rows, half), jnp.float32), ((tail // 2, half), jnp.float32), send, send, send],
        *keeps,
        *got,
        *sums,
    )
    got = [
        swap_both(sends[2], 2, 1),
        swap_both(sends[0], 2, 0),
        swap_both(sends[1], 0, 1),
    ]
    cols = width // dp_count
    tail = 2 * 2 * width // cols
    send = ((part_rows + tail, cols), jnp.bfloat16)
    peers = dp_count // 2
    total, sums, *sends = whole_call(
        line_kernel,
        "line_parts",
        [((part_rows, cols), jnp.float32), ((tail // 2, cols), jnp.float32)] + [send] * (peers - 1),
        own,
        plane_sums,
        *got,
    )
    for distance in range(1, peers):
        packed = swap(sends[distance - 1], "dp", 2 * distance).astype(jnp.float32)
        total = total + packed[:part_rows]
        sums = sums + (packed[part_rows : part_rows + tail // 2] + packed[part_rows + tail // 2 :])
    return total, sums.reshape(2, width)


def swap_both(block, seg_flip, dp_flip):
    dp_count = lax.axis_size("dp")
    route = [
        (s * dp_count + d, (s ^ seg_flip) * dp_count + (d ^ dp_flip))
        for s in range(lax.axis_size("seg"))
        for d in range(dp_count)
    ]
    return lax.ppermute(block, ("seg", "dp"), route)


def shards(queries, keys, values, rel_keys, bias_u, bias_v, d_out):
    seg_rows, width = queries.shape[1:]
    mem_len = rel_keys.shape[0] - seg_rows
    edges = [(sum(CHUNKS[:n]), span) for n, span in enumerate(CHUNKS)]
    memory = [
        [
            from_behind(block[0, seg_rows - mem_len :, start : start + span], "seg", 1)
            for block in (keys, values)
        ]
        for start, span in edges
    ]
    grads, keeps, sends, sums = (), [], [], []
    for (start, span), (key_memory, value_memory) in zip(edges, memory):
        rest = rel_keys, bias_u, bias_v, d_out[0]
        *grads, keep, send, sum_pair = attention(
            start, span, grads, queries[0], keys[0], values[0], key_memory, value_memory, rest
        )
        keeps.append(keep)
        sends.append(send)
        sums.append(sum_pair)
    planes = lax.axis_size("seg") == 4 and lax.axis_size("dp") == 8
    reduce = reduce_by_planes if planes else reduce_by_halves
    total, sums = reduce(keeps, sends, sums)
    return (grads[0][None], grads[1][None], total, sums[0], sums[1])


def solution(mesh):
    placed = (
        P("dp", "seg", None),
        P("dp", "seg", None),
        P("dp", "seg", None),
        P(),
        P(),
        P(),
        P("dp", "seg", None),
    )
    return jax.shard_map(
        shards,
        mesh=mesh,
        in_specs=placed,
        out_specs=(P("dp", "seg", None), P("dp", "seg", None), P("seg", "dp"), P(), P()),
        check_vma=False,
    )
```

time: 68.2 us -> 48.5 us (0.71)
  starting transfers between devices: 29.4 us -> 21 us
  Pallas kernels: 14.6 us -> 9.18 us
  local copies, waits for them, and re-layouts: 7.05 us -> 2.39 us
    ppermute x9 -> x5, starting transfers between devices: 22.4 us -> 5.89 us  [swap(): lax.ppermute(block, axis, [(i, i ^ flip) for i in range(lax.axis_size(axi...]
    ppermute x0 -> x3, waiting for transfers between devices: none -> 6.96 us  [swap_both(): return lax.ppermute(block, ('seg', 'dp'), route)]
    ppermute x9 -> x5, waiting for transfers between devices: 13 us -> 7.15 us  [swap(): lax.ppermute(block, axis, [(i, i ^ flip) for i in range(lax.axis_size(axi...]
    pallas_call x1 -> x4, Pallas kernels: 14.6 us -> 9.18 us  [the longest x2 8.89 us: attention(): pl.pallas_call(functools.partial(attention_kernel, len(grads)), name='att...]
    unnamed x14 -> x9, local copies, waits for them, and re-layouts: 6.09 us -> 1.23 us
    ppermute x0 -> x3, starting transfers between devices: none -> 4.36 us  [swap_both(): return lax.ppermute(block, ('seg', 'dp'), route)]
    ppermute x2 -> x4, starting transfers between devices: 6.93 us -> 10.8 us  [from_behind(): return lax.ppermute(block, axis, route)]
    ppermute x2 -> x4, waiting for transfers between devices: 1.69 us -> 0.01 us  [from_behind(): return lax.ppermute(block, axis, route)]
  transfers between devices with their start and end apart: 11 -> 12, of which waited for: 7 -> 7; matrix products, arithmetic and copies ran while one was open for 0% -> 0% of each run, Pallas kernels for 0% -> 9%
where the time goes in v2:
time: 48.5 us; the launch traced here: 48.2 us
  starting transfers between devices  21 us (43%)
  waiting for transfers between devices  14.1 us (29%)
  Pallas kernels  9.18 us (19%)
  local copies, waits for them, and re-layouts  2.39 us (5%)
  between operations  0.79 us (2%)
  other arithmetic  0.69 us (1%)
    ppermute x4, starting transfers between devices, from_behind(): return lax.ppermute(block, axis, route)  10.8 us
    pallas_call x2, Pallas kernels, attention(): pl.pallas_call(functools.partial(attention_kernel, len(grads)), name='att...  8.89 us
    ppermute x5, waiting for transfers between devices, swap(): lax.ppermute(block, axis, [(i, i ^ flip) for i in range(lax.axis_size(axi...  7.15 us
    ppermute x3, waiting for transfers between devices, swap_both(): return lax.ppermute(block, ('seg', 'dp'), route)  6.96 us
    ppermute x5, starting transfers between devices, swap(): lax.ppermute(block, axis, [(i, i ^ flip) for i in range(lax.axis_size(axi...  5.89 us
    ppermute x3, starting transfers between devices, swap_both(): return lax.ppermute(block, ('seg', 'dp'), route)  4.36 us
    unnamed x9, local copies, waits for them, and re-layouts  1.23 us
    squeeze x2, local copies, waits for them, and re-layouts, shards(): block[0, seg_rows - mem_len:, start:start + span]  1.16 us
  transfers between devices with their start and end apart: 12, of which 7 were waited for; matrix products, arithmetic and copies ran while one was open for 0% of the time, Pallas kernels for 9%

profile of v2, /device:TPU:0, one launch (start us, length us, event | category | flops | bytes accessed | tf_op | source)
XLA Modules:
  0.0 48.2 jit_solution(8904288399106099937)
XLA Ops:
  0.6 0.0 copy-start.2
  0.6 1.1 %slice_bitcast_fusion.1 = (bf16[128,1024]{1,0:T(8,128)(2,1)S(1)}, bf16[128,1024]{1,0:T(8,128)(2,1)S(1)}) fusion(bf16[1,128,2048]{2,1,0:T(8,128)(2,1)} %param.8), kind=kLoop, calls=%fused_computation.1 | loop fusion | bytes 1048576 | tf_op jit(solution)/shard_map/squeeze | solution.py:386
  1.8 2.4 %collective-permute-start.2 = (bf16[128,1024]{1,0:T(8,128)(2,1)S(1)}, bf16[128,1024]{1,0:T(8,128)(2,1)S(1)}, u32[]{:S(2)}, u32[]{:S(2)}) collective-permute-start(bf16[128,1024]{1,0:T(8,128)(2,1)S(1)} %get-tuple-element.47), channel_id=1, source_target_pairs={{0,8},{8,16},{16,24},{1,9},{9,17},{17,25},{2,10},{10,18},{18,26},{... | collective-permute-start | bytes 786440 | tf_op jit(solution)/shard_map/ppermute | solution.py:176
  4.1 0.0 copy-done.2
  4.2 0.0 copy-start.1
  4.2 0.0 copy-start
  4.2 4.5 %collective-permute-start.3 = (bf16[128,1024]{1,0:T(8,128)(2,1)S(1)}, bf16[128,1024]{1,0:T(8,128)(2,1)S(1)}, u32[]{:S(2)}, u32[]{:S(2)}) collective-permute-start(bf16[128,1024]{1,0:T(8,128)(2,1)S(1)} %get-tuple-element.45), channel_id=1, source_target_pairs={{0,8},{8,16},{16,24},{1,9},{9,17},{17,25},{2,10},{10,18},{18,26},{... | collective-permute-start | bytes 786440 | tf_op jit(solution)/shard_map/ppermute | solution.py:176
  8.8 1.9 %collective-permute-start = (bf16[128,1024]{1,0:T(8,128)(2,1)S(1)}, bf16[128,1024]{1,0:T(8,128)(2,1)S(1)}, u32[]{:S(2)}, u32[]{:S(2)}) collective-permute-start(bf16[128,1024]{1,0:T(8,128)(2,1)S(1)} %get-tuple-element.48), channel_id=1, source_target_pairs={{0,8},{8,16},{16,24},{1,9},{9,17},{17,25},{2,10},{10,18},{18,26},{... | collective-permute-start | bytes 786440 | tf_op jit(solution)/shard_map/ppermute | solution.py:176
  10.7 1.9 %collective-permute-start.1 = (bf16[128,1024]{1,0:T(8,128)(2,1)S(1)}, bf16[128,1024]{1,0:T(8,128)(2,1)S(1)}, u32[]{:S(2)}, u32[]{:S(2)}) collective-permute-start(bf16[128,1024]{1,0:T(8,128)(2,1)S(1)} %get-tuple-element.46), channel_id=1, source_target_pairs={{0,8},{8,16},{16,24},{1,9},{9,17},{17,25},{2,10},{10,18},{18,26},{... | collective-permute-start | bytes 786440 | tf_op jit(solution)/shard_map/ppermute | solution.py:176
  12.6 0.0 collective-permute-done.2.k_mem_ref
  12.6 0.0 collective-permute-done.3.v_mem_ref
  12.7 0.0 copy-done.1
  12.7 0.0 copy-done
  12.7 4.4 %attention_grads.2 = (bf16[128,2048]{1,0:T(8,128)(2,1)}, bf16[128,2048]{1,0:T(8,128)(2,1)}, f32[2,64,1024]{2,1,0:T(8,128)S(1)}, bf16[136,1024]{1,0:T(8,128)(2,1)S(1)}, f32[2,1024]{1,0:T(2,128)S(1)}) custom-call(bf16[128,2048]{1,0:T(8,128)(2,1)} %bitcast.30, bf16[128,2048]{1,0:T(8,128)(2,1)} %bitcast.26, bf16[128,2048]{1,0:T(8,128)(2,1)} %bitcast.28, ...), custom_call_target="tpu_custom_call" | custom-call | tf_op jit(solution)/shard_map/attention_grads/pallas_call | solution.py:131
  17.1 0.0 collective-permute-done.k_mem_ref
  17.1 0.0 collective-permute-done.1.v_mem_ref
  17.1 4.5 %attention_grads.3 = (bf16[128,2048]{1,0:T(8,128)(2,1)}, bf16[128,2048]{1,0:T(8,128)(2,1)}, f32[2,64,1024]{2,1,0:T(8,128)S(1)}, bf16[136,1024]{1,0:T(8,128)(2,1)S(1)}, f32[2,1024]{1,0:T(2,128)S(1)}) custom-call(bf16[128,2048]{1,0:T(8,128)(2,1)} %bitcast.31, bf16[128,2048]{1,0:T(8,128)(2,1)} %bitcast.27, ...), custom_call_target="tpu_custom_call", output_to_operand_aliasing={{0}: (9, {}), {1}: (10, {})} | custom-call | tf_op jit(solution)/shard_map/attention_grads/pallas_call | solution.py:131
  21.6 1.4 %collective-permute-start.5 = (bf16[136,1024]{1,0:T(8,128)(2,1)S(1)}, bf16[136,1024]{1,0:T(8,128)(2,1)S(1)}, u32[]{:S(2)}, u32[]{:S(2)}) collective-permute-start(bf16[136,1024]{1,0:T(8,128)(2,1)S(1)} %get-tuple-element.32), channel_id=1, source_target_pairs={{0,8},{8,0},{16,24},{24,16},{1,9},{9,1},{17,25},{25,17},{2,10},{10... | collective-permute-start | bytes 835592 | tf_op jit(solution)/shard_map/ppermute | solution.py:180
  23.0 0.1 collective-permute-start.4
  23.0 1.1 %collective-permute-done.5.refs_3_ = bf16[136,1024]{1,0:T(8,128)(2,1)S(1)} collective-permute-done((bf16[136,1024]{1,0:T(8,128)(2,1)S(1)}, bf16[136,1024]{1,0:T(8,128)(2,1)S(1)}, u32[]{:S(2)}, u32[]{:S(2)}) %collective-permute-start.5) | collective-permute-done | bytes 278560 | tf_op jit(solution)/shard_map/ppermute | solution.py:180
  24.1 0.4 collective-permute-done.4.refs_2_
  24.5 0.2 plane_parts.1
  24.7 3.7 %collective-permute-start.6 = (bf16[72,1024]{1,0:T(8,128)(2,1)S(1)}, bf16[72,1024]{1,0:T(8,128)(2,1)S(1)}, u32[]{:S(2)}, u32[]{:S(2)}) collective-permute-start(bf16[72,1024]{1,0:T(8,128)(2,1)S(1)} %get-tuple-element.37), channel_id=1, source_target_pairs={{0,17},{1,16},{2,19},{3,18},{4,21},{5,20},{6,23},{7,22},{8,25},{9,... | collective-permute-start | bytes 442376 | tf_op jit(solution)/shard_map/ppermute | solution.py:377
  28.5 0.0 collective-permute-start.7
  28.5 0.6 %collective-permute-start.8 = (bf16[72,1024]{1,0:T(8,128)(2,1)S(1)}, bf16[72,1024]{1,0:T(8,128)(2,1)S(1)}, u32[]{:S(2)}, u32[]{:S(2)}) collective-permute-start(bf16[72,1024]{1,0:T(8,128)(2,1)S(1)} %get-tuple-element.39), channel_id=1, source_target_pairs={{0,1},{1,0},{2,3},{3,2},{4,5},{5,4},{6,7},{7,6},{8,9},{9,8},{10,11... | collective-permute-start | bytes 442376 | tf_op jit(solution)/shard_map/ppermute | solution.py:377
  29.1 4.0 %collective-permute-done.6.refs_0_ = bf16[72,1024]{1,0:T(8,128)(2,1)S(1)} collective-permute-done((bf16[72,1024]{1,0:T(8,128)(2,1)S(1)}, bf16[72,1024]{1,0:T(8,128)(2,1)S(1)}, u32[]{:S(2)}, u32[]{:S(2)}) %collective-permute-start.6) | collective-permute-done | bytes 147488 | tf_op jit(solution)/shard_map/ppermute | solution.py:377
  33.1 2.7 %collective-permute-done.7.refs_1_ = bf16[72,1024]{1,0:T(8,128)(2,1)S(1)} collective-permute-done((bf16[72,1024]{1,0:T(8,128)(2,1)S(1)}, bf16[72,1024]{1,0:T(8,128)(2,1)S(1)}, u32[]{:S(2)}, u32[]{:S(2)}) %collective-permute-start.7) | collective-permute-done | bytes 147488 | tf_op jit(solution)/shard_map/ppermute | solution.py:377
  35.8 0.3 collective-permute-done.8.refs_2_
  36.1 0.1 line_parts.1
  36.2 1.7 %collective-permute-start.9 = (bf16[96,256]{1,0:T(8,128)(2,1)S(1)}, bf16[96,256]{1,0:T(8,128)(2,1)S(1)}, u32[]{:S(2)}, u32[]{:S(2)}) collective-permute-start(bf16[96,256]{1,0:T(8,128)(2,1)S(1)} %get-tuple-element.41), channel_id=1, source_target_pairs={{0,2},{1,3},{2,0},{3,1},{4,6},{5,7},{6,4},{7,5},{8,10},{9,11},{10,... | collective-permute-start | bytes 147464 | tf_op jit(solution)/shard_map/ppermute | solution.py:180
  37.8 2.6 %collective-permute-start.10 = (bf16[96,256]{1,0:T(8,128)(2,1)S(1)}, bf16[96,256]{1,0:T(8,128)(2,1)S(1)}, u32[]{:S(2)}, u32[]{:S(2)}) collective-permute-start(bf16[96,256]{1,0:T(8,128)(2,1)S(1)} %get-tuple-element.42), channel_id=1, source_target_pairs={{0,4},{1,5},{2,6},{3,7},{4,0},{5,1},{6,2},{7,3},{8,12},{9,13},{10,... | collective-permute-start | bytes 147464 | tf_op jit(solution)/shard_map/ppermute | solution.py:180
  40.4 0.2 collective-permute-start.11
  40.6 0.0 collective-permute-done.9
  40.6 3.0 %collective-permute-done.10 = bf16[96,256]{1,0:T(8,128)(2,1)S(1)} collective-permute-done((bf16[96,256]{1,0:T(8,128)(2,1)S(1)}, bf16[96,256]{1,0:T(8,128)(2,1)S(1)}, u32[]{:S(2)}, u32[]{:S(2)}) %collective-permute-start.10) | collective-permute-done | bytes 49184 | tf_op jit(solution)/shard_map/ppermute | solution.py:180
  43.6 2.6 %collective-permute-done.11 = bf16[96,256]{1,0:T(8,128)(2,1)S(1)} collective-permute-done((bf16[96,256]{1,0:T(8,128)(2,1)S(1)}, bf16[96,256]{1,0:T(8,128)(2,1)S(1)}, u32[]{:S(2)}, u32[]{:S(2)}) %collective-permute-start.11) | collective-permute-done | bytes 49184 | tf_op jit(solution)/shard_map/ppermute | solution.py:180
  46.3 0.7 %slice_add_fusion = f32[64,256]{1,0:T(8,128)} fusion(f32[96,256]{1,0:T(8,128)S(1)} %convert_element_type.11, f32[96,256]{1,0:T(8,128)S(1)} %convert_element_type.10, f32[64,256]{1,0:T(8,128)S(1)} %get-tuple-element.40, f32[96,256]{1,0:T(8,128)S(1)} %convert_element_type.9), kind=kLoop, calls=%fused_computation.4 | loop fusion | flops 49152 | bytes 327680 | tf_op jit(solution)/shard_map/add | solution.py:365
  47.0 0.6 %copy.15 = f32[1,2,8,128]{3,1,2,0:T(2,128)} copy(f32[1,2,8,128]{3,2,1,0:T(8,128)S(1)} %get-tuple-element.49) | data formatting | bytes 16384
  47.6 0.6 %copy.14 = f32[1,2,8,128]{3,1,2,0:T(2,128)} copy(f32[1,2,8,128]{3,2,1,0:T(8,128)S(1)} %get-tuple-element.50) | data formatting | bytes 16384
  (6 shorter events, 0.1 us)
Async XLA Ops:
  0.6 3.5 %copy-start.2 = (bf16[1,128,2048]{2,1,0:T(8,128)(2,1)S(1)}, bf16[1,128,2048]{2,1,0:T(8,128)(2,1)}, u32[]{:S(2)}) copy-start(bf16[1,128,2048]{2,1,0:T(8,128)(2,1)} %param.9) | copy-start | bytes 1572868
  1.8 10.9 %collective-permute-start.2 = (bf16[128,1024]{1,0:T(8,128)(2,1)S(1)}, bf16[128,1024]{1,0:T(8,128)(2,1)S(1)}, u32[]{:S(2)}, u32[]{:S(2)}) collective-permute-start(bf16[128,1024]{1,0:T(8,128)(2,1)S(1)} %get-tuple-element.47), channel_id=1, source_target_pairs={{0,8},{8,16},{16,24},{1,9},{9,17},{17,25},{2,10},{10,18},{18,26},{... | collective-permute-start | bytes 786440 | tf_op jit(solution)/shard_map/ppermute | solution.py:176
  4.2 8.4 %copy-start.1 = (f32[2048]{0:T(1024)S(1)}, f32[2048]{0:T(1024)}, u32[]{:S(2)}) copy-start(f32[2048]{0:T(1024)} %param.12) | copy-start | bytes 24580
  4.2 8.4 %copy-start = (f32[2048]{0:T(1024)S(1)}, f32[2048]{0:T(1024)}, u32[]{:S(2)}) copy-start(f32[2048]{0:T(1024)} %param.11) | copy-start | bytes 24580
  4.2 8.4 %collective-permute-start.3 = (bf16[128,1024]{1,0:T(8,128)(2,1)S(1)}, bf16[128,1024]{1,0:T(8,128)(2,1)S(1)}, u32[]{:S(2)}, u32[]{:S(2)}) collective-permute-start(bf16[128,1024]{1,0:T(8,128)(2,1)S(1)} %get-tuple-element.45), channel_id=1, source_target_pairs={{0,8},{8,16},{16,24},{1,9},{9,17},{17,25},{2,10},{10,18},{18,26},{... | collective-permute-start | bytes 786440 | tf_op jit(solution)/shard_map/ppermute | solution.py:176
  8.8 8.3 %collective-permute-start = (bf16[128,1024]{1,0:T(8,128)(2,1)S(1)}, bf16[128,1024]{1,0:T(8,128)(2,1)S(1)}, u32[]{:S(2)}, u32[]{:S(2)}) collective-permute-start(bf16[128,1024]{1,0:T(8,128)(2,1)S(1)} %get-tuple-element.48), channel_id=1, source_target_pairs={{0,8},{8,16},{16,24},{1,9},{9,17},{17,25},{2,10},{10,18},{18,26},{... | collective-permute-start | bytes 786440 | tf_op jit(solution)/shard_map/ppermute | solution.py:176
  10.7 6.4 %collective-permute-start.1 = (bf16[128,1024]{1,0:T(8,128)(2,1)S(1)}, bf16[128,1024]{1,0:T(8,128)(2,1)S(1)}, u32[]{:S(2)}, u32[]{:S(2)}) collective-permute-start(bf16[128,1024]{1,0:T(8,128)(2,1)S(1)} %get-tuple-element.46), channel_id=1, source_target_pairs={{0,8},{8,16},{16,24},{1,9},{9,17},{17,25},{2,10},{10,18},{18,26},{... | collective-permute-start | bytes 786440 | tf_op jit(solution)/shard_map/ppermute | solution.py:176
  21.6 2.6 %collective-permute-start.5 = (bf16[136,1024]{1,0:T(8,128)(2,1)S(1)}, bf16[136,1024]{1,0:T(8,128)(2,1)S(1)}, u32[]{:S(2)}, u32[]{:S(2)}) collective-permute-start(bf16[136,1024]{1,0:T(8,128)(2,1)S(1)} %get-tuple-element.32), channel_id=1, source_target_pairs={{0,8},{8,0},{16,24},{24,16},{1,9},{9,1},{17,25},{25,17},{2,10},{10... | collective-permute-start | bytes 835592 | tf_op jit(solution)/shard_map/ppermute | solution.py:180
  23.0 1.6 %collective-permute-start.4 = (bf16[136,1024]{1,0:T(8,128)(2,1)S(1)}, bf16[136,1024]{1,0:T(8,128)(2,1)S(1)}, u32[]{:S(2)}, u32[]{:S(2)}) collective-permute-start(bf16[136,1024]{1,0:T(8,128)(2,1)S(1)} %get-tuple-element.31), channel_id=1, source_target_pairs={{0,8},{8,0},{16,24},{24,16},{1,9},{9,1},{17,25},{25,17},{2,10},{10... | collective-permute-start | bytes 835592 | tf_op jit(solution)/shard_map/ppermute | solution.py:180
  24.7 8.4 %collective-permute-start.6 = (bf16[72,1024]{1,0:T(8,128)(2,1)S(1)}, bf16[72,1024]{1,0:T(8,128)(2,1)S(1)}, u32[]{:S(2)}, u32[]{:S(2)}) collective-permute-start(bf16[72,1024]{1,0:T(8,128)(2,1)S(1)} %get-tuple-element.37), channel_id=1, source_target_pairs={{0,17},{1,16},{2,19},{3,18},{4,21},{5,20},{6,23},{7,22},{8,25},{9,... | collective-permute-start | bytes 442376 | tf_op jit(solution)/shard_map/ppermute | solution.py:377
  28.5 7.3 %collective-permute-start.7 = (bf16[72,1024]{1,0:T(8,128)(2,1)S(1)}, bf16[72,1024]{1,0:T(8,128)(2,1)S(1)}, u32[]{:S(2)}, u32[]{:S(2)}) collective-permute-start(bf16[72,1024]{1,0:T(8,128)(2,1)S(1)} %get-tuple-element.38), channel_id=1, source_target_pairs={{0,16},{1,17},{2,18},{3,19},{4,20},{5,21},{6,22},{7,23},{8,24},{9,... | collective-permute-start | bytes 442376 | tf_op jit(solution)/shard_map/ppermute | solution.py:377
  28.5 7.6 %collective-permute-start.8 = (bf16[72,1024]{1,0:T(8,128)(2,1)S(1)}, bf16[72,1024]{1,0:T(8,128)(2,1)S(1)}, u32[]{:S(2)}, u32[]{:S(2)}) collective-permute-start(bf16[72,1024]{1,0:T(8,128)(2,1)S(1)} %get-tuple-element.39), channel_id=1, source_target_pairs={{0,1},{1,0},{2,3},{3,2},{4,5},{5,4},{6,7},{7,6},{8,9},{9,8},{10,11... | collective-permute-start | bytes 442376 | tf_op jit(solution)/shard_map/ppermute | solution.py:377
  36.2 4.5 %collective-permute-start.9 = (bf16[96,256]{1,0:T(8,128)(2,1)S(1)}, bf16[96,256]{1,0:T(8,128)(2,1)S(1)}, u32[]{:S(2)}, u32[]{:S(2)}) collective-permute-start(bf16[96,256]{1,0:T(8,128)(2,1)S(1)} %get-tuple-element.41), channel_id=1, source_target_pairs={{0,2},{1,3},{2,0},{3,1},{4,6},{5,7},{6,4},{7,5},{8,10},{9,11},{10,... | collective-permute-start | bytes 147464 | tf_op jit(solution)/shard_map/ppermute | solution.py:180
  37.8 5.8 %collective-permute-start.10 = (bf16[96,256]{1,0:T(8,128)(2,1)S(1)}, bf16[96,256]{1,0:T(8,128)(2,1)S(1)}, u32[]{:S(2)}, u32[]{:S(2)}) collective-permute-start(bf16[96,256]{1,0:T(8,128)(2,1)S(1)} %get-tuple-element.42), channel_id=1, source_target_pairs={{0,4},{1,5},{2,6},{3,7},{4,0},{5,1},{6,2},{7,3},{8,12},{9,13},{10,... | collective-permute-start | bytes 147464 | tf_op jit(solution)/shard_map/ppermute | solution.py:180
  40.4 5.9 %collective-permute-start.11 = (bf16[96,256]{1,0:T(8,128)(2,1)S(1)}, bf16[96,256]{1,0:T(8,128)(2,1)S(1)}, u32[]{:S(2)}, u32[]{:S(2)}) collective-permute-start(bf16[96,256]{1,0:T(8,128)(2,1)S(1)} %get-tuple-element.43), channel_id=1, source_target_pairs={{0,6},{1,7},{2,4},{3,5},{4,2},{5,3},{6,0},{7,1},{8,14},{9,15},{10,... | collective-permute-start | bytes 147464 | tf_op jit(solution)/shard_map/ppermute | solution.py:180

commit v3 on v2

--- a/solution.py
+++ b/solution.py
@@ -29,8 +29,7 @@
     q_ref,
     k_ref,
     v_ref,
-    k_mem_ref,
-    v_mem_ref,
+    memory_ref,
     rel_ref,
     bias_u_ref,
     bias_v_ref,
@@ -40,7 +39,7 @@
     d_q_ref, d_k_ref, keep_ref, send_ref, bias_ref = out_refs[aliased:]
 
     seg_rows = q_ref.shape[0]
-    mem_len = k_mem_ref.shape[0]
+    mem_len = memory_ref.shape[0] // 2
     key_count = seg_rows + mem_len
     pair_count, part_rows, _ = keep_ref.shape
     seg_index = lax.axis_index("seg")
@@ -62,10 +61,10 @@
         q_content = [(q_wide[t] + bias_u_ref[:, cols[t]]).astype(jnp.bfloat16) for t in n]
         q_position = [(q_wide[t] + bias_v_ref[:, cols[t]]).astype(jnp.bfloat16) for t in n]
         by_distance = [contract(q_position[t], rel_ref[:, cols[t]], 1, 1) for t in n]
-        keys_all = [jnp.concatenate([k_mem_ref[:, c], k_ref[:, c]], 0) for c in cols]
+        keys_all = [jnp.concatenate([memory_ref[:mem_len, c], k_ref[:, c]], 0) for c in cols]
         content = [contract(q_content[t], keys_all[t], 1, 1) for t in n]
         position = [pltpu.roll(by_distance[t], key_count - seg_rows + 1, 1, stride=1, stride_axis=0) for t in n]
-        values_all = [jnp.concatenate([v_mem_ref[:, c], v_ref[:, c]], 0) for c in cols]
+        values_all = [jnp.concatenate([memory_ref[mem_len:, c], v_ref[:, c]], 0) for c in cols]
         d_weights = [contract(d_out_ref[:, cols[t]], values_all[t], 1, 1) for t in n]
         scores = [jnp.where(allowed, (score_scale * LOG2_E) * (content[t] + position[t]), -1e30) for t in n]
         top = [jnp.max(s, axis=1, keepdims=True) for s in scores]
@@ -109,7 +108,7 @@
         group_grads(heads[first:first+GROUP])
 
 
-def attention(start, span, grads, queries, keys, values, key_memory, value_memory, rest):
+def attention(start, span, grads, queries, keys, values, memory, rest):
     rel_keys, bias_u, bias_v, d_out = rest
     seg_rows, width = queries.shape
     key_count = rel_keys.shape[0]
@@ -133,8 +132,7 @@
         name="attention_grads",
         grid=(span // step_cols,),
         in_specs=[block(seg_rows)] * 3
-        + [own(mem_len)] * 2
-        + [block(key_count), block(1), block(1), block(seg_rows)]
+        + [own(2 * mem_len), block(key_count), block(1), block(1), block(seg_rows)]
         + [in_place] * len(grads),
         out_specs=[
             block(seg_rows),
@@ -150,30 +148,28 @@
             jax.ShapeDtypeStruct((send_rows, span), jnp.bfloat16),
             jax.ShapeDtypeStruct((2, span), jnp.float32),
         ],
-        input_output_aliases={9 + n: n for n in range(len(grads))},
+        input_output_aliases={8 + n: n for n in range(len(grads))},
         compiler_params=pltpu.CompilerParams(
             dimension_semantics=("arbitrary",), vmem_limit_bytes=48 * 1024 * 1024
         ),
     )(
-        *(in_hbm(block) for block in (queries, keys, values)),
-        key_memory,
-        value_memory,
-        in_hbm(rel_keys),
+        *(in_vmem(block) for block in (queries, keys, values)),
+        memory,
+        in_vmem(rel_keys),
         bias_u[None],
         bias_v[None],
-        in_hbm(d_out),
+        in_vmem(d_out),
         *grads,
     )
 
 
-def in_hbm(block):
-    return pltpu.with_memory_space_constraint(block, pltpu.HBM)
-
-
-def from_behind(block, axis, distance):
-    devices = range(lax.axis_size(axis))
-    route = [(i - distance, i) for i in devices if i - distance in devices]
-    return lax.ppermute(block, axis, route)
+def in_vmem(block):
+    return pltpu.with_memory_space_constraint(block, pltpu.VMEM)
+
+
+def from_behind(block, axis):
+    count = lax.axis_size(axis)
+    return lax.ppermute(block, axis, [(i, (i + 1) % count) for i in range(count)])
 
 
 def swap(block, axis, flip):
@@ -305,7 +301,17 @@
     for ref in got_refs:
         halves = ref[part_rows:, :].astype(jnp.float32)
         sums = sums + (halves[: sums.shape[0]] + halves[sums.shape[0] :])
-    rows, tail = split_rows(sums, cols)
+    lanes = cols // 2
+    half = sums.shape[0] // 2
+    rows = []
+    for side in (sums[:half], sums[half:]):
+        pieces = [
+            side[row : row + 1, col : col + lanes]
+            for row in range(half)
+            for col in range(0, side.shape[1], lanes)
+        ]
+        rows.append(jnp.concatenate(pieces, 0))
+    rows = jnp.concatenate(rows, 1)
     rows_ref[...] = rows
     for distance, ref in zip(range(count), (total_ref, *send_refs)):
         block = blocks[distance]
@@ -315,7 +321,19 @@
             ref[...] = block
         else:
             ref[:part_rows, :] = block.astype(jnp.bfloat16)
-            ref[part_rows:, :] = tail.astype(jnp.bfloat16)
+            ref[part_rows:, :] = rows.astype(jnp.bfloat16)
+
+
+def last_kernel(total_ref, rows_ref, *refs):
+    got_refs, (out_ref, bias_u_ref, bias_v_ref) = refs[:-3], refs[-3:]
+    part_rows, cols = total_ref.shape
+    total, rows = total_ref[...], rows_ref[...]
+    for ref in got_refs:
+        total = total + ref[:part_rows, :].astype(jnp.float32)
+        rows = rows + ref[part_rows:, :].astype(jnp.float32)
+    out_ref[...] = total
+    bias_u_ref[...] = rows[:, : cols // 2]
+    bias_v_ref[...] = rows[:, cols // 2 :]
 
 
 def whole_call(kernel, name, out_shape, *operands):
@@ -349,22 +367,23 @@
         swap_both(sends[1], 0, 1),
     ]
     cols = width // dp_count
-    tail = 2 * 2 * width // cols
+    tail = 2 * width // cols
     send = ((part_rows + tail, cols), jnp.bfloat16)
     peers = dp_count // 2
-    total, sums, *sends = whole_call(
+    total, rows, *sends = whole_call(
         line_kernel,
         "line_parts",
-        [((part_rows, cols), jnp.float32), ((tail // 2, cols), jnp.float32)] + [send] * (peers - 1),
+        [((part_rows, cols), jnp.float32), ((tail, cols), jnp.float32)] + [send] * (peers - 1),
         own,
         plane_sums,
         *got,
     )
-    for distance in range(1, peers):
-        packed = swap(sends[distance - 1], "dp", 2 * distance).astype(jnp.float32)
-        total = total + packed[:part_rows]
-        sums = sums + (packed[part_rows : part_rows + tail // 2] + packed[part_rows + tail // 2 :])
-    return total, sums.reshape(2, width)
+    got = [swap(send, "dp", 2 * distance) for distance, send in enumerate(sends, 1)]
+    side = ((tail, cols // 2), jnp.float32)
+    total, *sums = whole_call(
+        last_kernel, "last_sums", [((part_rows, cols), jnp.float32), side, side], total, rows, *got
+    )
+    return total, [half.reshape(width) for half in sums]
 
 
 def swap_both(block, seg_flip, dp_flip):
@@ -382,17 +401,23 @@
     mem_len = rel_keys.shape[0] - seg_rows
     edges = [(sum(CHUNKS[:n]), span) for n, span in enumerate(CHUNKS)]
     memory = [
-        [
-            from_behind(block[0, seg_rows - mem_len :, start : start + span], "seg", 1)
-            for block in (keys, values)
-        ]
+        from_behind(
+            jnp.concatenate(
+                [
+                    block[0, seg_rows - mem_len :, start : start + span]
+                    for block in (keys, values)
+                ],
+                0,
+            ),
+            "seg",
+        )
         for start, span in edges
     ]
     grads, keeps, sends, sums = (), [], [], []
-    for (start, span), (key_memory, value_memory) in zip(edges, memory):
+    for (start, span), block in zip(edges, memory):
         rest = rel_keys, bias_u, bias_v, d_out[0]
         *grads, keep, send, sum_pair = attention(
-            start, span, grads, queries[0], keys[0], values[0], key_memory, value_memory, rest
+            start, span, grads, queries[0], keys[0], values[0], block, rest
         )
         keeps.append(keep)
         sends.append(send)

time: 48.5 us -> 44.5 us (0.918)
  starting transfers between devices: 21 us -> 12.1 us
  waiting for transfers between devices: 14.1 us -> 22.2 us
  Pallas kernels: 9.18 us -> 7.84 us
  local copies, waits for them, and re-layouts: 2.39 us -> 1.41 us
  other arithmetic: 0.69 us -> 0.07 us
    ppermute x4 -> x2, waiting for transfers between devices: 0.01 us -> 8.22 us  [from_behind(): lax.ppermute(block, axis, [(i, (i + 1) % count) for i in range(count)])]
    ppermute x4 -> x2, starting transfers between devices: 10.8 us -> 3.19 us  [from_behind(): lax.ppermute(block, axis, [(i, (i + 1) % count) for i in range(count)])]
    pallas_call x2, Pallas kernels: 8.89 us -> 6.88 us  [attention(): pl.pallas_call(functools.partial(attention_kernel, len(grads)), name='att...]
    unnamed x9 -> x14, local copies, waits for them, and re-layouts: 1.23 us -> 0.03 us
    ppermute x5, starting transfers between devices: 5.89 us -> 4.96 us  [swap(): lax.ppermute(block, axis, [(i, i ^ flip) for i in range(lax.axis_size(axi...]
    add x2 -> x0, other arithmetic: 0.66 us -> none  [the longest x1 0.65 us: reduce_by_planes(): total = total + packed[:part_rows]]
    pallas_call x2 -> x3, Pallas kernels: 0.29 us -> 0.95 us  [whole_call(): pl.pallas_call(kernel, name=name, out_shape=[jax.ShapeDtypeStruct(*shape)...]
    squeeze x2 -> x1, local copies, waits for them, and re-layouts: 1.16 us -> 1.37 us  [shards(): block[0, seg_rows - mem_len:, start:start + span]]
  transfers between devices with their start and end apart: 12 -> 10, of which waited for: 7 -> 9; matrix products, arithmetic and copies ran while one was open for 0% -> 0% of each run, Pallas kernels for 9% -> 8%
where the time goes in v3:
time: 44.5 us; the launch traced here: 44.4 us
  waiting for transfers between devices  22.2 us (50%)
  starting transfers between devices  12.1 us (27%)
  Pallas kernels  7.84 us (18%)
  local copies, waits for them, and re-layouts  1.41 us (3%)
  between operations  0.75 us (2%)
    ppermute x2, waiting for transfers between devices, from_behind(): lax.ppermute(block, axis, [(i, (i + 1) % count) for i in range(count)])  8.22 us
    ppermute x5, waiting for transfers between devices, swap(): lax.ppermute(block, axis, [(i, i ^ flip) for i in range(lax.axis_size(axi...  7.03 us
    ppermute x3, waiting for transfers between devices, swap_both(): return lax.ppermute(block, ('seg', 'dp'), route)  6.95 us
    pallas_call x2, Pallas kernels, attention(): pl.pallas_call(functools.partial(attention_kernel, len(grads)), name='att...  6.88 us
    ppermute x5, starting transfers between devices, swap(): lax.ppermute(block, axis, [(i, i ^ flip) for i in range(lax.axis_size(axi...  4.96 us
    ppermute x3, starting transfers between devices, swap_both(): return lax.ppermute(block, ('seg', 'dp'), route)  3.94 us
    ppermute x2, starting transfers between devices, from_behind(): lax.ppermute(block, axis, [(i, (i + 1) % count) for i in range(count)])  3.19 us
    squeeze x1, local copies, waits for them, and re-layouts, shards(): block[0, seg_rows - mem_len:, start:start + span]  1.37 us
  transfers between devices with their start and end apart: 10, of which 9 were waited for; matrix products, arithmetic and copies ran while one was open for 0% of the time, Pallas kernels for 8%

profile of v3, /device:TPU:0, one launch (start us, length us, event | category | flops | bytes accessed | tf_op | source)
XLA Modules:
  0.0 44.4 jit_solution(3528115821851375647)
XLA Ops:
  0.6 0.0 copy-start.3
  0.6 0.0 copy-start.4
  0.7 1.4 %slice_bitcast_fusion = (bf16[128,1024]{1,0:T(8,128)(2,1)S(1)}, bf16[128,1024]{1,0:T(8,128)(2,1)S(1)}, bf16[128,1024]{1,0:T(8,128)(2,1)S(1)}, bf16[128,1024]{1,0:T(8,128)(2,1)S(1)}) fusion(bf16[1,128,2048]{2,1,0:T(8,128)(2,1)} %param.9, bf16[1,128,2048]{2,1,0:T(8,128)(2,1)} %param.8), kind=kLoop, calls=%fused_computation.2 | loop fusion | bytes 2097152 | tf_op jit(solution)/shard_map/squeeze | solution.py:407
  2.0 0.0 copy-start.6
  2.0 0.0 copy-start.2
  2.1 0.5 %collective-permute-start.1 = (bf16[256,1024]{1,0:T(8,128)(2,1)S(1)}, bf16[256,1024]{1,0:T(8,128)(2,1)S(1)}, u32[]{:S(2)}, u32[]{:S(2)}) collective-permute-start(bf16[256,1024]{1,0:T(8,128)(2,1)S(1)} %pad_maximum_fusion.1), channel_id=1, source_target_pairs={{0,8},{8,16},{16,24},{24,0},{1,9},{9,17},{17,25},{25,1},{2,10},{10... | collective-permute-start | bytes 1572872 | tf_op jit(solution)/shard_map/ppermute | solution.py:172
  2.6 0.0 copy-start
  2.6 0.0 copy-start.1
  2.6 0.0 copy-start.5
  2.7 2.7 %collective-permute-start = (bf16[256,1024]{1,0:T(8,128)(2,1)S(1)}, bf16[256,1024]{1,0:T(8,128)(2,1)S(1)}, u32[]{:S(2)}, u32[]{:S(2)}) collective-permute-start(bf16[256,1024]{1,0:T(8,128)(2,1)S(1)} %pad_maximum_fusion), channel_id=1, source_target_pairs={{0,8},{8,16},{16,24},{24,0},{1,9},{9,17},{17,25},{25,1},{2,10},{10... | collective-permute-start | bytes 1572872 | tf_op jit(solution)/shard_map/ppermute | solution.py:172
  5.3 6.1 %collective-permute-done.1.memory_ref = bf16[256,1024]{1,0:T(8,128)(2,1)S(1)} collective-permute-done((bf16[256,1024]{1,0:T(8,128)(2,1)S(1)}, bf16[256,1024]{1,0:T(8,128)(2,1)S(1)}, u32[]{:S(2)}, u32[]{:S(2)}) %collective-permute-start.1) | collective-permute-done | bytes 524320 | tf_op jit(solution)/shard_map/ppermute | solution.py:172
  11.4 0.0 copy-done.3
  11.4 0.0 copy-done.4
  11.4 0.0 copy-done.6
  11.4 0.0 copy-done.2
  11.4 0.0 copy-done
  11.5 0.0 copy-done.1
  11.5 0.0 copy-done.5
  11.5 3.4 %attention_grads.2 = (bf16[128,2048]{1,0:T(8,128)(2,1)}, bf16[128,2048]{1,0:T(8,128)(2,1)}, f32[2,64,1024]{2,1,0:T(8,128)S(1)}, bf16[136,1024]{1,0:T(8,128)(2,1)S(1)}, f32[2,1024]{1,0:T(2,128)S(1)}) custom-call(bf16[128,2048]{1,0:T(8,128)(2,1)S(1)} %bitcast.22, bf16[128,2048]{1,0:T(8,128)(2,1)S(1)} %bitcast.18, bf16[128,2048]{1,0:T(8,128)(2,1)S(1)} %bitcast.20, ...), custom_call_target="tpu_custom_call" | custom-call | tf_op jit(solution)/shard_map/attention_grads/pallas_call | solution.py:130
  14.9 2.1 %collective-permute-done.memory_ref = bf16[256,1024]{1,0:T(8,128)(2,1)S(1)} collective-permute-done((bf16[256,1024]{1,0:T(8,128)(2,1)S(1)}, bf16[256,1024]{1,0:T(8,128)(2,1)S(1)}, u32[]{:S(2)}, u32[]{:S(2)}) %collective-permute-start) | collective-permute-done | bytes 524320 | tf_op jit(solution)/shard_map/ppermute | solution.py:172
  17.0 3.5 %attention_grads.3 = (bf16[128,2048]{1,0:T(8,128)(2,1)}, bf16[128,2048]{1,0:T(8,128)(2,1)}, f32[2,64,1024]{2,1,0:T(8,128)S(1)}, bf16[136,1024]{1,0:T(8,128)(2,1)S(1)}, f32[2,1024]{1,0:T(2,128)S(1)}) custom-call(bf16[128,2048]{1,0:T(8,128)(2,1)S(1)} %bitcast.23, bf16[128,2048]{1,0:T(8,128)(2,1)S(1)} %bitcast.19, ...), custom_call_target="tpu_custom_call", output_to_operand_aliasing={{0}: (8, {}), {1}: (9, {})} | custom-call | tf_op jit(solution)/shard_map/attention_grads/pallas_call | solution.py:130
  20.5 0.0 collective-permute-start.3
  20.5 0.5 %collective-permute-start.2 = (bf16[136,1024]{1,0:T(8,128)(2,1)S(1)}, bf16[136,1024]{1,0:T(8,128)(2,1)S(1)}, u32[]{:S(2)}, u32[]{:S(2)}) collective-permute-start(bf16[136,1024]{1,0:T(8,128)(2,1)S(1)} %get-tuple-element.34), channel_id=1, source_target_pairs={{0,8},{8,0},{16,24},{24,16},{1,9},{9,1},{17,25},{25,17},{2,10},{10... | collective-permute-start | bytes 835592 | tf_op jit(solution)/shard_map/ppermute | solution.py:176
  21.0 1.0 %collective-permute-done.3.refs_3_ = bf16[136,1024]{1,0:T(8,128)(2,1)S(1)} collective-permute-done((bf16[136,1024]{1,0:T(8,128)(2,1)S(1)}, bf16[136,1024]{1,0:T(8,128)(2,1)S(1)}, u32[]{:S(2)}, u32[]{:S(2)}) %collective-permute-start.3) | collective-permute-done | bytes 278560 | tf_op jit(solution)/shard_map/ppermute | solution.py:176
  22.1 0.4 collective-permute-done.2.refs_2_
  22.5 0.2 plane_parts.1
  22.7 3.3 %collective-permute-start.4 = (bf16[72,1024]{1,0:T(8,128)(2,1)S(1)}, bf16[72,1024]{1,0:T(8,128)(2,1)S(1)}, u32[]{:S(2)}, u32[]{:S(2)}) collective-permute-start(bf16[72,1024]{1,0:T(8,128)(2,1)S(1)} %get-tuple-element.40), channel_id=1, source_target_pairs={{0,17},{1,16},{2,19},{3,18},{4,21},{5,20},{6,23},{7,22},{8,25},{9,... | collective-permute-start | bytes 442376 | tf_op jit(solution)/shard_map/ppermute | solution.py:396
  26.0 0.5 %collective-permute-start.5 = (bf16[72,1024]{1,0:T(8,128)(2,1)S(1)}, bf16[72,1024]{1,0:T(8,128)(2,1)S(1)}, u32[]{:S(2)}, u32[]{:S(2)}) collective-permute-start(bf16[72,1024]{1,0:T(8,128)(2,1)S(1)} %get-tuple-element.41), channel_id=1, source_target_pairs={{0,16},{1,17},{2,18},{3,19},{4,20},{5,21},{6,22},{7,23},{8,24},{9,... | collective-permute-start | bytes 442376 | tf_op jit(solution)/shard_map/ppermute | solution.py:396
  26.5 0.1 collective-permute-start.6
  26.6 4.0 %collective-permute-done.4.refs_0_ = bf16[72,1024]{1,0:T(8,128)(2,1)S(1)} collective-permute-done((bf16[72,1024]{1,0:T(8,128)(2,1)S(1)}, bf16[72,1024]{1,0:T(8,128)(2,1)S(1)}, u32[]{:S(2)}, u32[]{:S(2)}) %collective-permute-start.4) | collective-permute-done | bytes 147488 | tf_op jit(solution)/shard_map/ppermute | solution.py:396
  30.6 2.7 %collective-permute-done.5.refs_1_ = bf16[72,1024]{1,0:T(8,128)(2,1)S(1)} collective-permute-done((bf16[72,1024]{1,0:T(8,128)(2,1)S(1)}, bf16[72,1024]{1,0:T(8,128)(2,1)S(1)}, u32[]{:S(2)}, u32[]{:S(2)}) %collective-permute-start.5) | collective-permute-done | bytes 147488 | tf_op jit(solution)/shard_map/ppermute | solution.py:396
  33.3 0.3 collective-permute-done.6.refs_2_
  33.5 0.1 line_parts.1
  33.7 1.6 %collective-permute-start.7 = (bf16[80,256]{1,0:T(8,128)(2,1)S(1)}, bf16[80,256]{1,0:T(8,128)(2,1)S(1)}, u32[]{:S(2)}, u32[]{:S(2)}) collective-permute-start(bf16[80,256]{1,0:T(8,128)(2,1)S(1)} %get-tuple-element.45), channel_id=1, source_target_pairs={{0,2},{1,3},{2,0},{3,1},{4,6},{5,7},{6,4},{7,5},{8,10},{9,11},{10,... | collective-permute-start | bytes 122888 | tf_op jit(solution)/shard_map/ppermute | solution.py:176
  35.3 2.6 %collective-permute-start.8 = (bf16[80,256]{1,0:T(8,128)(2,1)S(1)}, bf16[80,256]{1,0:T(8,128)(2,1)S(1)}, u32[]{:S(2)}, u32[]{:S(2)}) collective-permute-start(bf16[80,256]{1,0:T(8,128)(2,1)S(1)} %get-tuple-element.46), channel_id=1, source_target_pairs={{0,4},{1,5},{2,6},{3,7},{4,0},{5,1},{6,2},{7,3},{8,12},{9,13},{10,... | collective-permute-start | bytes 122888 | tf_op jit(solution)/shard_map/ppermute | solution.py:176
  37.9 0.2 collective-permute-start.9
  38.1 0.0 collective-permute-done.7.refs_0_
  38.1 2.9 %collective-permute-done.8.refs_1_ = bf16[80,256]{1,0:T(8,128)(2,1)S(1)} collective-permute-done((bf16[80,256]{1,0:T(8,128)(2,1)S(1)}, bf16[80,256]{1,0:T(8,128)(2,1)S(1)}, u32[]{:S(2)}, u32[]{:S(2)}) %collective-permute-start.8) | collective-permute-done | bytes 40992 | tf_op jit(solution)/shard_map/ppermute | solution.py:176
  41.1 2.6 %collective-permute-done.9.refs_2_ = bf16[80,256]{1,0:T(8,128)(2,1)S(1)} collective-permute-done((bf16[80,256]{1,0:T(8,128)(2,1)S(1)}, bf16[80,256]{1,0:T(8,128)(2,1)S(1)}, u32[]{:S(2)}, u32[]{:S(2)}) %collective-permute-start.9) | collective-permute-done | bytes 40992 | tf_op jit(solution)/shard_map/ppermute | solution.py:176
  43.7 0.7 %last_sums.1 = (f32[64,256]{1,0:T(8,128)}, f32[16,128]{1,0:T(8,128)}, f32[16,128]{1,0:T(8,128)}) custom-call(f32[64,256]{1,0:T(8,128)S(1)} %get-tuple-element.43.total_ref, f32[16,256]{1,0:T(8,128)S(1)} %get-tuple-element.44.rows_ref, bf16[80,256]{1,0:T(8,128)(2,1)S(1)} %collective-permute-done.7.refs_0_, ...), custom_call_target="tpu_custom_call" | custom-call | tf_op jit(solution)/shard_map/last_sums/pallas_call | solution.py:340
  (2 shorter events, 0.1 us)
Async XLA Ops:
  0.6 10.8 %copy-start.3 = (bf16[1,128,2048]{2,1,0:T(8,128)(2,1)S(1)}, bf16[1,128,2048]{2,1,0:T(8,128)(2,1)}, u32[]{:S(2)}) copy-start(bf16[1,128,2048]{2,1,0:T(8,128)(2,1)} %param.7) | copy-start | bytes 1572868
  0.6 10.8 %copy-start.4 = (bf16[1,128,2048]{2,1,0:T(8,128)(2,1)S(1)}, bf16[1,128,2048]{2,1,0:T(8,128)(2,1)}, u32[]{:S(2)}) copy-start(bf16[1,128,2048]{2,1,0:T(8,128)(2,1)} %param.13) | copy-start | bytes 1572868
  2.0 9.4 %copy-start.6 = (f32[2048]{0:T(1024)S(1)}, f32[2048]{0:T(1024)}, u32[]{:S(2)}) copy-start(f32[2048]{0:T(1024)} %param.12) | copy-start | bytes 24580
  2.0 9.4 %copy-start.2 = (bf16[256,2048]{1,0:T(8,128)(2,1)S(1)}, bf16[256,2048]{1,0:T(8,128)(2,1)}, u32[]{:S(2)}) copy-start(bf16[256,2048]{1,0:T(8,128)(2,1)} %rel_ref.3) | copy-start | bytes 3145732
  2.1 9.3 %collective-permute-start.1 = (bf16[256,1024]{1,0:T(8,128)(2,1)S(1)}, bf16[256,1024]{1,0:T(8,128)(2,1)S(1)}, u32[]{:S(2)}, u32[]{:S(2)}) collective-permute-start(bf16[256,1024]{1,0:T(8,128)(2,1)S(1)} %pad_maximum_fusion.1), channel_id=1, source_target_pairs={{0,8},{8,16},{16,24},{24,0},{1,9},{9,17},{17,25},{25,1},{2,10},{10... | collective-permute-start | bytes 1572872 | tf_op jit(solution)/shard_map/ppermute | solution.py:172
  2.6 8.8 %copy-start = (bf16[1,128,2048]{2,1,0:T(8,128)(2,1)S(1)}, bf16[1,128,2048]{2,1,0:T(8,128)(2,1)}, u32[]{:S(2)}) copy-start(bf16[1,128,2048]{2,1,0:T(8,128)(2,1)} %param.8) | copy-start | bytes 1572868
  2.6 8.9 %copy-start.1 = (bf16[1,128,2048]{2,1,0:T(8,128)(2,1)S(1)}, bf16[1,128,2048]{2,1,0:T(8,128)(2,1)}, u32[]{:S(2)}) copy-start(bf16[1,128,2048]{2,1,0:T(8,128)(2,1)} %param.9) | copy-start | bytes 1572868
  2.6 8.8 %copy-start.5 = (f32[2048]{0:T(1024)S(1)}, f32[2048]{0:T(1024)}, u32[]{:S(2)}) copy-start(f32[2048]{0:T(1024)} %param.11) | copy-start | bytes 24580
  2.7 14.4 %collective-permute-start = (bf16[256,1024]{1,0:T(8,128)(2,1)S(1)}, bf16[256,1024]{1,0:T(8,128)(2,1)S(1)}, u32[]{:S(2)}, u32[]{:S(2)}) collective-permute-start(bf16[256,1024]{1,0:T(8,128)(2,1)S(1)} %pad_maximum_fusion), channel_id=1, source_target_pairs={{0,8},{8,16},{16,24},{24,0},{1,9},{9,17},{17,25},{25,1},{2,10},{10... | collective-permute-start | bytes 1572872 | tf_op jit(solution)/shard_map/ppermute | solution.py:172
  20.5 1.6 %collective-permute-start.3 = (bf16[136,1024]{1,0:T(8,128)(2,1)S(1)}, bf16[136,1024]{1,0:T(8,128)(2,1)S(1)}, u32[]{:S(2)}, u32[]{:S(2)}) collective-permute-start(bf16[136,1024]{1,0:T(8,128)(2,1)S(1)} %get-tuple-element.35), channel_id=1, source_target_pairs={{0,8},{8,0},{16,24},{24,16},{1,9},{9,1},{17,25},{25,17},{2,10},{10... | collective-permute-start | bytes 835592 | tf_op jit(solution)/shard_map/ppermute | solution.py:176
  20.5 2.0 %collective-permute-start.2 = (bf16[136,1024]{1,0:T(8,128)(2,1)S(1)}, bf16[136,1024]{1,0:T(8,128)(2,1)S(1)}, u32[]{:S(2)}, u32[]{:S(2)}) collective-permute-start(bf16[136,1024]{1,0:T(8,128)(2,1)S(1)} %get-tuple-element.34), channel_id=1, source_target_pairs={{0,8},{8,0},{16,24},{24,16},{1,9},{9,1},{17,25},{25,17},{2,10},{10... | collective-permute-start | bytes 835592 | tf_op jit(solution)/shard_map/ppermute | solution.py:176
  22.7 7.9 %collective-permute-start.4 = (bf16[72,1024]{1,0:T(8,128)(2,1)S(1)}, bf16[72,1024]{1,0:T(8,128)(2,1)S(1)}, u32[]{:S(2)}, u32[]{:S(2)}) collective-permute-start(bf16[72,1024]{1,0:T(8,128)(2,1)S(1)} %get-tuple-element.40), channel_id=1, source_target_pairs={{0,17},{1,16},{2,19},{3,18},{4,21},{5,20},{6,23},{7,22},{8,25},{9,... | collective-permute-start | bytes 442376 | tf_op jit(solution)/shard_map/ppermute | solution.py:396
  26.0 7.3 %collective-permute-start.5 = (bf16[72,1024]{1,0:T(8,128)(2,1)S(1)}, bf16[72,1024]{1,0:T(8,128)(2,1)S(1)}, u32[]{:S(2)}, u32[]{:S(2)}) collective-permute-start(bf16[72,1024]{1,0:T(8,128)(2,1)S(1)} %get-tuple-element.41), channel_id=1, source_target_pairs={{0,16},{1,17},{2,18},{3,19},{4,20},{5,21},{6,22},{7,23},{8,24},{9,... | collective-permute-start | bytes 442376 | tf_op jit(solution)/shard_map/ppermute | solution.py:396
  26.5 7.1 %collective-permute-start.6 = (bf16[72,1024]{1,0:T(8,128)(2,1)S(1)}, bf16[72,1024]{1,0:T(8,128)(2,1)S(1)}, u32[]{:S(2)}, u32[]{:S(2)}) collective-permute-start(bf16[72,1024]{1,0:T(8,128)(2,1)S(1)} %get-tuple-element.42), channel_id=1, source_target_pairs={{0,1},{1,0},{2,3},{3,2},{4,5},{5,4},{6,7},{7,6},{8,9},{9,8},{10,11... | collective-permute-start | bytes 442376 | tf_op jit(solution)/shard_map/ppermute | solution.py:396
  33.7 4.5 %collective-permute-start.7 = (bf16[80,256]{1,0:T(8,128)(2,1)S(1)}, bf16[80,256]{1,0:T(8,128)(2,1)S(1)}, u32[]{:S(2)}, u32[]{:S(2)}) collective-permute-start(bf16[80,256]{1,0:T(8,128)(2,1)S(1)} %get-tuple-element.45), channel_id=1, source_target_pairs={{0,2},{1,3},{2,0},{3,1},{4,6},{5,7},{6,4},{7,5},{8,10},{9,11},{10,... | collective-permute-start | bytes 122888 | tf_op jit(solution)/shard_map/ppermute | solution.py:176
  35.3 5.8 %collective-permute-start.8 = (bf16[80,256]{1,0:T(8,128)(2,1)S(1)}, bf16[80,256]{1,0:T(8,128)(2,1)S(1)}, u32[]{:S(2)}, u32[]{:S(2)}) collective-permute-start(bf16[80,256]{1,0:T(8,128)(2,1)S(1)} %get-tuple-element.46), channel_id=1, source_target_pairs={{0,4},{1,5},{2,6},{3,7},{4,0},{5,1},{6,2},{7,3},{8,12},{9,13},{10,... | collective-permute-start | bytes 122888 | tf_op jit(solution)/shard_map/ppermute | solution.py:176
  37.9 5.8 %collective-permute-start.9 = (bf16[80,256]{1,0:T(8,128)(2,1)S(1)}, bf16[80,256]{1,0:T(8,128)(2,1)S(1)}, u32[]{:S(2)}, u32[]{:S(2)}) collective-permute-start(bf16[80,256]{1,0:T(8,128)(2,1)S(1)} %get-tuple-element.47), channel_id=1, source_target_pairs={{0,6},{1,7},{2,4},{3,5},{4,2},{5,3},{6,0},{7,1},{8,14},{9,15},{10,... | collective-permute-start | bytes 122888 | tf_op jit(solution)/shard_map/ppermute | solution.py:176

commit v4 on v3

--- a/solution.py
+++ b/solution.py
@@ -11,6 +11,8 @@
 LOG2_E = 1.4426950408889634
 GROUP = 4
 CHUNKS = (1024, 1024)
+VMEM_BYTES = 24 * 1024 * 1024
+SCORE_SCALE = DH ** (-0.5)
 BIAS_ROWS = 8
 DIRECT_PEERS = 8
 
@@ -24,143 +26,204 @@
     )
 
 
-def attention_kernel(
-    aliased,
-    q_ref,
-    k_ref,
-    v_ref,
-    memory_ref,
-    rel_ref,
-    bias_u_ref,
-    bias_v_ref,
-    d_out_ref,
-    *out_refs,
-):
-    d_q_ref, d_k_ref, keep_ref, send_ref, bias_ref = out_refs[aliased:]
-
+def local_kernel(q_ref, k_ref, rel_ref, bias_u_ref, bias_v_ref, score_ref, content_ref, flipped_ref):
     seg_rows = q_ref.shape[0]
-    mem_len = memory_ref.shape[0] // 2
-    key_count = seg_rows + mem_len
-    pair_count, part_rows, _ = keep_ref.shape
-    seg_index = lax.axis_index("seg")
-    first_key = jnp.where(seg_index > 0, 0, mem_len)
-    odd = jnp.bitwise_and(seg_index, 1) == 1
+    key_count = rel_ref.shape[0]
+    mem_len = key_count - seg_rows
+    first_key = jnp.where(lax.axis_index("seg") > 0, 0, mem_len)
     row_index = lax.broadcasted_iota(jnp.int32, (seg_rows, key_count), 0)
     key_index = lax.broadcasted_iota(jnp.int32, (seg_rows, key_count), 1)
     allowed = (key_index <= row_index + mem_len) & (key_index >= first_key)
-
-    flip_row = lax.broadcasted_iota(jnp.int32, (seg_rows, seg_rows), 0)
-    flip_col = lax.broadcasted_iota(jnp.int32, (seg_rows, seg_rows), 1)
-    flip = (flip_row + flip_col == seg_rows - 1).astype(jnp.bfloat16)
-    score_scale = DH ** (-0.5)
-    heads = range(q_ref.shape[1] // DH)
-    def group_grads(group):
-        cols = [slice(h * DH, (h + 1) * DH) for h in group]
-        n = range(len(group))
-        q_wide = [q_ref[:, c].astype(jnp.float32) for c in cols]
-        q_content = [(q_wide[t] + bias_u_ref[:, cols[t]]).astype(jnp.bfloat16) for t in n]
-        q_position = [(q_wide[t] + bias_v_ref[:, cols[t]]).astype(jnp.bfloat16) for t in n]
+    flip = row_flip(seg_rows)
+    for group in head_groups(0, q_ref.shape[1]):
+        cols = columns_of(group)
+        n = range(len(cols))
+        wide = [q_ref[:, c].astype(jnp.float32) for c in cols]
+        q_position = [(wide[t] + bias_v_ref[:, cols[t]]).astype(jnp.bfloat16) for t in n]
         by_distance = [contract(q_position[t], rel_ref[:, cols[t]], 1, 1) for t in n]
-        keys_all = [jnp.concatenate([memory_ref[:mem_len, c], k_ref[:, c]], 0) for c in cols]
-        content = [contract(q_content[t], keys_all[t], 1, 1) for t in n]
-        position = [pltpu.roll(by_distance[t], key_count - seg_rows + 1, 1, stride=1, stride_axis=0) for t in n]
-        values_all = [jnp.concatenate([memory_ref[mem_len:, c], v_ref[:, c]], 0) for c in cols]
+        q_content = [(wide[t] + bias_u_ref[:, cols[t]]).astype(jnp.bfloat16) for t in n]
+        content = [contract(q_content[t], k_ref[:, cols[t]], 1, 1) for t in n]
+        flipped = [contract(flip, q_position[t], 1, 0).astype(jnp.bfloat16) for t in n]
+        position = [
+            pltpu.roll(raw, key_count - seg_rows + 1, 1, stride=1, stride_axis=0) for raw in by_distance
+        ]
+        for t in n:
+            scores = jnp.concatenate(
+                [position[t][:, :mem_len], position[t][:, mem_len:] + content[t]], 1
+            )
+            score_ref[group[t]] = jnp.where(allowed, SCORE_SCALE * LOG2_E * scores, -1e30)
+            content_ref[:, cols[t]] = q_content[t]
+            flipped_ref[:, cols[t]] = flipped[t]
+
+
+def weights_kernel(score_ref, content_ref, k_mem_ref, weights_ref):
+    mem_len = k_mem_ref.shape[0]
+    for group in head_groups(0, content_ref.shape[1]):
+        cols = columns_of(group)
+        n = range(len(cols))
+        content = [contract(content_ref[:, c], k_mem_ref[:, c], 1, 1) for c in cols]
+        left = [score_ref[group[t], :, :mem_len] + SCORE_SCALE * LOG2_E * content[t] for t in n]
+        scores = [jnp.concatenate([left[t], score_ref[group[t], :, mem_len:]], 1) for t in n]
+        top = [jnp.max(score, axis=1, keepdims=True) for score in scores]
+        raised = [jnp.exp2(scores[t] - top[t]) for t in n]
+        total = [jnp.sum(each, axis=1, keepdims=True) for each in raised]
+        for t in n:
+            weights_ref[group[t]] = raised[t] * (SCORE_SCALE / total[t])
+
+
+def scores_kernel(
+    start,
+    weights_ref,
+    flipped_ref,
+    k_ref,
+    v_ref,
+    k_mem_ref,
+    v_mem_ref,
+    rel_ref,
+    d_out_ref,
+    grad_ref,
+    grad_rel_ref,
+    keep_ref,
+    send_ref,
+    bias_ref,
+):
+    seg_rows = k_ref.shape[0]
+    pair_count, part_rows, _ = keep_ref.shape
+    odd = jnp.bitwise_and(lax.axis_index("seg"), 1) == 1
+    flip = row_flip(seg_rows)
+    fill = jnp.zeros((BIAS_ROWS - 4, DH), jnp.bfloat16)
+    for group in head_groups(start, v_mem_ref.shape[1]):
+        cols = columns_of(group)
+        own = columns_of(group, start)
+        n = range(len(cols))
+        values_all = [
+            jnp.concatenate([v_mem_ref[:, own[t]], v_ref[:, cols[t]]], 0) for t in n
+        ]
         d_weights = [contract(d_out_ref[:, cols[t]], values_all[t], 1, 1) for t in n]
-        scores = [jnp.where(allowed, (score_scale * LOG2_E) * (content[t] + position[t]), -1e30) for t in n]
-        top = [jnp.max(s, axis=1, keepdims=True) for s in scores]
-        raised = [jnp.exp2(scores[t] - top[t]) for t in n]
-        total = [jnp.sum(r, axis=1, keepdims=True) for r in raised]
-        cross = [jnp.sum(raised[t] * d_weights[t], axis=1, keepdims=True) for t in n]
-        inverse = [1.0 / s for s in total]
-        grad_scores = [((raised[t] * (score_scale * inverse[t])) * (d_weights[t] - cross[t] * inverse[t])).astype(jnp.bfloat16) for t in n]
-        flipped = [contract(flip, g, 1, 0) for g in grad_scores]
-        grad_rel = [pltpu.roll(f, 0, 1, stride=1, stride_axis=0).astype(jnp.bfloat16) for f in flipped]
-        d_content = [contract(grad_scores[t], keys_all[t], 1, 0) for t in n]
+        scaled = [weights_ref[group[t]] * d_weights[t] for t in n]
+        mean = [jnp.sum(each, axis=1, keepdims=True) * (1.0 / SCORE_SCALE) for each in scaled]
+        grad = [(weights_ref[group[t]] * (d_weights[t] - mean[t])).astype(jnp.bfloat16) for t in n]
+        flipped = [contract(flip, each, 1, 0) for each in grad]
+        rolled = [pltpu.roll(each, 0, 1, stride=1, stride_axis=0) for each in flipped]
+        grad_rel = [each.astype(jnp.bfloat16) for each in rolled]
+        d_rel_all = [contract(grad_rel[t], flipped_ref[:, cols[t]], 0, 0) for t in n]
+        keys_all = [jnp.concatenate([k_mem_ref[:, c], k_ref[:, c]], 0) for c in cols]
+        content = [row_sum_product(flipped[t], keys_all[t]) for t in n]
+        position = [row_sum_product(rolled[t], rel_ref[:, cols[t]]) for t in n]
         for t in n:
-            d_k_ref[:, cols[t]] = contract(grad_scores[t][:, mem_len:], q_content[t], 0, 0).astype(jnp.bfloat16)
-        q_flip = [contract(flip, q_ref[:, c], 1, 0) for c in cols]
-        q_flip = [(q_flip[t] + bias_v_ref[:, cols[t]]).astype(jnp.bfloat16) for t in n]
-        grad_back = [contract(flip, g, 1, 0).astype(jnp.bfloat16) for g in grad_rel]
-        d_position = [contract(grad_back[t], rel_ref[:, cols[t]], 1, 0) for t in n]
-        d_rel_all = [contract(grad_rel[t], q_flip[t], 0, 0) for t in n]
-        for t in n:
-            c = cols[t]
-            d_q_ref[:, c] = (d_content[t] + d_position[t]).astype(jnp.bfloat16)
-            sums = jnp.concatenate(
-                [jnp.sum(d_content[t], 0, keepdims=True), jnp.sum(d_position[t], 0, keepdims=True)], 0
-            )
+            c = own[t]
+            grad_ref[group[t] - start // DH] = grad[t]
+            grad_rel_ref[group[t] - start // DH] = grad_rel[t]
+            sums = jnp.concatenate([content[t], position[t]], 0)
             bias_ref[:, c] = sums
-            high = sums.astype(jnp.bfloat16)
-            low = (sums - high.astype(jnp.float32)).astype(jnp.bfloat16)
-            fill = jnp.zeros((BIAS_ROWS - 4, DH), jnp.bfloat16)
+            high, low = split_bias(sums)
             d_rel = d_rel_all[t]
             for pair in range(pair_count):
-                start = 2 * pair * part_rows
-                even_part = d_rel[start : start + part_rows]
-                odd_part = d_rel[start + part_rows : start + 2 * part_rows]
+                at = 2 * pair * part_rows
+                even_part = d_rel[at : at + part_rows]
+                odd_part = d_rel[at + part_rows : at + 2 * part_rows]
                 keep_ref[pair, :, c] = jnp.where(odd, odd_part, even_part)
                 send_ref[pair * part_rows : (pair + 1) * part_rows, c] = jnp.where(
                     odd, even_part, odd_part
                 ).astype(jnp.bfloat16)
             send_ref[pair_count * part_rows :, c] = jnp.concatenate([high, low, fill], 0)
 
-    for first in range(0, len(heads), GROUP):
-        group_grads(heads[first:first+GROUP])
-
-
-def attention(start, span, grads, queries, keys, values, memory, rest):
-    rel_keys, bias_u, bias_v, d_out = rest
+
+def row_sum_product(left, right):
+    rest = jnp.sum(left, 0, keepdims=True)
+    parts = []
+    for _ in range(3):
+        part = rest.astype(jnp.bfloat16)
+        rest = rest - part.astype(jnp.float32)
+        parts.append(part)
+    fill = jnp.zeros((5, left.shape[1]), jnp.bfloat16)
+    return jnp.sum(contract(jnp.concatenate([*parts, fill], 0), right, 1, 0), 0, keepdims=True)
+
+
+def rows_kernel(chunk_count, *refs):
+    grad_refs, grad_rel_refs = refs[:chunk_count], refs[chunk_count : 2 * chunk_count]
+    content_ref, k_ref, k_mem_ref, rel_ref, d_q_ref, d_k_ref = refs[2 * chunk_count :]
+    mem_len = k_mem_ref.shape[0]
+    flip = row_flip(k_ref.shape[0])
+    heads = [(n, head) for n, ref in enumerate(grad_refs) for head in range(ref.shape[0])]
+    for group in head_groups(0, k_ref.shape[1]):
+        cols = columns_of(group)
+        places = [heads[head] for head in group]
+        n = range(len(cols))
+        grad = [grad_refs[chunk][head] for chunk, head in places]
+        back = [
+            contract(flip, grad_rel_refs[chunk][head], 1, 0).astype(jnp.bfloat16)
+            for chunk, head in places
+        ]
+        keys_all = [jnp.concatenate([k_mem_ref[:, c], k_ref[:, c]], 0) for c in cols]
+        d_content = [contract(grad[t], keys_all[t], 1, 0) for t in n]
+        d_key = [contract(grad[t][:, mem_len:], content_ref[:, cols[t]], 0, 0) for t in n]
+        d_position = [contract(back[t], rel_ref[:, cols[t]], 1, 0) for t in n]
+        for t in n:
+            d_q_ref[:, cols[t]] = (d_content[t] + d_position[t]).astype(jnp.bfloat16)
+            d_k_ref[:, cols[t]] = d_key[t].astype(jnp.bfloat16)
+
+
+def row_flip(rows):
+    row = lax.broadcasted_iota(jnp.int32, (rows, rows), 0)
+    col = lax.broadcasted_iota(jnp.int32, (rows, rows), 1)
+    return (row + col == rows - 1).astype(jnp.bfloat16)
+
+
+def head_groups(start, span):
+    heads = range(start // DH, (start + span) // DH)
+    return [heads[at : at + GROUP] for at in range(0, len(heads), GROUP)]
+
+
+def columns_of(heads, start=0):
+    return [slice(head * DH - start, (head + 1) * DH - start) for head in heads]
+
+
+def local_scores(queries, keys, rel_keys, bias_u, bias_v):
     seg_rows, width = queries.shape
-    key_count = rel_keys.shape[0]
+    rows = ((seg_rows, width), jnp.bfloat16)
+    scores = ((width // DH, seg_rows, rel_keys.shape[0]), jnp.float32)
+    operands = queries, keys, rel_keys, bias_u[None], bias_v[None]
+    return whole_call(local_kernel, "local_scores", [scores, rows, rows], *operands)
+
+
+def soft_weights(scores, q_content, key_memory):
+    shape = [(scores.shape, jnp.float32)]
+    return whole_call(weights_kernel, "soft_weights", shape, scores, q_content, key_memory)[0]
+
+
+def score_grads(start, span, shared, value_memory):
+    weights, q_flipped, keys, values, key_memory, rel_keys, d_out = shared
     seg_count = lax.axis_size("seg")
     pair_count = seg_count // 2
-    part_rows = key_count // seg_count
-    step_cols = GROUP * DH
-    first = start // step_cols
-
-    def block(rows):
-        return pl.BlockSpec((rows, step_cols), lambda step: (0, first + step))
-
-    def own(rows):
-        return pl.BlockSpec((rows, step_cols), lambda step: (0, step))
-
-    mem_len = key_count - seg_rows
-    send_rows = pair_count * part_rows + BIAS_ROWS
-    in_place = pl.BlockSpec(memory_space=pl.ANY)
-    return pl.pallas_call(
-        functools.partial(attention_kernel, len(grads)),
-        name="attention_grads",
-        grid=(span // step_cols,),
-        in_specs=[block(seg_rows)] * 3
-        + [own(2 * mem_len), block(key_count), block(1), block(1), block(seg_rows)]
-        + [in_place] * len(grads),
-        out_specs=[
-            block(seg_rows),
-            block(seg_rows),
-            pl.BlockSpec((pair_count, part_rows, step_cols), lambda step: (0, 0, step)),
-            own(send_rows),
-            own(2),
+    part_rows = rel_keys.shape[0] // seg_count
+    grad = ((span // DH, *weights.shape[1:]), jnp.bfloat16)
+    return whole_call(
+        functools.partial(scores_kernel, start),
+        "score_grads",
+        [
+            grad,
+            grad,
+            ((pair_count, part_rows, span), jnp.float32),
+            ((pair_count * part_rows + BIAS_ROWS, span), jnp.bfloat16),
+            ((2, span), jnp.float32),
         ],
-        out_shape=[
-            jax.ShapeDtypeStruct((seg_rows, width), jnp.bfloat16),
-            jax.ShapeDtypeStruct((seg_rows, width), jnp.bfloat16),
-            jax.ShapeDtypeStruct((pair_count, part_rows, span), jnp.float32),
-            jax.ShapeDtypeStruct((send_rows, span), jnp.bfloat16),
-            jax.ShapeDtypeStruct((2, span), jnp.float32),
-        ],
-        input_output_aliases={8 + n: n for n in range(len(grads))},
-        compiler_params=pltpu.CompilerParams(
-            dimension_semantics=("arbitrary",), vmem_limit_bytes=48 * 1024 * 1024
-        ),
-    )(
-        *(in_vmem(block) for block in (queries, keys, values)),
-        memory,
-        in_vmem(rel_keys),
-        bias_u[None],
-        bias_v[None],
-        in_vmem(d_out),
-        *grads,
-    )
+        weights,
+        q_flipped,
+        keys,
+        values,
+        key_memory,
+        value_memory,
+        rel_keys,
+        d_out,
+    )
+
+
+def row_grads(grads, grads_rel, q_content, keys, key_memory, rel_keys):
+    rows = (keys.shape, jnp.bfloat16)
+    operands = *grads, *grads_rel, q_content, keys, key_memory, rel_keys
+    kernel = functools.partial(rows_kernel, len(grads))
+    return whole_call(kernel, "row_grads", [rows, rows], *operands)
 
 
 def in_vmem(block):
@@ -341,7 +404,7 @@
         kernel,
         name=name,
         out_shape=[jax.ShapeDtypeStruct(*shape) for shape in out_shape],
-        compiler_params=pltpu.CompilerParams(vmem_limit_bytes=48 * 1024 * 1024),
+        compiler_params=pltpu.CompilerParams(vmem_limit_bytes=VMEM_BYTES),
     )(*operands)
 
 
@@ -400,32 +463,26 @@
     seg_rows, width = queries.shape[1:]
     mem_len = rel_keys.shape[0] - seg_rows
     edges = [(sum(CHUNKS[:n]), span) for n, span in enumerate(CHUNKS)]
-    memory = [
-        from_behind(
-            jnp.concatenate(
-                [
-                    block[0, seg_rows - mem_len :, start : start + span]
-                    for block in (keys, values)
-                ],
-                0,
-            ),
-            "seg",
-        )
+    key_memory = from_behind(keys[0, seg_rows - mem_len :], "seg")
+    value_memory = [
+        from_behind(values[0, seg_rows - mem_len :, start : start + span], "seg")
         for start, span in edges
     ]
-    grads, keeps, sends, sums = (), [], [], []
-    for (start, span), block in zip(edges, memory):
-        rest = rel_keys, bias_u, bias_v, d_out[0]
-        *grads, keep, send, sum_pair = attention(
-            start, span, grads, queries[0], keys[0], values[0], block, rest
-        )
-        keeps.append(keep)
-        sends.append(send)
-        sums.append(sum_pair)
+    own_q, own_k, own_v, rel_keys, own_d = (
+        in_vmem(block) for block in (queries[0], keys[0], values[0], rel_keys, d_out[0])
+    )
+    scores, q_content, q_flipped = local_scores(own_q, own_k, rel_keys, bias_u, bias_v)
+    weights = soft_weights(scores, q_content, key_memory)
+    shared = weights, q_flipped, own_k, own_v, key_memory, rel_keys, own_d
+    parts = [
+        score_grads(start, span, shared, block) for (start, span), block in zip(edges, value_memory)
+    ]
+    grads, grads_rel, keeps, sends, sums = zip(*parts)
     planes = lax.axis_size("seg") == 4 and lax.axis_size("dp") == 8
     reduce = reduce_by_planes if planes else reduce_by_halves
     total, sums = reduce(keeps, sends, sums)
-    return (grads[0][None], grads[1][None], total, sums[0], sums[1])
+    d_query, d_key = row_grads(grads, grads_rel, q_content, own_k, key_memory, rel_keys)
+    return (d_query[None], d_key[None], total, sums[0], sums[1])
 
 
 def solution(mesh):

time: 44.5 us -> 41.3 us (0.928)
  waiting for transfers between devices: 22.2 us -> 14.1 us
  local copies, waits for them, and re-layouts: 1.41 us -> 5.79 us
  Pallas kernels: 7.84 us -> 8.52 us
    pallas_call x3 -> x8, Pallas kernels: 0.95 us -> 8.52 us  [whole_call(): pl.pallas_call(kernel, name=name, out_shape=[jax.ShapeDtypeStruct(*shape)...]
    pallas_call x2 -> x0, Pallas kernels: 6.88 us -> none  [attention(): pl.pallas_call(functools.partial(attention_kernel, len(grads)), name='att...]
    ppermute x2 -> x3, waiting for transfers between devices: 8.22 us -> 2.24 us  [from_behind(): lax.ppermute(block, axis, [(i, (i + 1) % count) for i in range(count)])]
    unnamed x14 -> x18, local copies, waits for them, and re-layouts: 0.03 us -> 4.72 us
    ppermute x5, waiting for transfers between devices: 7.03 us -> 4.94 us  [swap(): lax.ppermute(block, axis, [(i, i ^ flip) for i in range(lax.axis_size(axi...]
    ppermute x2 -> x3, starting transfers between devices: 3.19 us -> 3.25 us  [from_behind(): lax.ppermute(block, axis, [(i, (i + 1) % count) for i in range(count)])]
  transfers between devices with their start and end apart: 10 -> 11, of which waited for: 9 -> 8; matrix products, arithmetic and copies ran while one was open for 0% -> 3% of each run, Pallas kernels for 8% -> 18%
where the time goes in v4:
time: 41.3 us; the launch traced here: 41 us
  waiting for transfers between devices  14.1 us (34%)
  starting transfers between devices  11.8 us (29%)
  Pallas kernels  8.52 us (21%)
  local copies, waits for them, and re-layouts  5.79 us (14%)
  between operations  0.76 us (2%)
    pallas_call x8, Pallas kernels, whole_call(): pl.pallas_call(kernel, name=name, out_shape=[jax.ShapeDtypeStruct(*shape)...  8.52 us
    ppermute x3, waiting for transfers between devices, swap_both(): return lax.ppermute(block, ('seg', 'dp'), route)  6.96 us
    ppermute x5, waiting for transfers between devices, swap(): lax.ppermute(block, axis, [(i, i ^ flip) for i in range(lax.axis_size(axi...  4.94 us
    unnamed x18, local copies, waits for them, and re-layouts  4.72 us
    ppermute x5, starting transfers between devices, swap(): lax.ppermute(block, axis, [(i, i ^ flip) for i in range(lax.axis_size(axi...  4.59 us
    ppermute x3, starting transfers between devices, swap_both(): return lax.ppermute(block, ('seg', 'dp'), route)  3.93 us
    ppermute x3, starting transfers between devices, from_behind(): lax.ppermute(block, axis, [(i, (i + 1) % count) for i in range(count)])  3.25 us
    ppermute x3, waiting for transfers between devices, from_behind(): lax.ppermute(block, axis, [(i, (i + 1) % count) for i in range(count)])  2.24 us
  transfers between devices with their start and end apart: 11, of which 8 were waited for; matrix products, arithmetic and copies ran while one was open for 3% of the time, Pallas kernels for 18%

profile of v4, /device:TPU:0, one launch (start us, length us, event | category | flops | bytes accessed | tf_op | source)
XLA Modules:
  0.0 41.0 jit_solution(12570995987271261007)
XLA Ops:
  0.6 0.5 %collective-permute-start = (bf16[128,2048]{1,0:T(8,128)(2,1)}, bf16[128,2048]{1,0:T(8,128)(2,1)S(1)}, u32[]{:S(2)}, u32[]{:S(2)}) collective-permute-start(bf16[128,2048]{1,0:T(8,128)(2,1)} %bitcast.14), channel_id=1, source_target_pairs={{0,8},{8,16},{16,24},{24,0},{1,9},{9,17},{17,25},{25,1},{2,10},{10... | collective-permute-start | bytes 1572872 | tf_op jit(solution)/shard_map/ppermute | solution.py:235
  1.1 1.1 %slice_bitcast_fusion = (bf16[128,1024]{1,0:T(8,128)(2,1)S(1)}, bf16[128,1024]{1,0:T(8,128)(2,1)S(1)}) fusion(bf16[1,128,2048]{2,1,0:T(8,128)(2,1)} %param.9), kind=kLoop, calls=%fused_computation | loop fusion | bytes 1048576 | tf_op jit(solution)/shard_map/squeeze | solution.py:468
  2.2 2.7 %collective-permute-start.2 = (bf16[128,1024]{1,0:T(8,128)(2,1)S(1)}, bf16[128,1024]{1,0:T(8,128)(2,1)S(1)}, u32[]{:S(2)}, u32[]{:S(2)}) collective-permute-start(bf16[128,1024]{1,0:T(8,128)(2,1)S(1)} %get-tuple-element.61), channel_id=1, source_target_pairs={{0,8},{8,16},{16,24},{24,0},{1,9},{9,17},{17,25},{25,1},{2,10},{10... | collective-permute-start | bytes 786440 | tf_op jit(solution)/shard_map/ppermute | solution.py:235
  4.9 0.1 collective-permute-start.1
  4.9 0.0 copy-start
  5.0 1.2 %copy-done = bf16[256,2048]{1,0:T(8,128)(2,1)S(1)} copy-done((bf16[256,2048]{1,0:T(8,128)(2,1)S(1)}, bf16[256,2048]{1,0:T(8,128)(2,1)}, u32[]{:S(2)}) %copy-start) | copy-done | bytes 1048600
  6.2 0.0 copy-start.2
  6.2 1.0 %copy-done.2 = bf16[1,128,2048]{2,1,0:T(8,128)(2,1)S(1)} copy-done((bf16[1,128,2048]{2,1,0:T(8,128)(2,1)S(1)}, bf16[1,128,2048]{2,1,0:T(8,128)(2,1)}, u32[]{:S(2)}) %copy-start.2) | copy-done | bytes 524312
  7.2 0.0 copy-start.6
  7.2 1.0 %copy-done.6 = bf16[1,128,2048]{2,1,0:T(8,128)(2,1)S(1)} copy-done((bf16[1,128,2048]{2,1,0:T(8,128)(2,1)S(1)}, bf16[1,128,2048]{2,1,0:T(8,128)(2,1)}, u32[]{:S(2)}) %copy-start.6) | copy-done | bytes 524312
  8.3 0.0 copy-start.7
  8.3 0.7 %copy-done.7 = f32[2048]{0:T(1024)S(1)} copy-done((f32[2048]{0:T(1024)S(1)}, f32[2048]{0:T(1024)}, u32[]{:S(2)}) %copy-start.7) | copy-done | bytes 8216
  9.0 0.0 copy-start.8
  9.0 0.7 %copy-done.8 = f32[2048]{0:T(1024)S(1)} copy-done((f32[2048]{0:T(1024)S(1)}, f32[2048]{0:T(1024)}, u32[]{:S(2)}) %copy-start.8) | copy-done | bytes 8216
  9.7 1.1 %local_scores.1 = (f32[16,128,256]{2,1,0:T(8,128)S(1)}, bf16[128,2048]{1,0:T(8,128)(2,1)S(1)}, bf16[128,2048]{1,0:T(8,128)(2,1)S(1)}) custom-call(bf16[128,2048]{1,0:T(8,128)(2,1)S(1)} %bitcast.23, bf16[128,2048]{1,0:T(8,128)(2,1)S(1)} %bitcast.15, bf16[256,2048]{1,0:T(8,128)(2,1)S(1)} %copy-done, f32[1,2048]{1,0:T(1,128)S(1)} %bitcast.24, ...), custom_call_target="tpu_custom_call" | custom-call | tf_op jit(solution)/shard_map/local_scores/pallas_call | solution.py:403
  10.8 0.0 collective-permute-done.k_mem_ref.refs_6_
  10.8 0.0 copy-start.1
  10.8 0.0 copy-start.3
  10.8 0.0 copy-start.4
  10.8 0.0 copy-start.5
  10.8 0.9 %soft_weights.1.weights_ref = f32[16,128,256]{2,1,0:T(8,128)S(1)} custom-call(f32[16,128,256]{2,1,0:T(8,128)S(1)} %get-tuple-element.33.score_ref, bf16[128,2048]{1,0:T(8,128)(2,1)S(1)} %get-tuple-element.34.content_ref.refs_4_, bf16[128,2048]{1,0:T(8,128)(2,1)S(1)} %collective-permute-done.k_mem_ref.refs_6_), custom_call_target="tpu_custom_call" | custom-call | tf_op jit(solution)/shard_map/soft_weights/pallas_call | solution.py:403
  11.7 1.2 %collective-permute-done.2.v_mem_ref = bf16[128,1024]{1,0:T(8,128)(2,1)S(1)} collective-permute-done((bf16[128,1024]{1,0:T(8,128)(2,1)S(1)}, bf16[128,1024]{1,0:T(8,128)(2,1)S(1)}, u32[]{:S(2)}, u32[]{:S(2)}) %collective-permute-start.2) | collective-permute-done | bytes 262176 | tf_op jit(solution)/shard_map/ppermute | solution.py:235
  13.0 0.0 copy-done.1
  13.0 0.0 copy-done.3
  13.0 0.0 copy-done.4
  13.0 0.0 copy-done.5
  13.0 1.7 %score_grads.3 = (bf16[8,128,256]{2,1,0:T(8,128)(2,1)S(1)}, bf16[8,128,256]{2,1,0:T(8,128)(2,1)S(1)}, f32[2,64,1024]{2,1,0:T(8,128)S(1)}, bf16[136,1024]{1,0:T(8,128)(2,1)S(1)}, f32[2,1024]{1,0:T(2,128)S(1)}) custom-call(f32[16,128,256]{2,1,0:T(8,128)S(1)} %soft_weights.1.weights_ref, bf16[128,2048]{1,0:T(8,128)(2,1)S(1)} %get-tuple-element.35.flipped_ref, ...), custom_call_target="tpu_custom_call" | custom-call | tf_op jit(solution)/shard_map/score_grads/pallas_call | solution.py:403
  14.7 0.1 collective-permute-start.4
  14.8 1.0 %collective-permute-done.1.v_mem_ref = bf16[128,1024]{1,0:T(8,128)(2,1)S(1)} collective-permute-done((bf16[128,1024]{1,0:T(8,128)(2,1)S(1)}, bf16[128,1024]{1,0:T(8,128)(2,1)S(1)}, u32[]{:S(2)}, u32[]{:S(2)}) %collective-permute-start.1) | collective-permute-done | bytes 262176 | tf_op jit(solution)/shard_map/ppermute | solution.py:235
  15.8 1.7 %score_grads.2 = (bf16[8,128,256]{2,1,0:T(8,128)(2,1)S(1)}, bf16[8,128,256]{2,1,0:T(8,128)(2,1)S(1)}, f32[2,64,1024]{2,1,0:T(8,128)S(1)}, bf16[136,1024]{1,0:T(8,128)(2,1)S(1)}, f32[2,1024]{1,0:T(2,128)S(1)}) custom-call(f32[16,128,256]{2,1,0:T(8,128)S(1)} %soft_weights.1.weights_ref, bf16[128,2048]{1,0:T(8,128)(2,1)S(1)} %get-tuple-element.35.flipped_ref, ...), custom_call_target="tpu_custom_call" | custom-call | tf_op jit(solution)/shard_map/score_grads/pallas_call | solution.py:403
  17.5 0.1 collective-permute-start.3
  17.6 0.0 collective-permute-done.4.refs_3_
  17.6 1.5 %collective-permute-done.3.refs_2_ = bf16[136,1024]{1,0:T(8,128)(2,1)S(1)} collective-permute-done((bf16[136,1024]{1,0:T(8,128)(2,1)S(1)}, bf16[136,1024]{1,0:T(8,128)(2,1)S(1)}, u32[]{:S(2)}, u32[]{:S(2)}) %collective-permute-start.3) | collective-permute-done | bytes 278560 | tf_op jit(solution)/shard_map/ppermute | solution.py:239
  19.1 0.2 plane_parts.1
  19.3 3.3 %collective-permute-start.5 = (bf16[72,1024]{1,0:T(8,128)(2,1)S(1)}, bf16[72,1024]{1,0:T(8,128)(2,1)S(1)}, u32[]{:S(2)}, u32[]{:S(2)}) collective-permute-start(bf16[72,1024]{1,0:T(8,128)(2,1)S(1)} %get-tuple-element.50), channel_id=1, source_target_pairs={{0,17},{1,16},{2,19},{3,18},{4,21},{5,20},{6,23},{7,22},{8,25},{9,... | collective-permute-start | bytes 442376 | tf_op jit(solution)/shard_map/ppermute | solution.py:459
  22.6 0.5 %collective-permute-start.6 = (bf16[72,1024]{1,0:T(8,128)(2,1)S(1)}, bf16[72,1024]{1,0:T(8,128)(2,1)S(1)}, u32[]{:S(2)}, u32[]{:S(2)}) collective-permute-start(bf16[72,1024]{1,0:T(8,128)(2,1)S(1)} %get-tuple-element.51), channel_id=1, source_target_pairs={{0,16},{1,17},{2,18},{3,19},{4,20},{5,21},{6,22},{7,23},{8,24},{9,... | collective-permute-start | bytes 442376 | tf_op jit(solution)/shard_map/ppermute | solution.py:459
  23.1 0.1 collective-permute-start.7
  23.2 4.0 %collective-permute-done.5.refs_0_ = bf16[72,1024]{1,0:T(8,128)(2,1)S(1)} collective-permute-done((bf16[72,1024]{1,0:T(8,128)(2,1)S(1)}, bf16[72,1024]{1,0:T(8,128)(2,1)S(1)}, u32[]{:S(2)}, u32[]{:S(2)}) %collective-permute-start.5) | collective-permute-done | bytes 147488 | tf_op jit(solution)/shard_map/ppermute | solution.py:459
  27.2 2.7 %collective-permute-done.6.refs_1_ = bf16[72,1024]{1,0:T(8,128)(2,1)S(1)} collective-permute-done((bf16[72,1024]{1,0:T(8,128)(2,1)S(1)}, bf16[72,1024]{1,0:T(8,128)(2,1)S(1)}, u32[]{:S(2)}, u32[]{:S(2)}) %collective-permute-start.6) | collective-permute-done | bytes 147488 | tf_op jit(solution)/shard_map/ppermute | solution.py:459
  29.9 0.3 collective-permute-done.7.refs_2_
  30.2 0.1 line_parts.1
  30.3 1.6 %collective-permute-start.8 = (bf16[80,256]{1,0:T(8,128)(2,1)S(1)}, bf16[80,256]{1,0:T(8,128)(2,1)S(1)}, u32[]{:S(2)}, u32[]{:S(2)}) collective-permute-start(bf16[80,256]{1,0:T(8,128)(2,1)S(1)} %get-tuple-element.55), channel_id=1, source_target_pairs={{0,2},{1,3},{2,0},{3,1},{4,6},{5,7},{6,4},{7,5},{8,10},{9,11},{10,... | collective-permute-start | bytes 122888 | tf_op jit(solution)/shard_map/ppermute | solution.py:239
  31.9 2.6 %collective-permute-start.9 = (bf16[80,256]{1,0:T(8,128)(2,1)S(1)}, bf16[80,256]{1,0:T(8,128)(2,1)S(1)}, u32[]{:S(2)}, u32[]{:S(2)}) collective-permute-start(bf16[80,256]{1,0:T(8,128)(2,1)S(1)} %get-tuple-element.56), channel_id=1, source_target_pairs={{0,4},{1,5},{2,6},{3,7},{4,0},{5,1},{6,2},{7,3},{8,12},{9,13},{10,... | collective-permute-start | bytes 122888 | tf_op jit(solution)/shard_map/ppermute | solution.py:239
  34.5 0.2 collective-permute-start.10
  34.8 2.2 %row_grads.1 = (bf16[128,2048]{1,0:T(8,128)(2,1)}, bf16[128,2048]{1,0:T(8,128)(2,1)}) custom-call(bf16[8,128,256]{2,1,0:T(8,128)(2,1)S(1)} %get-tuple-element.36.refs_0_, bf16[8,128,256]{2,1,0:T(8,128)(2,1)S(1)} %get-tuple-element.37.refs_1_, bf16[8,128,256]{2,1,0:T(8,128)(2,1)S(1)} %get-tuple-element.38.refs_2_, ...), custom_call_target="tpu_custom_call" | custom-call | tf_op jit(solution)/shard_map/row_grads/pallas_call | solution.py:403
  36.9 0.0 collective-permute-done.8.refs_0_
  36.9 0.8 %collective-permute-done.9.refs_1_ = bf16[80,256]{1,0:T(8,128)(2,1)S(1)} collective-permute-done((bf16[80,256]{1,0:T(8,128)(2,1)S(1)}, bf16[80,256]{1,0:T(8,128)(2,1)S(1)}, u32[]{:S(2)}, u32[]{:S(2)}) %collective-permute-start.9) | collective-permute-done | bytes 40992 | tf_op jit(solution)/shard_map/ppermute | solution.py:239
  37.7 2.6 %collective-permute-done.10.refs_2_ = bf16[80,256]{1,0:T(8,128)(2,1)S(1)} collective-permute-done((bf16[80,256]{1,0:T(8,128)(2,1)S(1)}, bf16[80,256]{1,0:T(8,128)(2,1)S(1)}, u32[]{:S(2)}, u32[]{:S(2)}) %collective-permute-start.10) | collective-permute-done | bytes 40992 | tf_op jit(solution)/shard_map/ppermute | solution.py:239
  40.3 0.7 %last_sums.1 = (f32[64,256]{1,0:T(8,128)}, f32[16,128]{1,0:T(8,128)}, f32[16,128]{1,0:T(8,128)}) custom-call(f32[64,256]{1,0:T(8,128)S(1)} %get-tuple-element.53.total_ref, f32[16,256]{1,0:T(8,128)S(1)} %get-tuple-element.54.rows_ref, bf16[80,256]{1,0:T(8,128)(2,1)S(1)} %collective-permute-done.8.refs_0_, ...), custom_call_target="tpu_custom_call" | custom-call | tf_op jit(solution)/shard_map/last_sums/pallas_call | solution.py:403
Async XLA Ops:
  0.6 10.1 %collective-permute-start = (bf16[128,2048]{1,0:T(8,128)(2,1)}, bf16[128,2048]{1,0:T(8,128)(2,1)S(1)}, u32[]{:S(2)}, u32[]{:S(2)}) collective-permute-start(bf16[128,2048]{1,0:T(8,128)(2,1)} %bitcast.14), channel_id=1, source_target_pairs={{0,8},{8,16},{16,24},{24,0},{1,9},{9,17},{17,25},{25,1},{2,10},{10... | collective-permute-start | bytes 1572872 | tf_op jit(solution)/shard_map/ppermute | solution.py:235
  2.2 10.8 %collective-permute-start.2 = (bf16[128,1024]{1,0:T(8,128)(2,1)S(1)}, bf16[128,1024]{1,0:T(8,128)(2,1)S(1)}, u32[]{:S(2)}, u32[]{:S(2)}) collective-permute-start(bf16[128,1024]{1,0:T(8,128)(2,1)S(1)} %get-tuple-element.61), channel_id=1, source_target_pairs={{0,8},{8,16},{16,24},{24,0},{1,9},{9,17},{17,25},{25,1},{2,10},{10... | collective-permute-start | bytes 786440 | tf_op jit(solution)/shard_map/ppermute | solution.py:235
  4.9 10.9 %collective-permute-start.1 = (bf16[128,1024]{1,0:T(8,128)(2,1)S(1)}, bf16[128,1024]{1,0:T(8,128)(2,1)S(1)}, u32[]{:S(2)}, u32[]{:S(2)}) collective-permute-start(bf16[128,1024]{1,0:T(8,128)(2,1)S(1)} %get-tuple-element.62), channel_id=1, source_target_pairs={{0,8},{8,16},{16,24},{24,0},{1,9},{9,17},{17,25},{25,1},{2,10},{10... | collective-permute-start | bytes 786440 | tf_op jit(solution)/shard_map/ppermute | solution.py:235
  4.9 1.2 %copy-start = (bf16[256,2048]{1,0:T(8,128)(2,1)S(1)}, bf16[256,2048]{1,0:T(8,128)(2,1)}, u32[]{:S(2)}) copy-start(bf16[256,2048]{1,0:T(8,128)(2,1)} %refs_7_.1) | copy-start | bytes 3145732
  6.2 1.0 %copy-start.2 = (bf16[1,128,2048]{2,1,0:T(8,128)(2,1)S(1)}, bf16[1,128,2048]{2,1,0:T(8,128)(2,1)}, u32[]{:S(2)}) copy-start(bf16[1,128,2048]{2,1,0:T(8,128)(2,1)} %param.8) | copy-start | bytes 1572868
  7.2 1.0 %copy-start.6 = (bf16[1,128,2048]{2,1,0:T(8,128)(2,1)S(1)}, bf16[1,128,2048]{2,1,0:T(8,128)(2,1)}, u32[]{:S(2)}) copy-start(bf16[1,128,2048]{2,1,0:T(8,128)(2,1)} %param.7) | copy-start | bytes 1572868
  8.3 0.7 %copy-start.7 = (f32[2048]{0:T(1024)S(1)}, f32[2048]{0:T(1024)}, u32[]{:S(2)}) copy-start(f32[2048]{0:T(1024)} %param.11) | copy-start | bytes 24580
  9.0 0.7 %copy-start.8 = (f32[2048]{0:T(1024)S(1)}, f32[2048]{0:T(1024)}, u32[]{:S(2)}) copy-start(f32[2048]{0:T(1024)} %param.12) | copy-start | bytes 24580
  10.8 2.2 %copy-start.1 = (bf16[256,2048]{1,0:T(8,128)(2,1)S(1)}, bf16[256,2048]{1,0:T(8,128)(2,1)}, u32[]{:S(2)}) copy-start(bf16[256,2048]{1,0:T(8,128)(2,1)} %refs_7_.1) | copy-start | bytes 3145732
  10.8 2.2 %copy-start.3 = (bf16[1,128,2048]{2,1,0:T(8,128)(2,1)S(1)}, bf16[1,128,2048]{2,1,0:T(8,128)(2,1)}, u32[]{:S(2)}) copy-start(bf16[1,128,2048]{2,1,0:T(8,128)(2,1)} %param.8) | copy-start | bytes 1572868
  10.8 2.2 %copy-start.4 = (bf16[1,128,2048]{2,1,0:T(8,128)(2,1)S(1)}, bf16[1,128,2048]{2,1,0:T(8,128)(2,1)}, u32[]{:S(2)}) copy-start(bf16[1,128,2048]{2,1,0:T(8,128)(2,1)} %param.9) | copy-start | bytes 1572868
  10.8 2.2 %copy-start.5 = (bf16[1,128,2048]{2,1,0:T(8,128)(2,1)S(1)}, bf16[1,128,2048]{2,1,0:T(8,128)(2,1)}, u32[]{:S(2)}) copy-start(bf16[1,128,2048]{2,1,0:T(8,128)(2,1)} %param.13) | copy-start | bytes 1572868
  14.7 2.9 %collective-permute-start.4 = (bf16[136,1024]{1,0:T(8,128)(2,1)S(1)}, bf16[136,1024]{1,0:T(8,128)(2,1)S(1)}, u32[]{:S(2)}, u32[]{:S(2)}) collective-permute-start(bf16[136,1024]{1,0:T(8,128)(2,1)S(1)} %get-tuple-element.45), channel_id=1, source_target_pairs={{0,8},{8,0},{16,24},{24,16},{1,9},{9,1},{17,25},{25,17},{2,10},{10... | collective-permute-start | bytes 835592 | tf_op jit(solution)/shard_map/ppermute | solution.py:239
  17.5 1.6 %collective-permute-start.3 = (bf16[136,1024]{1,0:T(8,128)(2,1)S(1)}, bf16[136,1024]{1,0:T(8,128)(2,1)S(1)}, u32[]{:S(2)}, u32[]{:S(2)}) collective-permute-start(bf16[136,1024]{1,0:T(8,128)(2,1)S(1)} %get-tuple-element.44), channel_id=1, source_target_pairs={{0,8},{8,0},{16,24},{24,16},{1,9},{9,1},{17,25},{25,17},{2,10},{10... | collective-permute-start | bytes 835592 | tf_op jit(solution)/shard_map/ppermute | solution.py:239
  19.3 7.9 %collective-permute-start.5 = (bf16[72,1024]{1,0:T(8,128)(2,1)S(1)}, bf16[72,1024]{1,0:T(8,128)(2,1)S(1)}, u32[]{:S(2)}, u32[]{:S(2)}) collective-permute-start(bf16[72,1024]{1,0:T(8,128)(2,1)S(1)} %get-tuple-element.50), channel_id=1, source_target_pairs={{0,17},{1,16},{2,19},{3,18},{4,21},{5,20},{6,23},{7,22},{8,25},{9,... | collective-permute-start | bytes 442376 | tf_op jit(solution)/shard_map/ppermute | solution.py:459
  22.6 7.3 %collective-permute-start.6 = (bf16[72,1024]{1,0:T(8,128)(2,1)S(1)}, bf16[72,1024]{1,0:T(8,128)(2,1)S(1)}, u32[]{:S(2)}, u32[]{:S(2)}) collective-permute-start(bf16[72,1024]{1,0:T(8,128)(2,1)S(1)} %get-tuple-element.51), channel_id=1, source_target_pairs={{0,16},{1,17},{2,18},{3,19},{4,20},{5,21},{6,22},{7,23},{8,24},{9,... | collective-permute-start | bytes 442376 | tf_op jit(solution)/shard_map/ppermute | solution.py:459
  23.1 7.1 %collective-permute-start.7 = (bf16[72,1024]{1,0:T(8,128)(2,1)S(1)}, bf16[72,1024]{1,0:T(8,128)(2,1)S(1)}, u32[]{:S(2)}, u32[]{:S(2)}) collective-permute-start(bf16[72,1024]{1,0:T(8,128)(2,1)S(1)} %get-tuple-element.52), channel_id=1, source_target_pairs={{0,1},{1,0},{2,3},{3,2},{4,5},{5,4},{6,7},{7,6},{8,9},{9,8},{10,11... | collective-permute-start | bytes 442376 | tf_op jit(solution)/shard_map/ppermute | solution.py:459
  30.3 6.6 %collective-permute-start.8 = (bf16[80,256]{1,0:T(8,128)(2,1)S(1)}, bf16[80,256]{1,0:T(8,128)(2,1)S(1)}, u32[]{:S(2)}, u32[]{:S(2)}) collective-permute-start(bf16[80,256]{1,0:T(8,128)(2,1)S(1)} %get-tuple-element.55), channel_id=1, source_target_pairs={{0,2},{1,3},{2,0},{3,1},{4,6},{5,7},{6,4},{7,5},{8,10},{9,11},{10,... | collective-permute-start | bytes 122888 | tf_op jit(solution)/shard_map/ppermute | solution.py:239
  31.9 5.7 %collective-permute-start.9 = (bf16[80,256]{1,0:T(8,128)(2,1)S(1)}, bf16[80,256]{1,0:T(8,128)(2,1)S(1)}, u32[]{:S(2)}, u32[]{:S(2)}) collective-permute-start(bf16[80,256]{1,0:T(8,128)(2,1)S(1)} %get-tuple-element.56), channel_id=1, source_target_pairs={{0,4},{1,5},{2,6},{3,7},{4,0},{5,1},{6,2},{7,3},{8,12},{9,13},{10,... | collective-permute-start | bytes 122888 | tf_op jit(solution)/shard_map/ppermute | solution.py:239
  34.5 5.8 %collective-permute-start.10 = (bf16[80,256]{1,0:T(8,128)(2,1)S(1)}, bf16[80,256]{1,0:T(8,128)(2,1)S(1)}, u32[]{:S(2)}, u32[]{:S(2)}) collective-permute-start(bf16[80,256]{1,0:T(8,128)(2,1)S(1)} %get-tuple-element.57), channel_id=1, source_target_pairs={{0,6},{1,7},{2,4},{3,5},{4,2},{5,3},{6,0},{7,1},{8,14},{9,15},{10,... | collective-permute-start | bytes 122888 | tf_op jit(solution)/shard_map/ppermute | solution.py:239

commit v5 on v4

--- a/solution.py
+++ b/solution.py
@@ -10,7 +10,7 @@
 DH = 128
 LOG2_E = 1.4426950408889634
 GROUP = 4
-CHUNKS = (1024, 1024)
+CHUNKS = (768, 768, 512)
 VMEM_BYTES = 24 * 1024 * 1024
 SCORE_SCALE = DH ** (-0.5)
 BIAS_ROWS = 8
@@ -26,16 +26,61 @@
     )
 
 
-def local_kernel(q_ref, k_ref, rel_ref, bias_u_ref, bias_v_ref, score_ref, content_ref, flipped_ref):
-    seg_rows = q_ref.shape[0]
+def local_kernel(
+    q_hbm,
+    k_hbm,
+    rel_hbm,
+    v_hbm,
+    d_out_hbm,
+    bias_u_hbm,
+    bias_v_hbm,
+    score_ref,
+    content_ref,
+    flipped_ref,
+    k_ref,
+    rel_ref,
+    v_ref,
+    d_out_ref,
+    q_ref,
+    bias_u_ref,
+    bias_v_ref,
+    head_sems,
+    bias_sems,
+    rest_sems,
+):
+    seg_rows, width = q_ref.shape
     key_count = rel_ref.shape[0]
     mem_len = key_count - seg_rows
+    groups = head_groups(0, width)
+    pairs = (q_hbm, q_ref), (rel_hbm, rel_ref), (k_hbm, k_ref)
+    biases = [
+        pltpu.make_async_copy(bias_u_hbm, bias_u_ref, bias_sems.at[0]),
+        pltpu.make_async_copy(bias_v_hbm, bias_v_ref, bias_sems.at[1]),
+    ]
+    copies = []
+    for n, group in enumerate(groups):
+        span = pl.ds(group[0] * DH, len(group) * DH)
+        copies.append(
+            [
+                pltpu.make_async_copy(src.at[:, span], dst.at[:, span], head_sems.at[n, at])
+                for at, (src, dst) in enumerate(pairs)
+            ]
+        )
+    rest = [
+        pltpu.make_async_copy(v_hbm, v_ref, rest_sems.at[0]),
+        pltpu.make_async_copy(d_out_hbm, d_out_ref, rest_sems.at[1]),
+    ]
+    copies[0] = biases + copies[0]
+    for copy in [each for part in copies for each in part] + rest:
+        copy.start()
     first_key = jnp.where(lax.axis_index("seg") > 0, 0, mem_len)
     row_index = lax.broadcasted_iota(jnp.int32, (seg_rows, key_count), 0)
     key_index = lax.broadcasted_iota(jnp.int32, (seg_rows, key_count), 1)
     allowed = (key_index <= row_index + mem_len) & (key_index >= first_key)
     flip = row_flip(seg_rows)
-    for group in head_groups(0, q_ref.shape[1]):
+    for group, part in zip(groups, copies):
+        for copy in part:
+            copy.wait()
         cols = columns_of(group)
         n = range(len(cols))
         wide = [q_ref[:, c].astype(jnp.float32) for c in cols]
@@ -45,7 +90,8 @@
         content = [contract(q_content[t], k_ref[:, cols[t]], 1, 1) for t in n]
         flipped = [contract(flip, q_position[t], 1, 0).astype(jnp.bfloat16) for t in n]
         position = [
-            pltpu.roll(raw, key_count - seg_rows + 1, 1, stride=1, stride_axis=0) for raw in by_distance
+            pltpu.roll(raw, key_count - seg_rows + 1, 1, stride=1, stride_axis=0)
+            for raw in by_distance
         ]
         for t in n:
             scores = jnp.concatenate(
@@ -54,6 +100,8 @@
             score_ref[group[t]] = jnp.where(allowed, SCORE_SCALE * LOG2_E * scores, -1e30)
             content_ref[:, cols[t]] = q_content[t]
             flipped_ref[:, cols[t]] = flipped[t]
+    for copy in rest:
+        copy.wait()
 
 
 def weights_kernel(score_ref, content_ref, k_mem_ref, weights_ref):
@@ -172,19 +220,38 @@
 
 def head_groups(start, span):
     heads = range(start // DH, (start + span) // DH)
-    return [heads[at : at + GROUP] for at in range(0, len(heads), GROUP)]
+    size = GROUP if len(heads) % GROUP == 0 else len(heads)
+    return [heads[at : at + size] for at in range(0, len(heads), size)]
 
 
 def columns_of(heads, start=0):
     return [slice(head * DH - start, (head + 1) * DH - start) for head in heads]
 
 
-def local_scores(queries, keys, rel_keys, bias_u, bias_v):
+def local_scores(queries, keys, rel_keys, values, d_out, bias_u, bias_v):
     seg_rows, width = queries.shape
-    rows = ((seg_rows, width), jnp.bfloat16)
-    scores = ((width // DH, seg_rows, rel_keys.shape[0]), jnp.float32)
-    operands = queries, keys, rel_keys, bias_u[None], bias_v[None]
-    return whole_call(local_kernel, "local_scores", [scores, rows, rows], *operands)
+    rows = jax.ShapeDtypeStruct((seg_rows, width), jnp.bfloat16)
+    groups = len(head_groups(0, width))
+    scores = jax.ShapeDtypeStruct((width // DH, seg_rows, rel_keys.shape[0]), jnp.float32)
+    rel = jax.ShapeDtypeStruct(rel_keys.shape, jnp.bfloat16)
+    stays = pl.BlockSpec(memory_space=pl.ANY)
+    whole = pl.BlockSpec(memory_space=pltpu.VMEM)
+    return pl.pallas_call(
+        local_kernel,
+        name="local_scores",
+        in_specs=[stays] * 7,
+        out_specs=[whole] * 7,
+        out_shape=[scores, rows, rows, rows, rel, rows, rows],
+        scratch_shapes=[
+            pltpu.VMEM((seg_rows, width), jnp.bfloat16),
+            pltpu.VMEM((1, width), jnp.float32),
+            pltpu.VMEM((1, width), jnp.float32),
+            pltpu.SemaphoreType.DMA((groups, 3)),
+            pltpu.SemaphoreType.DMA((2,)),
+            pltpu.SemaphoreType.DMA((2,)),
+        ],
+        compiler_params=pltpu.CompilerParams(vmem_limit_bytes=VMEM_BYTES),
+    )(*map(in_hbm, (queries, keys, rel_keys, values, d_out, bias_u[None], bias_v[None])))
 
 
 def soft_weights(scores, q_content, key_memory):
@@ -226,8 +293,8 @@
     return whole_call(kernel, "row_grads", [rows, rows], *operands)
 
 
-def in_vmem(block):
-    return pltpu.with_memory_space_constraint(block, pltpu.VMEM)
+def in_hbm(block):
+    return pltpu.with_memory_space_constraint(block, pltpu.HBM)
 
 
 def from_behind(block, axis):
@@ -441,7 +508,7 @@
         plane_sums,
         *got,
     )
-    got = [swap(send, "dp", 2 * distance) for distance, send in enumerate(sends, 1)]
+    got = [swap(sends[distance - 1], "dp", 2 * distance) for distance in (2, 3, 1)]
     side = ((tail, cols // 2), jnp.float32)
     total, *sums = whole_call(
         last_kernel, "last_sums", [((part_rows, cols), jnp.float32), side, side], total, rows, *got
@@ -468,10 +535,9 @@
         from_behind(values[0, seg_rows - mem_len :, start : start + span], "seg")
         for start, span in edges
     ]
-    own_q, own_k, own_v, rel_keys, own_d = (
-        in_vmem(block) for block in (queries[0], keys[0], values[0], rel_keys, d_out[0])
-    )
-    scores, q_content, q_flipped = local_scores(own_q, own_k, rel_keys, bias_u, bias_v)
+    scores, q_content, q_flipped, own_k, rel_keys, own_v, own_d = local_scores(
+        queries[0], keys[0], rel_keys, values[0], d_out[0], bias_u, bias_v
+    )
     weights = soft_weights(scores, q_content, key_memory)
     shared = weights, q_flipped, own_k, own_v, key_memory, rel_keys, own_d
     parts = [

time: 41.3 us -> 38.7 us (0.937)
  local copies, waits for them, and re-layouts: 5.79 us -> 1.96 us
  Pallas kernels: 8.52 us -> 10.3 us
  waiting for transfers between devices: 14.1 us -> 13.6 us
    unnamed x18 -> x0, local copies, waits for them, and re-layouts: 4.72 us -> none
    pallas_call x0 -> x1, Pallas kernels: none -> 3.3 us  [local_scores(): pl.pallas_call(local_kernel, name='local_scores', in_specs=[stays] * 7, o...]
    ppermute x5 -> x6, waiting for transfers between devices: 4.94 us -> 3.22 us  [swap(): lax.ppermute(block, axis, [(i, i ^ flip) for i in range(lax.axis_size(axi...]
    pallas_call x8, Pallas kernels: 8.52 us -> 7.02 us  [whole_call(): pl.pallas_call(kernel, name=name, out_shape=[jax.ShapeDtypeStruct(*shape)...]
    ppermute x3 -> x4, waiting for transfers between devices: 2.24 us -> 3.33 us  [from_behind(): lax.ppermute(block, axis, [(i, (i + 1) % count) for i in range(count)])]
    squeeze x1 -> x2, local copies, waits for them, and re-layouts: 1.06 us -> 1.96 us  [shards(): values[0, seg_rows - mem_len:, start:start + span]]
    ppermute x5 -> x6, starting transfers between devices: 4.59 us -> 4.69 us  [swap(): lax.ppermute(block, axis, [(i, i ^ flip) for i in range(lax.axis_size(axi...]
    ppermute x3 -> x4, starting transfers between devices: 3.25 us -> 3.32 us  [from_behind(): lax.ppermute(block, axis, [(i, (i + 1) % count) for i in range(count)])]
  transfers between devices with their start and end apart: 11 -> 13, of which waited for: 8 -> 9; matrix products, arithmetic and copies ran while one was open for 3% -> 5% of each run, Pallas kernels for 18% -> 24%
where the time goes in v5:
time: 38.7 us; the launch traced here: 38.6 us
  waiting for transfers between devices  13.6 us (35%)
  starting transfers between devices  11.9 us (31%)
  Pallas kernels  10.3 us (27%)
  local copies, waits for them, and re-layouts  1.96 us (5%)
  between operations  0.71 us (2%)
    ppermute x3, waiting for transfers between devices, swap_both(): return lax.ppermute(block, ('seg', 'dp'), route)  7.07 us
    pallas_call x8, Pallas kernels, whole_call(): pl.pallas_call(kernel, name=name, out_shape=[jax.ShapeDtypeStruct(*shape)...  7.02 us
    ppermute x6, starting transfers between devices, swap(): lax.ppermute(block, axis, [(i, i ^ flip) for i in range(lax.axis_size(axi...  4.69 us
    ppermute x3, starting transfers between devices, swap_both(): return lax.ppermute(block, ('seg', 'dp'), route)  3.93 us
    ppermute x4, waiting for transfers between devices, from_behind(): lax.ppermute(block, axis, [(i, (i + 1) % count) for i in range(count)])  3.33 us
    ppermute x4, starting transfers between devices, from_behind(): lax.ppermute(block, axis, [(i, (i + 1) % count) for i in range(count)])  3.32 us
    pallas_call x1, Pallas kernels, local_scores(): pl.pallas_call(local_kernel, name='local_scores', in_specs=[stays] * 7, o...  3.3 us
    ppermute x6, waiting for transfers between devices, swap(): lax.ppermute(block, axis, [(i, i ^ flip) for i in range(lax.axis_size(axi...  3.22 us
  transfers between devices with their start and end apart: 13, of which 9 were waited for; matrix products, arithmetic and copies ran while one was open for 5% of the time, Pallas kernels for 24%

profile of v5, /device:TPU:0, one launch (start us, length us, event | category | flops | bytes accessed | tf_op | source)
XLA Modules:
  0.0 38.6 jit_solution(381980464294919453)
XLA Ops:
  0.6 0.5 %collective-permute-start = (bf16[128,2048]{1,0:T(8,128)(2,1)}, bf16[128,2048]{1,0:T(8,128)(2,1)S(1)}, u32[]{:S(2)}, u32[]{:S(2)}) collective-permute-start(bf16[128,2048]{1,0:T(8,128)(2,1)} %bitcast.19), channel_id=1, source_target_pairs={{0,8},{8,16},{16,24},{24,0},{1,9},{9,17},{17,25},{25,1},{2,10},{10... | collective-permute-start | bytes 1572872 | tf_op jit(solution)/shard_map/ppermute | solution.py:302
  1.1 1.0 %slice_bitcast_fusion = (bf16[128,768]{1,0:T(8,128)(2,1)S(1)}, bf16[128,768]{1,0:T(8,128)(2,1)S(1)}) fusion(bf16[1,128,2048]{2,1,0:T(8,128)(2,1)} %param.9), kind=kLoop, calls=%fused_computation | loop fusion | bytes 786432 | tf_op jit(solution)/shard_map/squeeze | solution.py:535
  2.2 2.7 %collective-permute-start.2 = (bf16[128,768]{1,0:T(8,128)(2,1)S(1)}, bf16[128,768]{1,0:T(8,128)(2,1)S(1)}, u32[]{:S(2)}, u32[]{:S(2)}) collective-permute-start(bf16[128,768]{1,0:T(8,128)(2,1)S(1)} %get-tuple-element.79), channel_id=1, source_target_pairs={{0,8},{8,16},{16,24},{24,0},{1,9},{9,17},{17,25},{25,1},{2,10},{10... | collective-permute-start | bytes 589832 | tf_op jit(solution)/shard_map/ppermute | solution.py:302
  4.9 0.1 collective-permute-start.1
  4.9 0.9 %slice_bitcast_fusion.2 = bf16[128,512]{1,0:T(8,128)(2,1)S(1)} fusion(bf16[1,128,2048]{2,1,0:T(8,128)(2,1)} %param.9), kind=kLoop, calls=%fused_computation.2 | loop fusion | bytes 262144 | tf_op jit(solution)/shard_map/squeeze | solution.py:535
  5.8 0.1 collective-permute-start.3
  5.9 3.3 %local_scores.1 = (f32[16,128,256]{2,1,0:T(8,128)S(1)}, bf16[128,2048]{1,0:T(8,128)(2,1)S(1)}, bf16[128,2048]{1,0:T(8,128)(2,1)S(1)}, bf16[128,2048]{1,0:T(8,128...) custom-call(bf16[128,2048]{1,0:T(8,128)(2,1)} %bitcast.17, ...), custom_call_target="tpu_custom_call" | custom-call | tf_op jit(solution)/shard_map/local_scores/pallas_call | solution.py:239
  9.2 0.9 %collective-permute-done.k_mem_ref.refs_8_ = bf16[128,2048]{1,0:T(8,128)(2,1)S(1)} collective-permute-done((bf16[128,2048]{1,0:T(8,128)(2,1)}, bf16[128,2048]{1,0:T(8,128)(2,1)S(1)}, u32[]{:S(2)}, u32[]{:S(2)}) %collective-permute-start) | collective-permute-done | bytes 524320 | tf_op jit(solution)/shard_map/ppermute | solution.py:302
  10.2 0.9 %soft_weights.1.weights_ref = f32[16,128,256]{2,1,0:T(8,128)S(1)} custom-call(f32[16,128,256]{2,1,0:T(8,128)S(1)} %get-tuple-element.42.score_ref, bf16[128,2048]{1,0:T(8,128)(2,1)S(1)} %get-tuple-element.43.content_ref.refs_6_, bf16[128,2048]{1,0:T(8,128)(2,1)S(1)} %collective-permute-done.k_mem_ref.refs_8_), custom_call_target="tpu_custom_call" | custom-call | tf_op jit(solution)/shard_map/soft_weights/pallas_call | solution.py:470
  11.1 1.2 %collective-permute-done.2.v_mem_ref = bf16[128,768]{1,0:T(8,128)(2,1)S(1)} collective-permute-done((bf16[128,768]{1,0:T(8,128)(2,1)S(1)}, bf16[128,768]{1,0:T(8,128)(2,1)S(1)}, u32[]{:S(2)}, u32[]{:S(2)}) %collective-permute-start.2) | collective-permute-done | bytes 196640 | tf_op jit(solution)/shard_map/ppermute | solution.py:302
  12.3 1.1 %score_grads.4 = (bf16[6,128,256]{2,1,0:T(8,128)(2,1)S(1)}, bf16[6,128,256]{2,1,0:T(8,128)(2,1)S(1)}, f32[2,64,768]{2,1,0:T(8,128)S(1)}, bf16[136,768]{1,0:T(8,128)(2,1)S(1)}, f32[2,768]{1,0:T(2,128)S(1)}) custom-call(f32[16,128,256]{2,1,0:T(8,128)S(1)} %soft_weights.1.weights_ref, bf16[128,2048]{1,0:T(8,128)(2,1)S(1)} %get-tuple-element.44.flipped_ref, ...), custom_call_target="tpu_custom_call" | custom-call | tf_op jit(solution)/shard_map/score_grads/pallas_call | solution.py:470
  13.3 0.1 collective-permute-start.5
  13.4 1.0 %collective-permute-done.1.v_mem_ref = bf16[128,768]{1,0:T(8,128)(2,1)S(1)} collective-permute-done((bf16[128,768]{1,0:T(8,128)(2,1)S(1)}, bf16[128,768]{1,0:T(8,128)(2,1)S(1)}, u32[]{:S(2)}, u32[]{:S(2)}) %collective-permute-start.1) | collective-permute-done | bytes 196640 | tf_op jit(solution)/shard_map/ppermute | solution.py:302
  14.4 1.1 %score_grads.3 = (bf16[6,128,256]{2,1,0:T(8,128)(2,1)S(1)}, bf16[6,128,256]{2,1,0:T(8,128)(2,1)S(1)}, f32[2,64,768]{2,1,0:T(8,128)S(1)}, bf16[136,768]{1,0:T(8,128)(2,1)S(1)}, f32[2,768]{1,0:T(2,128)S(1)}) custom-call(f32[16,128,256]{2,1,0:T(8,128)S(1)} %soft_weights.1.weights_ref, bf16[128,2048]{1,0:T(8,128)(2,1)S(1)} %get-tuple-element.44.flipped_ref, ...), custom_call_target="tpu_custom_call" | custom-call | tf_op jit(solution)/shard_map/score_grads/pallas_call | solution.py:470
  15.5 0.1 collective-permute-start.4
  15.5 0.3 collective-permute-done.3.v_mem_ref
  15.8 0.9 %score_grads.5 = (bf16[4,128,256]{2,1,0:T(8,128)(2,1)S(1)}, bf16[4,128,256]{2,1,0:T(8,128)(2,1)S(1)}, f32[2,64,512]{2,1,0:T(8,128)S(1)}, bf16[136,512]{1,0:T(8,128)(2,1)S(1)}, f32[2,512]{1,0:T(2,128)S(1)}) custom-call(f32[16,128,256]{2,1,0:T(8,128)S(1)} %soft_weights.1.weights_ref, bf16[128,2048]{1,0:T(8,128)(2,1)S(1)} %get-tuple-element.44.flipped_ref, ...), custom_call_target="tpu_custom_call" | custom-call | tf_op jit(solution)/shard_map/score_grads/pallas_call | solution.py:470
  16.7 0.3 collective-permute-start.6
  17.0 1.1 %collective-permute-done.6.refs_5_ = bf16[136,512]{1,0:T(8,128)(2,1)S(1)} collective-permute-done((bf16[136,512]{1,0:T(8,128)(2,1)S(1)}, bf16[136,512]{1,0:T(8,128)(2,1)S(1)}, u32[]{:S(2)}, u32[]{:S(2)}) %collective-permute-start.6) | collective-permute-done | bytes 139296 | tf_op jit(solution)/shard_map/ppermute | solution.py:306
  18.1 0.0 collective-permute-done.5.refs_4_
  18.1 0.0 collective-permute-done.4.refs_3_
  18.1 0.2 plane_parts.1
  18.3 3.3 %collective-permute-start.7 = (bf16[72,1024]{1,0:T(8,128)(2,1)S(1)}, bf16[72,1024]{1,0:T(8,128)(2,1)S(1)}, u32[]{:S(2)}, u32[]{:S(2)}) collective-permute-start(bf16[72,1024]{1,0:T(8,128)(2,1)S(1)} %get-tuple-element.68), channel_id=1, source_target_pairs={{0,17},{1,16},{2,19},{3,18},{4,21},{5,20},{6,23},{7,22},{8,25},{9,... | collective-permute-start | bytes 442376 | tf_op jit(solution)/shard_map/ppermute | solution.py:526
  21.6 0.5 %collective-permute-start.8 = (bf16[72,1024]{1,0:T(8,128)(2,1)S(1)}, bf16[72,1024]{1,0:T(8,128)(2,1)S(1)}, u32[]{:S(2)}, u32[]{:S(2)}) collective-permute-start(bf16[72,1024]{1,0:T(8,128)(2,1)S(1)} %get-tuple-element.69), channel_id=1, source_target_pairs={{0,16},{1,17},{2,18},{3,19},{4,20},{5,21},{6,22},{7,23},{8,24},{9,... | collective-permute-start | bytes 442376 | tf_op jit(solution)/shard_map/ppermute | solution.py:526
  22.1 0.1 collective-permute-start.9
  22.3 4.0 %collective-permute-done.7.refs_0_ = bf16[72,1024]{1,0:T(8,128)(2,1)S(1)} collective-permute-done((bf16[72,1024]{1,0:T(8,128)(2,1)S(1)}, bf16[72,1024]{1,0:T(8,128)(2,1)S(1)}, u32[]{:S(2)}, u32[]{:S(2)}) %collective-permute-start.7) | collective-permute-done | bytes 147488 | tf_op jit(solution)/shard_map/ppermute | solution.py:526
  26.2 2.8 %collective-permute-done.8.refs_1_ = bf16[72,1024]{1,0:T(8,128)(2,1)S(1)} collective-permute-done((bf16[72,1024]{1,0:T(8,128)(2,1)S(1)}, bf16[72,1024]{1,0:T(8,128)(2,1)S(1)}, u32[]{:S(2)}, u32[]{:S(2)}) %collective-permute-start.8) | collective-permute-done | bytes 147488 | tf_op jit(solution)/shard_map/ppermute | solution.py:526
  29.1 0.3 collective-permute-done.9.refs_2_
  29.3 0.1 line_parts.1
  29.5 2.7 %collective-permute-start.10 = (bf16[80,256]{1,0:T(8,128)(2,1)S(1)}, bf16[80,256]{1,0:T(8,128)(2,1)S(1)}, u32[]{:S(2)}, u32[]{:S(2)}) collective-permute-start(bf16[80,256]{1,0:T(8,128)(2,1)S(1)} %get-tuple-element.73), channel_id=1, source_target_pairs={{0,4},{1,5},{2,6},{3,7},{4,0},{5,1},{6,2},{7,3},{8,12},{9,13},{10,... | collective-permute-start | bytes 122888 | tf_op jit(solution)/shard_map/ppermute | solution.py:306
  32.1 1.3 %collective-permute-start.11 = (bf16[80,256]{1,0:T(8,128)(2,1)S(1)}, bf16[80,256]{1,0:T(8,128)(2,1)S(1)}, u32[]{:S(2)}, u32[]{:S(2)}) collective-permute-start(bf16[80,256]{1,0:T(8,128)(2,1)S(1)} %get-tuple-element.74), channel_id=1, source_target_pairs={{0,6},{1,7},{2,4},{3,5},{4,2},{5,3},{6,0},{7,1},{8,14},{9,15},{10,... | collective-permute-start | bytes 122888 | tf_op jit(solution)/shard_map/ppermute | solution.py:306
  33.5 0.2 collective-permute-start.12
  33.7 2.1 %row_grads.1 = (bf16[128,2048]{1,0:T(8,128)(2,1)}, bf16[128,2048]{1,0:T(8,128)(2,1)}) custom-call(bf16[6,128,256]{2,1,0:T(8,128)(2,1)S(1)} %get-tuple-element.49.refs_0_, bf16[6,128,256]{2,1,0:T(8,128)(2,1)S(1)} %get-tuple-element.50.refs_1_, bf16[4,128,256]{2,1,0:T(8,128)(2,1)S(1)} %get-tuple-element.51.refs_2_, ...), custom_call_target="tpu_custom_call" | custom-call | tf_op jit(solution)/shard_map/row_grads/pallas_call | solution.py:470
  35.8 0.0 collective-permute-done.10.refs_0_
  35.8 2.1 %collective-permute-done.11.refs_1_ = bf16[80,256]{1,0:T(8,128)(2,1)S(1)} collective-permute-done((bf16[80,256]{1,0:T(8,128)(2,1)S(1)}, bf16[80,256]{1,0:T(8,128)(2,1)S(1)}, u32[]{:S(2)}, u32[]{:S(2)}) %collective-permute-start.11) | collective-permute-done | bytes 40992 | tf_op jit(solution)/shard_map/ppermute | solution.py:306
  37.9 0.0 collective-permute-done.12.refs_2_
  37.9 0.7 %last_sums.1 = (f32[64,256]{1,0:T(8,128)}, f32[16,128]{1,0:T(8,128)}, f32[16,128]{1,0:T(8,128)}) custom-call(f32[64,256]{1,0:T(8,128)S(1)} %get-tuple-element.71.total_ref, f32[16,256]{1,0:T(8,128)S(1)} %get-tuple-element.72.rows_ref, bf16[80,256]{1,0:T(8,128)(2,1)S(1)} %collective-permute-done.10.refs_0_, ...), custom_call_target="tpu_custom_call" | custom-call | tf_op jit(solution)/shard_map/last_sums/pallas_call | solution.py:470
Async XLA Ops:
  0.6 9.5 %collective-permute-start = (bf16[128,2048]{1,0:T(8,128)(2,1)}, bf16[128,2048]{1,0:T(8,128)(2,1)S(1)}, u32[]{:S(2)}, u32[]{:S(2)}) collective-permute-start(bf16[128,2048]{1,0:T(8,128)(2,1)} %bitcast.19), channel_id=1, source_target_pairs={{0,8},{8,16},{16,24},{24,0},{1,9},{9,17},{17,25},{25,1},{2,10},{10... | collective-permute-start | bytes 1572872 | tf_op jit(solution)/shard_map/ppermute | solution.py:302
  2.2 10.1 %collective-permute-start.2 = (bf16[128,768]{1,0:T(8,128)(2,1)S(1)}, bf16[128,768]{1,0:T(8,128)(2,1)S(1)}, u32[]{:S(2)}, u32[]{:S(2)}) collective-permute-start(bf16[128,768]{1,0:T(8,128)(2,1)S(1)} %get-tuple-element.79), channel_id=1, source_target_pairs={{0,8},{8,16},{16,24},{24,0},{1,9},{9,17},{17,25},{25,1},{2,10},{10... | collective-permute-start | bytes 589832 | tf_op jit(solution)/shard_map/ppermute | solution.py:302
  4.9 9.5 %collective-permute-start.1 = (bf16[128,768]{1,0:T(8,128)(2,1)S(1)}, bf16[128,768]{1,0:T(8,128)(2,1)S(1)}, u32[]{:S(2)}, u32[]{:S(2)}) collective-permute-start(bf16[128,768]{1,0:T(8,128)(2,1)S(1)} %get-tuple-element.80), channel_id=1, source_target_pairs={{0,8},{8,16},{16,24},{24,0},{1,9},{9,17},{17,25},{25,1},{2,10},{10... | collective-permute-start | bytes 589832 | tf_op jit(solution)/shard_map/ppermute | solution.py:302
  5.8 9.9 %collective-permute-start.3 = (bf16[128,512]{1,0:T(8,128)(2,1)S(1)}, bf16[128,512]{1,0:T(8,128)(2,1)S(1)}, u32[]{:S(2)}, u32[]{:S(2)}) collective-permute-start(bf16[128,512]{1,0:T(8,128)(2,1)S(1)} %slice_bitcast_fusion.2), channel_id=1, source_target_pairs={{0,8},{8,16},{16,24},{24,0},{1,9},{9,17},{17,25},{25,1},{2,10},{10... | collective-permute-start | bytes 393224 | tf_op jit(solution)/shard_map/ppermute | solution.py:302
  13.3 4.8 %collective-permute-start.5 = (bf16[136,768]{1,0:T(8,128)(2,1)S(1)}, bf16[136,768]{1,0:T(8,128)(2,1)S(1)}, u32[]{:S(2)}, u32[]{:S(2)}) collective-permute-start(bf16[136,768]{1,0:T(8,128)(2,1)S(1)} %get-tuple-element.61), channel_id=1, source_target_pairs={{0,8},{8,0},{16,24},{24,16},{1,9},{9,1},{17,25},{25,17},{2,10},{10... | collective-permute-start | bytes 626696 | tf_op jit(solution)/shard_map/ppermute | solution.py:306
  15.5 2.7 %collective-permute-start.4 = (bf16[136,768]{1,0:T(8,128)(2,1)S(1)}, bf16[136,768]{1,0:T(8,128)(2,1)S(1)}, u32[]{:S(2)}, u32[]{:S(2)}) collective-permute-start(bf16[136,768]{1,0:T(8,128)(2,1)S(1)} %get-tuple-element.60), channel_id=1, source_target_pairs={{0,8},{8,0},{16,24},{24,16},{1,9},{9,1},{17,25},{25,17},{2,10},{10... | collective-permute-start | bytes 626696 | tf_op jit(solution)/shard_map/ppermute | solution.py:306
  16.7 1.4 %collective-permute-start.6 = (bf16[136,512]{1,0:T(8,128)(2,1)S(1)}, bf16[136,512]{1,0:T(8,128)(2,1)S(1)}, u32[]{:S(2)}, u32[]{:S(2)}) collective-permute-start(bf16[136,512]{1,0:T(8,128)(2,1)S(1)} %get-tuple-element.62), channel_id=1, source_target_pairs={{0,8},{8,0},{16,24},{24,16},{1,9},{9,1},{17,25},{25,17},{2,10},{10... | collective-permute-start | bytes 417800 | tf_op jit(solution)/shard_map/ppermute | solution.py:306
  18.3 7.9 %collective-permute-start.7 = (bf16[72,1024]{1,0:T(8,128)(2,1)S(1)}, bf16[72,1024]{1,0:T(8,128)(2,1)S(1)}, u32[]{:S(2)}, u32[]{:S(2)}) collective-permute-start(bf16[72,1024]{1,0:T(8,128)(2,1)S(1)} %get-tuple-element.68), channel_id=1, source_target_pairs={{0,17},{1,16},{2,19},{3,18},{4,21},{5,20},{6,23},{7,22},{8,25},{9,... | collective-permute-start | bytes 442376 | tf_op jit(solution)/shard_map/ppermute | solution.py:526
  21.6 7.4 %collective-permute-start.8 = (bf16[72,1024]{1,0:T(8,128)(2,1)S(1)}, bf16[72,1024]{1,0:T(8,128)(2,1)S(1)}, u32[]{:S(2)}, u32[]{:S(2)}) collective-permute-start(bf16[72,1024]{1,0:T(8,128)(2,1)S(1)} %get-tuple-element.69), channel_id=1, source_target_pairs={{0,16},{1,17},{2,18},{3,19},{4,20},{5,21},{6,22},{7,23},{8,24},{9,... | collective-permute-start | bytes 442376 | tf_op jit(solution)/shard_map/ppermute | solution.py:526
  22.1 7.2 %collective-permute-start.9 = (bf16[72,1024]{1,0:T(8,128)(2,1)S(1)}, bf16[72,1024]{1,0:T(8,128)(2,1)S(1)}, u32[]{:S(2)}, u32[]{:S(2)}) collective-permute-start(bf16[72,1024]{1,0:T(8,128)(2,1)S(1)} %get-tuple-element.70), channel_id=1, source_target_pairs={{0,1},{1,0},{2,3},{3,2},{4,5},{5,4},{6,7},{7,6},{8,9},{9,8},{10,11... | collective-permute-start | bytes 442376 | tf_op jit(solution)/shard_map/ppermute | solution.py:526
  29.5 6.4 %collective-permute-start.10 = (bf16[80,256]{1,0:T(8,128)(2,1)S(1)}, bf16[80,256]{1,0:T(8,128)(2,1)S(1)}, u32[]{:S(2)}, u32[]{:S(2)}) collective-permute-start(bf16[80,256]{1,0:T(8,128)(2,1)S(1)} %get-tuple-element.73), channel_id=1, source_target_pairs={{0,4},{1,5},{2,6},{3,7},{4,0},{5,1},{6,2},{7,3},{8,12},{9,13},{10,... | collective-permute-start | bytes 122888 | tf_op jit(solution)/shard_map/ppermute | solution.py:306
  32.1 5.8 %collective-permute-start.11 = (bf16[80,256]{1,0:T(8,128)(2,1)S(1)}, bf16[80,256]{1,0:T(8,128)(2,1)S(1)}, u32[]{:S(2)}, u32[]{:S(2)}) collective-permute-start(bf16[80,256]{1,0:T(8,128)(2,1)S(1)} %get-tuple-element.74), channel_id=1, source_target_pairs={{0,6},{1,7},{2,4},{3,5},{4,2},{5,3},{6,0},{7,1},{8,14},{9,15},{10,... | collective-permute-start | bytes 122888 | tf_op jit(solution)/shard_map/ppermute | solution.py:306
  33.5 4.5 %collective-permute-start.12 = (bf16[80,256]{1,0:T(8,128)(2,1)S(1)}, bf16[80,256]{1,0:T(8,128)(2,1)S(1)}, u32[]{:S(2)}, u32[]{:S(2)}) collective-permute-start(bf16[80,256]{1,0:T(8,128)(2,1)S(1)} %get-tuple-element.75), channel_id=1, source_target_pairs={{0,2},{1,3},{2,0},{3,1},{4,6},{5,7},{6,4},{7,5},{8,10},{9,11},{10,... | collective-permute-start | bytes 122888 | tf_op jit(solution)/shard_map/ppermute | solution.py:306

commit v6 on v5

--- a/solution.py
+++ b/solution.py
@@ -322,7 +322,7 @@
     return keep + partial, sums + (halves[:2] + halves[2:])
 
 
-def reduce_by_halves(keeps, sends, sums):
+def reduce_by_halves(keeps, sends, sums, row_operands):
     seg_count = lax.axis_size("seg")
     got = [swap(send, "seg", 1) for send in sends]
     added = [add_packed(*part) for part in zip(keeps, sums, got)]
@@ -366,27 +366,24 @@
         total = total + packed[:part_rows]
         halves = packed[part_rows:].reshape(2, 2, width)
         sums = sums + (halves[0] + halves[1])
-    return total, sums
-
-
-def split_rows(sums, width):
-    rows = [
-        sums[row : row + 1, col : col + width]
-        for row in range(sums.shape[0])
-        for col in range(0, sums.shape[1], width)
-    ]
-    rows = jnp.concatenate(rows, 0)
-    high = rows.astype(jnp.bfloat16).astype(jnp.float32)
-    return rows, jnp.concatenate([high, rows - high], 0)
+    return total, sums, row_grads(*row_operands)
+
+
+def side_by_side(sums):
+    sides = []
+    for row in range(sums.shape[0]):
+        pieces = [sums[row : row + 1, at : at + DH] for at in range(0, sums.shape[1], DH)]
+        sides.append(jnp.concatenate(pieces, 0))
+    return jnp.concatenate(sides, 1)
 
 
 def plane_kernel(chunk_count, *refs):
     keep_refs, got_refs, sum_refs = (refs[n * chunk_count : (n + 1) * chunk_count] for n in range(3))
     own_ref, sums_ref, send_y_ref, send_x_ref, send_xy_ref = refs[3 * chunk_count :]
-    part_rows, width = own_ref.shape
+    part_rows = keep_refs[0].shape[1]
+    cols = own_ref.shape[1]
     upper = lax.axis_index("seg") // 2 == 1
     right = lax.axis_index("dp") % 2 == 1
-    cols = 2 * width // lax.axis_size("dp")
     starts = [sum(ref.shape[1] for ref in sum_refs[:n]) for n in range(chunk_count)]
 
     def columns(start):
@@ -401,47 +398,34 @@
     for pair in range(lax.axis_size("dp") // 2):
         mine_left, other_left = columns(2 * pair * cols)
         mine_right, other_right = columns((2 * pair + 1) * cols)
-        at = slice(pair * cols, (pair + 1) * cols)
-        rows = slice(0, part_rows)
-        own_ref[:, at] = jnp.where(right, mine_right, mine_left)
-        send_x_ref[rows, at] = jnp.where(right, mine_left, mine_right).astype(jnp.bfloat16)
-        send_y_ref[rows, at] = jnp.where(right, other_right, other_left).astype(jnp.bfloat16)
-        send_xy_ref[rows, at] = jnp.where(right, other_left, other_right).astype(jnp.bfloat16)
+        rows = slice(pair * part_rows, (pair + 1) * part_rows)
+        own_ref[rows] = jnp.where(right, mine_right, mine_left)
+        send_x_ref[rows] = jnp.where(right, mine_left, mine_right).astype(jnp.bfloat16)
+        send_y_ref[rows] = jnp.where(right, other_right, other_left).astype(jnp.bfloat16)
+        send_xy_ref[rows] = jnp.where(right, other_left, other_right).astype(jnp.bfloat16)
     halves = [ref[2 * part_rows : 2 * part_rows + 4].astype(jnp.float32) for ref in got_refs]
     sums = [ref[...] + (half[:2] + half[2:]) for ref, half in zip(sum_refs, halves)]
-    sums, tail = split_rows(jnp.concatenate(sums, 1), width)
-    sums_ref[...] = sums
+    rows = side_by_side(jnp.concatenate(sums, 1))
+    sums_ref[...] = rows
     for ref in (send_y_ref, send_x_ref, send_xy_ref):
-        ref[part_rows:, :] = tail.astype(jnp.bfloat16)
+        ref[own_ref.shape[0] :] = rows.astype(jnp.bfloat16)
 
 
 def line_kernel(own_ref, sums_ref, *refs):
     got_refs, (total_ref, rows_ref, *send_refs) = refs[:3], refs[3:]
     part_rows, cols = total_ref.shape
     place = lax.axis_index("dp") // 2
-    count = own_ref.shape[1] // cols
+    count = own_ref.shape[0] // part_rows
     blocks = []
     for n in range(count):
-        at = slice(n * cols, (n + 1) * cols)
-        block = own_ref[:, at]
+        at = slice(n * part_rows, (n + 1) * part_rows)
+        block = own_ref[at]
         for ref in got_refs:
-            block = block + ref[:part_rows, at].astype(jnp.float32)
+            block = block + ref[at].astype(jnp.float32)
         blocks.append(block)
-    sums = sums_ref[...]
+    rows = sums_ref[...]
     for ref in got_refs:
-        halves = ref[part_rows:, :].astype(jnp.float32)
-        sums = sums + (halves[: sums.shape[0]] + halves[sums.shape[0] :])
-    lanes = cols // 2
-    half = sums.shape[0] // 2
-    rows = []
-    for side in (sums[:half], sums[half:]):
-        pieces = [
-            side[row : row + 1, col : col + lanes]
-            for row in range(half)
-            for col in range(0, side.shape[1], lanes)
-        ]
-        rows.append(jnp.concatenate(pieces, 0))
-    rows = jnp.concatenate(rows, 1)
+        rows = rows + ref[own_ref.shape[0] :].astype(jnp.float32)
     rows_ref[...] = rows
     for distance, ref in zip(range(count), (total_ref, *send_refs)):
         block = blocks[distance]
@@ -475,32 +459,34 @@
     )(*operands)
 
 
-def reduce_by_planes(keeps, sends, sums):
+def reduce_by_planes(keeps, sends, sums, row_operands):
     dp_count = lax.axis_size("dp")
     got = [swap(send, "seg", 1) for send in sends]
     part_rows = keeps[0].shape[1]
     width = sum(keep.shape[2] for keep in keeps)
-    half = width // 2
-    tail = 2 * 2 * width // half
-    send = ((part_rows + tail, half), jnp.bfloat16)
+    cols = width // dp_count
+    peers = dp_count // 2
+    tail = width // DH
+    own_rows = peers * part_rows
+    send = ((own_rows + tail, cols), jnp.bfloat16)
     own, plane_sums, *sends = whole_call(
         functools.partial(plane_kernel, len(keeps)),
         "plane_parts",
-        [((part_rows, half), jnp.float32), ((tail // 2, half), jnp.float32), send, send, send],
+        [((own_rows, cols), jnp.float32), ((tail, cols), jnp.float32), send, send, send],
         *keeps,
         *got,
         *sums,
     )
+    own, row_operands = lax.optimization_barrier((own, row_operands))
+    rows = row_grads(*row_operands)
     got = [
         swap_both(sends[2], 2, 1),
         swap_both(sends[0], 2, 0),
         swap_both(sends[1], 0, 1),
     ]
-    cols = width // dp_count
-    tail = 2 * width // cols
+    own, rows = lax.optimization_barrier((own, rows))
     send = ((part_rows + tail, cols), jnp.bfloat16)
-    peers = dp_count // 2
-    total, rows, *sends = whole_call(
+    total, bias_rows, *sends = whole_call(
         line_kernel,
         "line_parts",
         [((part_rows, cols), jnp.float32), ((tail, cols), jnp.float32)] + [send] * (peers - 1),
@@ -511,9 +497,9 @@
     got = [swap(sends[distance - 1], "dp", 2 * distance) for distance in (2, 3, 1)]
     side = ((tail, cols // 2), jnp.float32)
     total, *sums = whole_call(
-        last_kernel, "last_sums", [((part_rows, cols), jnp.float32), side, side], total, rows, *got
-    )
-    return total, [half.reshape(width) for half in sums]
+        last_kernel, "last_sums", [((part_rows, cols), jnp.float32), side, side], total, bias_rows, *got
+    )
+    return total, [half.reshape(width) for half in sums], rows
 
 
 def swap_both(block, seg_flip, dp_flip):
@@ -544,10 +530,11 @@
         score_grads(start, span, shared, block) for (start, span), block in zip(edges, value_memory)
     ]
     grads, grads_rel, keeps, sends, sums = zip(*parts)
-    planes = lax.axis_size("seg") == 4 and lax.axis_size("dp") == 8
+    cols = width // lax.axis_size("dp")
+    planes = lax.axis_size("seg") == 4 and lax.axis_size("dp") == 8 and cols == 2 * DH
     reduce = reduce_by_planes if planes else reduce_by_halves
-    total, sums = reduce(keeps, sends, sums)
-    d_query, d_key = row_grads(grads, grads_rel, q_content, own_k, key_memory, rel_keys)
+    row_operands = grads, grads_rel, q_content, own_k, key_memory, rel_keys
+    total, sums, (d_query, d_key) = reduce(keeps, sends, sums, row_operands)
     return (d_query[None], d_key[None], total, sums[0], sums[1])
 
 

time: 38.7 us -> 38.4 us (level)
  waiting for transfers between devices: 13.6 us -> 13.2 us
    ppermute x3, waiting for transfers between devices: 7.07 us -> 4.58 us  [swap_both(): return lax.ppermute(block, ('seg', 'dp'), route)]
    ppermute x6, waiting for transfers between devices: 3.22 us -> 5.34 us  [swap(): lax.ppermute(block, axis, [(i, i ^ flip) for i in range(lax.axis_size(axi...]
  transfers between devices with their start and end apart: 13 -> 13, of which waited for: 9 -> 10; matrix products, arithmetic and copies ran while one was open for 5% -> 5% of each run, Pallas kernels for 24% -> 25%
where the time goes in v6:
time: 38.4 us; the launch traced here: 38.2 us
  waiting for transfers between devices  13.2 us (34%)
  starting transfers between devices  11.9 us (31%)
  Pallas kernels  10.3 us (27%)
  local copies, waits for them, and re-layouts  1.96 us (5%)
  between operations  0.71 us (2%)
    pallas_call x8, Pallas kernels, whole_call(): pl.pallas_call(kernel, name=name, out_shape=[jax.ShapeDtypeStruct(*shape)...  7.03 us
    ppermute x6, waiting for transfers between devices, swap(): lax.ppermute(block, axis, [(i, i ^ flip) for i in range(lax.axis_size(axi...  5.34 us
    ppermute x6, starting transfers between devices, swap(): lax.ppermute(block, axis, [(i, i ^ flip) for i in range(lax.axis_size(axi...  4.69 us
    ppermute x3, waiting for transfers between devices, swap_both(): return lax.ppermute(block, ('seg', 'dp'), route)  4.58 us
    ppermute x3, starting transfers between devices, swap_both(): return lax.ppermute(block, ('seg', 'dp'), route)  3.93 us
    ppermute x4, waiting for transfers between devices, from_behind(): lax.ppermute(block, axis, [(i, (i + 1) % count) for i in range(count)])  3.33 us
    ppermute x4, starting transfers between devices, from_behind(): lax.ppermute(block, axis, [(i, (i + 1) % count) for i in range(count)])  3.32 us
    pallas_call x1, Pallas kernels, local_scores(): pl.pallas_call(local_kernel, name='local_scores', in_specs=[stays] * 7, o...  3.3 us
  transfers between devices with their start and end apart: 13, of which 10 were waited for; matrix products, arithmetic and copies ran while one was open for 5% of the time, Pallas kernels for 25%

profile of v6, /device:TPU:0, one launch (start us, length us, event | category | flops | bytes accessed | tf_op | source)
XLA Modules:
  0.0 38.2 jit_solution(10275680616254230118)
XLA Ops:
  0.6 0.5 %collective-permute-start = (bf16[128,2048]{1,0:T(8,128)(2,1)}, bf16[128,2048]{1,0:T(8,128)(2,1)S(1)}, u32[]{:S(2)}, u32[]{:S(2)}) collective-permute-start(bf16[128,2048]{1,0:T(8,128)(2,1)} %bitcast.19), channel_id=1, source_target_pairs={{0,8},{8,16},{16,24},{24,0},{1,9},{9,17},{17,25},{25,1},{2,10},{10... | collective-permute-start | bytes 1572872 | tf_op jit(solution)/shard_map/ppermute | solution.py:302
  1.1 1.0 %slice_bitcast_fusion = (bf16[128,768]{1,0:T(8,128)(2,1)S(1)}, bf16[128,768]{1,0:T(8,128)(2,1)S(1)}) fusion(bf16[1,128,2048]{2,1,0:T(8,128)(2,1)} %param.9), kind=kLoop, calls=%fused_computation | loop fusion | bytes 786432 | tf_op jit(solution)/shard_map/squeeze | solution.py:521
  2.2 2.7 %collective-permute-start.2 = (bf16[128,768]{1,0:T(8,128)(2,1)S(1)}, bf16[128,768]{1,0:T(8,128)(2,1)S(1)}, u32[]{:S(2)}, u32[]{:S(2)}) collective-permute-start(bf16[128,768]{1,0:T(8,128)(2,1)S(1)} %get-tuple-element.107), channel_id=1, source_target_pairs={{0,8},{8,16},{16,24},{24,0},{1,9},{9,17},{17,25},{25,1},{2,10},{10... | collective-permute-start | bytes 589832 | tf_op jit(solution)/shard_map/ppermute | solution.py:302
  4.9 0.1 collective-permute-start.1
  4.9 0.9 %slice_bitcast_fusion.2 = bf16[128,512]{1,0:T(8,128)(2,1)S(1)} fusion(bf16[1,128,2048]{2,1,0:T(8,128)(2,1)} %param.9), kind=kLoop, calls=%fused_computation.2 | loop fusion | bytes 262144 | tf_op jit(solution)/shard_map/squeeze | solution.py:521
  5.8 0.1 collective-permute-start.3
  5.9 3.3 %local_scores.1 = (f32[16,128,256]{2,1,0:T(8,128)S(1)}, bf16[128,2048]{1,0:T(8,128)(2,1)S(1)}, bf16[128,2048]{1,0:T(8,128)(2,1)S(1)}, bf16[128,2048]{1,0:T(8,128...) custom-call(bf16[128,2048]{1,0:T(8,128)(2,1)} %bitcast.17, ...), custom_call_target="tpu_custom_call" | custom-call | tf_op jit(solution)/shard_map/local_scores/pallas_call | solution.py:239
  9.2 0.9 %collective-permute-done.k_mem_ref.refs_8_ = bf16[128,2048]{1,0:T(8,128)(2,1)S(1)} collective-permute-done((bf16[128,2048]{1,0:T(8,128)(2,1)}, bf16[128,2048]{1,0:T(8,128)(2,1)S(1)}, u32[]{:S(2)}, u32[]{:S(2)}) %collective-permute-start) | collective-permute-done | bytes 524320 | tf_op jit(solution)/shard_map/ppermute | solution.py:302
  10.2 0.9 %soft_weights.1.weights_ref = f32[16,128,256]{2,1,0:T(8,128)S(1)} custom-call(f32[16,128,256]{2,1,0:T(8,128)S(1)} %get-tuple-element.56.score_ref, bf16[128,2048]{1,0:T(8,128)(2,1)S(1)} %get-tuple-element.86.content_ref.refs_6_, bf16[128,2048]{1,0:T(8,128)(2,1)S(1)} %collective-permute-done.k_mem_ref.refs_8_), custom_call_target="tpu_custom_call" | custom-call | tf_op jit(solution)/shard_map/soft_weights/pallas_call | solution.py:454
  11.1 1.2 %collective-permute-done.2.v_mem_ref = bf16[128,768]{1,0:T(8,128)(2,1)S(1)} collective-permute-done((bf16[128,768]{1,0:T(8,128)(2,1)S(1)}, bf16[128,768]{1,0:T(8,128)(2,1)S(1)}, u32[]{:S(2)}, u32[]{:S(2)}) %collective-permute-start.2) | collective-permute-done | bytes 196640 | tf_op jit(solution)/shard_map/ppermute | solution.py:302
  12.3 1.1 %score_grads.4 = (bf16[6,128,256]{2,1,0:T(8,128)(2,1)S(1)}, bf16[6,128,256]{2,1,0:T(8,128)(2,1)S(1)}, f32[2,64,768]{2,1,0:T(8,128)S(1)}, bf16[136,768]{1,0:T(8,128)(2,1)S(1)}, f32[2,768]{1,0:T(2,128)S(1)}) custom-call(f32[16,128,256]{2,1,0:T(8,128)S(1)} %soft_weights.1.weights_ref, bf16[128,2048]{1,0:T(8,128)(2,1)S(1)} %get-tuple-element.58.flipped_ref, ...), custom_call_target="tpu_custom_call" | custom-call | tf_op jit(solution)/shard_map/score_grads/pallas_call | solution.py:454
  13.3 0.1 collective-permute-start.5
  13.4 1.0 %collective-permute-done.1.v_mem_ref = bf16[128,768]{1,0:T(8,128)(2,1)S(1)} collective-permute-done((bf16[128,768]{1,0:T(8,128)(2,1)S(1)}, bf16[128,768]{1,0:T(8,128)(2,1)S(1)}, u32[]{:S(2)}, u32[]{:S(2)}) %collective-permute-start.1) | collective-permute-done | bytes 196640 | tf_op jit(solution)/shard_map/ppermute | solution.py:302
  14.4 1.1 %score_grads.3 = (bf16[6,128,256]{2,1,0:T(8,128)(2,1)S(1)}, bf16[6,128,256]{2,1,0:T(8,128)(2,1)S(1)}, f32[2,64,768]{2,1,0:T(8,128)S(1)}, bf16[136,768]{1,0:T(8,128)(2,1)S(1)}, f32[2,768]{1,0:T(2,128)S(1)}) custom-call(f32[16,128,256]{2,1,0:T(8,128)S(1)} %soft_weights.1.weights_ref, bf16[128,2048]{1,0:T(8,128)(2,1)S(1)} %get-tuple-element.58.flipped_ref, ...), custom_call_target="tpu_custom_call" | custom-call | tf_op jit(solution)/shard_map/score_grads/pallas_call | solution.py:454
  15.5 0.1 collective-permute-start.4
  15.5 0.3 collective-permute-done.3.v_mem_ref
  15.8 0.9 %score_grads.5 = (bf16[4,128,256]{2,1,0:T(8,128)(2,1)S(1)}, bf16[4,128,256]{2,1,0:T(8,128)(2,1)S(1)}, f32[2,64,512]{2,1,0:T(8,128)S(1)}, bf16[136,512]{1,0:T(8,128)(2,1)S(1)}, f32[2,512]{1,0:T(2,128)S(1)}) custom-call(f32[16,128,256]{2,1,0:T(8,128)S(1)} %soft_weights.1.weights_ref, bf16[128,2048]{1,0:T(8,128)(2,1)S(1)} %get-tuple-element.58.flipped_ref, ...), custom_call_target="tpu_custom_call" | custom-call | tf_op jit(solution)/shard_map/score_grads/pallas_call | solution.py:454
  16.7 0.3 collective-permute-start.6
  17.0 1.1 %collective-permute-done.6.refs_5_ = bf16[136,512]{1,0:T(8,128)(2,1)S(1)} collective-permute-done((bf16[136,512]{1,0:T(8,128)(2,1)S(1)}, bf16[136,512]{1,0:T(8,128)(2,1)S(1)}, u32[]{:S(2)}, u32[]{:S(2)}) %collective-permute-start.6) | collective-permute-done | bytes 139296 | tf_op jit(solution)/shard_map/ppermute | solution.py:306
  18.1 0.0 collective-permute-done.5.refs_4_
  18.1 0.0 collective-permute-done.4.refs_3_
  18.1 0.2 plane_parts.1
  18.3 3.3 %collective-permute-start.7 = (bf16[272,256]{1,0:T(8,128)(2,1)S(1)}, bf16[272,256]{1,0:T(8,128)(2,1)S(1)}, u32[]{:S(2)}, u32[]{:S(2)}) collective-permute-start(bf16[272,256]{1,0:T(8,128)(2,1)S(1)} %get-tuple-element.96), channel_id=1, source_target_pairs={{0,17},{1,16},{2,19},{3,18},{4,21},{5,20},{6,23},{7,22},{8,25},{9,... | collective-permute-start | bytes 417800 | tf_op jit(solution)/shard_map/ppermute | solution.py:512
  21.6 0.5 %collective-permute-start.8 = (bf16[272,256]{1,0:T(8,128)(2,1)S(1)}, bf16[272,256]{1,0:T(8,128)(2,1)S(1)}, u32[]{:S(2)}, u32[]{:S(2)}) collective-permute-start(bf16[272,256]{1,0:T(8,128)(2,1)S(1)} %get-tuple-element.97), channel_id=1, source_target_pairs={{0,16},{1,17},{2,18},{3,19},{4,20},{5,21},{6,22},{7,23},{8,24},{9,... | collective-permute-start | bytes 417800 | tf_op jit(solution)/shard_map/ppermute | solution.py:512
  22.1 0.1 collective-permute-start.9
  22.3 2.1 %row_grads.1 = (bf16[128,2048]{1,0:T(8,128)(2,1)}, bf16[128,2048]{1,0:T(8,128)(2,1)}) custom-call(bf16[6,128,256]{2,1,0:T(8,128)(2,1)S(1)} %get-tuple-element.80.refs_0_, bf16[6,128,256]{2,1,0:T(8,128)(2,1)S(1)} %get-tuple-element.81.refs_1_, bf16[4,128,256]{2,1,0:T(8,128)(2,1)S(1)} %get-tuple-element.82.refs_2_, ...), custom_call_target="tpu_custom_call" | custom-call | tf_op jit(solution)/shard_map/row_grads/pallas_call | solution.py:454
  24.4 1.6 %collective-permute-done.7.refs_0_ = bf16[272,256]{1,0:T(8,128)(2,1)S(1)} collective-permute-done((bf16[272,256]{1,0:T(8,128)(2,1)S(1)}, bf16[272,256]{1,0:T(8,128)(2,1)S(1)}, u32[]{:S(2)}, u32[]{:S(2)}) %collective-permute-start.7) | collective-permute-done | bytes 139296 | tf_op jit(solution)/shard_map/ppermute | solution.py:512
  26.0 2.7 %collective-permute-done.8.refs_1_ = bf16[272,256]{1,0:T(8,128)(2,1)S(1)} collective-permute-done((bf16[272,256]{1,0:T(8,128)(2,1)S(1)}, bf16[272,256]{1,0:T(8,128)(2,1)S(1)}, u32[]{:S(2)}, u32[]{:S(2)}) %collective-permute-start.8) | collective-permute-done | bytes 139296 | tf_op jit(solution)/shard_map/ppermute | solution.py:512
  28.7 0.3 collective-permute-done.9.refs_2_
  29.0 0.1 line_parts.1
  29.1 2.7 %collective-permute-start.10 = (bf16[80,256]{1,0:T(8,128)(2,1)S(1)}, bf16[80,256]{1,0:T(8,128)(2,1)S(1)}, u32[]{:S(2)}, u32[]{:S(2)}) collective-permute-start(bf16[80,256]{1,0:T(8,128)(2,1)S(1)} %get-tuple-element.101), channel_id=1, source_target_pairs={{0,4},{1,5},{2,6},{3,7},{4,0},{5,1},{6,2},{7,3},{8,12},{9,13},{10,... | collective-permute-start | bytes 122888 | tf_op jit(solution)/shard_map/ppermute | solution.py:306
  31.7 1.3 %collective-permute-start.11 = (bf16[80,256]{1,0:T(8,128)(2,1)S(1)}, bf16[80,256]{1,0:T(8,128)(2,1)S(1)}, u32[]{:S(2)}, u32[]{:S(2)}) collective-permute-start(bf16[80,256]{1,0:T(8,128)(2,1)S(1)} %get-tuple-element.102), channel_id=1, source_target_pairs={{0,6},{1,7},{2,4},{3,5},{4,2},{5,3},{6,0},{7,1},{8,14},{9,15},{10,... | collective-permute-start | bytes 122888 | tf_op jit(solution)/shard_map/ppermute | solution.py:306
  33.1 0.2 collective-permute-start.12
  33.3 1.1 %collective-permute-done.10.refs_0_ = bf16[80,256]{1,0:T(8,128)(2,1)S(1)} collective-permute-done((bf16[80,256]{1,0:T(8,128)(2,1)S(1)}, bf16[80,256]{1,0:T(8,128)(2,1)S(1)}, u32[]{:S(2)}, u32[]{:S(2)}) %collective-permute-start.10) | collective-permute-done | bytes 40992 | tf_op jit(solution)/shard_map/ppermute | solution.py:306
  34.5 3.1 %collective-permute-done.11.refs_1_ = bf16[80,256]{1,0:T(8,128)(2,1)S(1)} collective-permute-done((bf16[80,256]{1,0:T(8,128)(2,1)S(1)}, bf16[80,256]{1,0:T(8,128)(2,1)S(1)}, u32[]{:S(2)}, u32[]{:S(2)}) %collective-permute-start.11) | collective-permute-done | bytes 40992 | tf_op jit(solution)/shard_map/ppermute | solution.py:306
  37.5 0.0 collective-permute-done.12.refs_2_
  37.5 0.7 %last_sums.1 = (f32[64,256]{1,0:T(8,128)}, f32[16,128]{1,0:T(8,128)}, f32[16,128]{1,0:T(8,128)}) custom-call(f32[64,256]{1,0:T(8,128)S(1)} %get-tuple-element.99.total_ref, f32[16,256]{1,0:T(8,128)S(1)} %get-tuple-element.100.rows_ref, bf16[80,256]{1,0:T(8,128)(2,1)S(1)} %collective-permute-done.10.refs_0_, ...), custom_call_target="tpu_custom_call" | custom-call | tf_op jit(solution)/shard_map/last_sums/pallas_call | solution.py:454
Async XLA Ops:
  0.6 9.5 %collective-permute-start = (bf16[128,2048]{1,0:T(8,128)(2,1)}, bf16[128,2048]{1,0:T(8,128)(2,1)S(1)}, u32[]{:S(2)}, u32[]{:S(2)}) collective-permute-start(bf16[128,2048]{1,0:T(8,128)(2,1)} %bitcast.19), channel_id=1, source_target_pairs={{0,8},{8,16},{16,24},{24,0},{1,9},{9,17},{17,25},{25,1},{2,10},{10... | collective-permute-start | bytes 1572872 | tf_op jit(solution)/shard_map/ppermute | solution.py:302
  2.2 10.1 %collective-permute-start.2 = (bf16[128,768]{1,0:T(8,128)(2,1)S(1)}, bf16[128,768]{1,0:T(8,128)(2,1)S(1)}, u32[]{:S(2)}, u32[]{:S(2)}) collective-permute-start(bf16[128,768]{1,0:T(8,128)(2,1)S(1)} %get-tuple-element.107), channel_id=1, source_target_pairs={{0,8},{8,16},{16,24},{24,0},{1,9},{9,17},{17,25},{25,1},{2,10},{10... | collective-permute-start | bytes 589832 | tf_op jit(solution)/shard_map/ppermute | solution.py:302
  4.9 9.5 %collective-permute-start.1 = (bf16[128,768]{1,0:T(8,128)(2,1)S(1)}, bf16[128,768]{1,0:T(8,128)(2,1)S(1)}, u32[]{:S(2)}, u32[]{:S(2)}) collective-permute-start(bf16[128,768]{1,0:T(8,128)(2,1)S(1)} %get-tuple-element.108), channel_id=1, source_target_pairs={{0,8},{8,16},{16,24},{24,0},{1,9},{9,17},{17,25},{25,1},{2,10},{10... | collective-permute-start | bytes 589832 | tf_op jit(solution)/shard_map/ppermute | solution.py:302
  5.8 9.9 %collective-permute-start.3 = (bf16[128,512]{1,0:T(8,128)(2,1)S(1)}, bf16[128,512]{1,0:T(8,128)(2,1)S(1)}, u32[]{:S(2)}, u32[]{:S(2)}) collective-permute-start(bf16[128,512]{1,0:T(8,128)(2,1)S(1)} %slice_bitcast_fusion.2), channel_id=1, source_target_pairs={{0,8},{8,16},{16,24},{24,0},{1,9},{9,17},{17,25},{25,1},{2,10},{10... | collective-permute-start | bytes 393224 | tf_op jit(solution)/shard_map/ppermute | solution.py:302
  13.3 4.8 %collective-permute-start.5 = (bf16[136,768]{1,0:T(8,128)(2,1)S(1)}, bf16[136,768]{1,0:T(8,128)(2,1)S(1)}, u32[]{:S(2)}, u32[]{:S(2)}) collective-permute-start(bf16[136,768]{1,0:T(8,128)(2,1)S(1)} %get-tuple-element.67), channel_id=1, source_target_pairs={{0,8},{8,0},{16,24},{24,16},{1,9},{9,1},{17,25},{25,17},{2,10},{10... | collective-permute-start | bytes 626696 | tf_op jit(solution)/shard_map/ppermute | solution.py:306
  15.5 2.7 %collective-permute-start.4 = (bf16[136,768]{1,0:T(8,128)(2,1)S(1)}, bf16[136,768]{1,0:T(8,128)(2,1)S(1)}, u32[]{:S(2)}, u32[]{:S(2)}) collective-permute-start(bf16[136,768]{1,0:T(8,128)(2,1)S(1)} %get-tuple-element.66), channel_id=1, source_target_pairs={{0,8},{8,0},{16,24},{24,16},{1,9},{9,1},{17,25},{25,17},{2,10},{10... | collective-permute-start | bytes 626696 | tf_op jit(solution)/shard_map/ppermute | solution.py:306
  16.7 1.4 %collective-permute-start.6 = (bf16[136,512]{1,0:T(8,128)(2,1)S(1)}, bf16[136,512]{1,0:T(8,128)(2,1)S(1)}, u32[]{:S(2)}, u32[]{:S(2)}) collective-permute-start(bf16[136,512]{1,0:T(8,128)(2,1)S(1)} %get-tuple-element.68), channel_id=1, source_target_pairs={{0,8},{8,0},{16,24},{24,16},{1,9},{9,1},{17,25},{25,17},{2,10},{10... | collective-permute-start | bytes 417800 | tf_op jit(solution)/shard_map/ppermute | solution.py:306
  18.3 7.7 %collective-permute-start.7 = (bf16[272,256]{1,0:T(8,128)(2,1)S(1)}, bf16[272,256]{1,0:T(8,128)(2,1)S(1)}, u32[]{:S(2)}, u32[]{:S(2)}) collective-permute-start(bf16[272,256]{1,0:T(8,128)(2,1)S(1)} %get-tuple-element.96), channel_id=1, source_target_pairs={{0,17},{1,16},{2,19},{3,18},{4,21},{5,20},{6,23},{7,22},{8,25},{9,... | collective-permute-start | bytes 417800 | tf_op jit(solution)/shard_map/ppermute | solution.py:512
  21.6 7.1 %collective-permute-start.8 = (bf16[272,256]{1,0:T(8,128)(2,1)S(1)}, bf16[272,256]{1,0:T(8,128)(2,1)S(1)}, u32[]{:S(2)}, u32[]{:S(2)}) collective-permute-start(bf16[272,256]{1,0:T(8,128)(2,1)S(1)} %get-tuple-element.97), channel_id=1, source_target_pairs={{0,16},{1,17},{2,18},{3,19},{4,20},{5,21},{6,22},{7,23},{8,24},{9,... | collective-permute-start | bytes 417800 | tf_op jit(solution)/shard_map/ppermute | solution.py:512
  22.1 6.9 %collective-permute-start.9 = (bf16[272,256]{1,0:T(8,128)(2,1)S(1)}, bf16[272,256]{1,0:T(8,128)(2,1)S(1)}, u32[]{:S(2)}, u32[]{:S(2)}) collective-permute-start(bf16[272,256]{1,0:T(8,128)(2,1)S(1)} %get-tuple-element.98), channel_id=1, source_target_pairs={{0,1},{1,0},{2,3},{3,2},{4,5},{5,4},{6,7},{7,6},{8,9},{9,8},{10,11... | collective-permute-start | bytes 417800 | tf_op jit(solution)/shard_map/ppermute | solution.py:512
  29.1 5.4 %collective-permute-start.10 = (bf16[80,256]{1,0:T(8,128)(2,1)S(1)}, bf16[80,256]{1,0:T(8,128)(2,1)S(1)}, u32[]{:S(2)}, u32[]{:S(2)}) collective-permute-start(bf16[80,256]{1,0:T(8,128)(2,1)S(1)} %get-tuple-element.101), channel_id=1, source_target_pairs={{0,4},{1,5},{2,6},{3,7},{4,0},{5,1},{6,2},{7,3},{8,12},{9,13},{10,... | collective-permute-start | bytes 122888 | tf_op jit(solution)/shard_map/ppermute | solution.py:306
  31.7 5.8 %collective-permute-start.11 = (bf16[80,256]{1,0:T(8,128)(2,1)S(1)}, bf16[80,256]{1,0:T(8,128)(2,1)S(1)}, u32[]{:S(2)}, u32[]{:S(2)}) collective-permute-start(bf16[80,256]{1,0:T(8,128)(2,1)S(1)} %get-tuple-element.102), channel_id=1, source_target_pairs={{0,6},{1,7},{2,4},{3,5},{4,2},{5,3},{6,0},{7,1},{8,14},{9,15},{10,... | collective-permute-start | bytes 122888 | tf_op jit(solution)/shard_map/ppermute | solution.py:306
  33.1 4.5 %collective-permute-start.12 = (bf16[80,256]{1,0:T(8,128)(2,1)S(1)}, bf16[80,256]{1,0:T(8,128)(2,1)S(1)}, u32[]{:S(2)}, u32[]{:S(2)}) collective-permute-start(bf16[80,256]{1,0:T(8,128)(2,1)S(1)} %get-tuple-element.103), channel_id=1, source_target_pairs={{0,2},{1,3},{2,0},{3,1},{4,6},{5,7},{6,4},{7,5},{8,10},{9,11},{10,... | collective-permute-start | bytes 122888 | tf_op jit(solution)/shard_map/ppermute | solution.py:306

commit v7 on v6

--- a/solution.py
+++ b/solution.py
@@ -42,6 +42,7 @@
     v_ref,
     d_out_ref,
     q_ref,
+    d_raw_ref,
     bias_u_ref,
     bias_v_ref,
     head_sems,
@@ -68,7 +69,7 @@
         )
     rest = [
         pltpu.make_async_copy(v_hbm, v_ref, rest_sems.at[0]),
-        pltpu.make_async_copy(d_out_hbm, d_out_ref, rest_sems.at[1]),
+        pltpu.make_async_copy(d_out_hbm, d_raw_ref, rest_sems.at[1]),
     ]
     copies[0] = biases + copies[0]
     for copy in [each for part in copies for each in part] + rest:
@@ -76,7 +77,7 @@
     first_key = jnp.where(lax.axis_index("seg") > 0, 0, mem_len)
     row_index = lax.broadcasted_iota(jnp.int32, (seg_rows, key_count), 0)
     key_index = lax.broadcasted_iota(jnp.int32, (seg_rows, key_count), 1)
-    allowed = (key_index <= row_index + mem_len) & (key_index >= first_key)
+    allowed = (row_index + key_index < key_count) & (key_index >= first_key)
     flip = row_flip(seg_rows)
     for group, part in zip(groups, copies):
         for copy in part:
@@ -87,21 +88,38 @@
         q_position = [(wide[t] + bias_v_ref[:, cols[t]]).astype(jnp.bfloat16) for t in n]
         by_distance = [contract(q_position[t], rel_ref[:, cols[t]], 1, 1) for t in n]
         q_content = [(wide[t] + bias_u_ref[:, cols[t]]).astype(jnp.bfloat16) for t in n]
+        q_content = [contract(flip, each, 1, 0).astype(jnp.bfloat16) for each in q_content]
         content = [contract(q_content[t], k_ref[:, cols[t]], 1, 1) for t in n]
-        flipped = [contract(flip, q_position[t], 1, 0).astype(jnp.bfloat16) for t in n]
+        q_position = [contract(flip, each, 1, 0).astype(jnp.bfloat16) for each in q_position]
         position = [
             pltpu.roll(raw, key_count - seg_rows + 1, 1, stride=1, stride_axis=0)
             for raw in by_distance
         ]
+        position = [flip_exactly(flip, each) for each in position]
         for t in n:
             scores = jnp.concatenate(
                 [position[t][:, :mem_len], position[t][:, mem_len:] + content[t]], 1
             )
             score_ref[group[t]] = jnp.where(allowed, SCORE_SCALE * LOG2_E * scores, -1e30)
             content_ref[:, cols[t]] = q_content[t]
-            flipped_ref[:, cols[t]] = flipped[t]
+            flipped_ref[:, cols[t]] = q_position[t]
     for copy in rest:
         copy.wait()
+    d_out_ref[...] = contract(flip, d_raw_ref[...], 1, 0).astype(jnp.bfloat16)
+
+
+def bf16_parts(wide):
+    parts = []
+    for _ in range(3):
+        part = wide.astype(jnp.bfloat16)
+        wide = wide - part.astype(jnp.float32)
+        parts.append(part)
+    return parts
+
+
+def flip_exactly(flip, wide):
+    high, middle, low = (contract(flip, part, 1, 0) for part in bf16_parts(wide))
+    return (high + middle) + low
 
 
 def weights_kernel(score_ref, content_ref, k_mem_ref, weights_ref):
@@ -135,10 +153,8 @@
     send_ref,
     bias_ref,
 ):
-    seg_rows = k_ref.shape[0]
     pair_count, part_rows, _ = keep_ref.shape
     odd = jnp.bitwise_and(lax.axis_index("seg"), 1) == 1
-    flip = row_flip(seg_rows)
     fill = jnp.zeros((BIAS_ROWS - 4, DH), jnp.bfloat16)
     for group in head_groups(start, v_mem_ref.shape[1]):
         cols = columns_of(group)
@@ -151,12 +167,12 @@
         scaled = [weights_ref[group[t]] * d_weights[t] for t in n]
         mean = [jnp.sum(each, axis=1, keepdims=True) * (1.0 / SCORE_SCALE) for each in scaled]
         grad = [(weights_ref[group[t]] * (d_weights[t] - mean[t])).astype(jnp.bfloat16) for t in n]
-        flipped = [contract(flip, each, 1, 0) for each in grad]
-        rolled = [pltpu.roll(each, 0, 1, stride=1, stride_axis=0) for each in flipped]
+        grad_wide = [each.astype(jnp.float32) for each in grad]
+        rolled = [pltpu.roll(each, 0, 1, stride=1, stride_axis=0) for each in grad_wide]
         grad_rel = [each.astype(jnp.bfloat16) for each in rolled]
         d_rel_all = [contract(grad_rel[t], flipped_ref[:, cols[t]], 0, 0) for t in n]
         keys_all = [jnp.concatenate([k_mem_ref[:, c], k_ref[:, c]], 0) for c in cols]
-        content = [row_sum_product(flipped[t], keys_all[t]) for t in n]
+        content = [row_sum_product(grad_wide[t], keys_all[t]) for t in n]
         position = [row_sum_product(rolled[t], rel_ref[:, cols[t]]) for t in n]
         for t in n:
             c = own[t]
@@ -178,12 +194,7 @@
 
 
 def row_sum_product(left, right):
-    rest = jnp.sum(left, 0, keepdims=True)
-    parts = []
-    for _ in range(3):
-        part = rest.astype(jnp.bfloat16)
-        rest = rest - part.astype(jnp.float32)
-        parts.append(part)
+    parts = bf16_parts(jnp.sum(left, 0, keepdims=True))
     fill = jnp.zeros((5, left.shape[1]), jnp.bfloat16)
     return jnp.sum(contract(jnp.concatenate([*parts, fill], 0), right, 1, 0), 0, keepdims=True)
 
@@ -199,16 +210,14 @@
         places = [heads[head] for head in group]
         n = range(len(cols))
         grad = [grad_refs[chunk][head] for chunk, head in places]
-        back = [
-            contract(flip, grad_rel_refs[chunk][head], 1, 0).astype(jnp.bfloat16)
-            for chunk, head in places
-        ]
+        grad_rel = [grad_rel_refs[chunk][head] for chunk, head in places]
         keys_all = [jnp.concatenate([k_mem_ref[:, c], k_ref[:, c]], 0) for c in cols]
         d_content = [contract(grad[t], keys_all[t], 1, 0) for t in n]
         d_key = [contract(grad[t][:, mem_len:], content_ref[:, cols[t]], 0, 0) for t in n]
-        d_position = [contract(back[t], rel_ref[:, cols[t]], 1, 0) for t in n]
+        d_position = [contract(grad_rel[t], rel_ref[:, cols[t]], 1, 0) for t in n]
+        d_query = [(d_content[t] + d_position[t]).astype(jnp.bfloat16) for t in n]
         for t in n:
-            d_q_ref[:, cols[t]] = (d_content[t] + d_position[t]).astype(jnp.bfloat16)
+            d_q_ref[:, cols[t]] = contract(flip, d_query[t], 1, 0).astype(jnp.bfloat16)
             d_k_ref[:, cols[t]] = d_key[t].astype(jnp.bfloat16)
 
 
@@ -243,6 +252,7 @@
         out_specs=[whole] * 7,
         out_shape=[scores, rows, rows, rows, rel, rows, rows],
         scratch_shapes=[
+            pltpu.VMEM((seg_rows, width), jnp.bfloat16),
             pltpu.VMEM((seg_rows, width), jnp.bfloat16),
             pltpu.VMEM((1, width), jnp.float32),
             pltpu.VMEM((1, width), jnp.float32),

time: 38.4 us -> 38.1 us (level)
  waiting for transfers between devices: 13.2 us -> 11.8 us
  Pallas kernels: 10.3 us -> 11.6 us
    pallas_call x1, Pallas kernels: 3.3 us -> 4.76 us  [local_scores(): pl.pallas_call(local_kernel, name='local_scores', in_specs=[stays] * 7, o...]
    ppermute x4, waiting for transfers between devices: 3.33 us -> 2.07 us  [from_behind(): lax.ppermute(block, axis, [(i, (i + 1) % count) for i in range(count)])]
  transfers between devices with their start and end apart: 13 -> 13, of which waited for: 10 -> 9; matrix products, arithmetic and copies ran while one was open for 5% -> 5% of each run, Pallas kernels for 25% -> 28%
where the time goes in v7:
time: 38.1 us; the launch traced here: 37.9 us
  starting transfers between devices  11.8 us (31%)
  waiting for transfers between devices  11.8 us (31%)
  Pallas kernels  11.6 us (30%)
  local copies, waits for them, and re-layouts  1.96 us (5%)
  between operations  0.71 us (2%)
    pallas_call x8, Pallas kernels, whole_call(): pl.pallas_call(kernel, name=name, out_shape=[jax.ShapeDtypeStruct(*shape)...  6.83 us
    ppermute x6, waiting for transfers between devices, swap(): lax.ppermute(block, axis, [(i, i ^ flip) for i in range(lax.axis_size(axi...  5.44 us
    pallas_call x1, Pallas kernels, local_scores(): pl.pallas_call(local_kernel, name='local_scores', in_specs=[stays] * 7, o...  4.76 us
    ppermute x6, starting transfers between devices, swap(): lax.ppermute(block, axis, [(i, i ^ flip) for i in range(lax.axis_size(axi...  4.59 us
    ppermute x3, waiting for transfers between devices, swap_both(): return lax.ppermute(block, ('seg', 'dp'), route)  4.28 us
    ppermute x3, starting transfers between devices, swap_both(): return lax.ppermute(block, ('seg', 'dp'), route)  3.93 us
    ppermute x4, starting transfers between devices, from_behind(): lax.ppermute(block, axis, [(i, (i + 1) % count) for i in range(count)])  3.32 us
    ppermute x4, waiting for transfers between devices, from_behind(): lax.ppermute(block, axis, [(i, (i + 1) % count) for i in range(count)])  2.07 us
  transfers between devices with their start and end apart: 13, of which 9 were waited for; matrix products, arithmetic and copies ran while one was open for 5% of the time, Pallas kernels for 28%

profile of v7, /device:TPU:0, one launch (start us, length us, event | category | flops | bytes accessed | tf_op | source)
XLA Modules:
  0.0 37.9 jit_solution(2417729742432540923)
XLA Ops:
  0.6 0.5 %collective-permute-start = (bf16[128,2048]{1,0:T(8,128)(2,1)}, bf16[128,2048]{1,0:T(8,128)(2,1)S(1)}, u32[]{:S(2)}, u32[]{:S(2)}) collective-permute-start(bf16[128,2048]{1,0:T(8,128)(2,1)} %bitcast.19), channel_id=1, source_target_pairs={{0,8},{8,16},{16,24},{24,0},{1,9},{9,17},{17,25},{25,1},{2,10},{10... | collective-permute-start | bytes 1572872 | tf_op jit(solution)/shard_map/ppermute | solution.py:312
  1.1 1.0 %slice_bitcast_fusion = (bf16[128,768]{1,0:T(8,128)(2,1)S(1)}, bf16[128,768]{1,0:T(8,128)(2,1)S(1)}) fusion(bf16[1,128,2048]{2,1,0:T(8,128)(2,1)} %param.9), kind=kLoop, calls=%fused_computation | loop fusion | bytes 786432 | tf_op jit(solution)/shard_map/squeeze | solution.py:531
  2.2 2.7 %collective-permute-start.2 = (bf16[128,768]{1,0:T(8,128)(2,1)S(1)}, bf16[128,768]{1,0:T(8,128)(2,1)S(1)}, u32[]{:S(2)}, u32[]{:S(2)}) collective-permute-start(bf16[128,768]{1,0:T(8,128)(2,1)S(1)} %get-tuple-element.107), channel_id=1, source_target_pairs={{0,8},{8,16},{16,24},{24,0},{1,9},{9,17},{17,25},{25,1},{2,10},{10... | collective-permute-start | bytes 589832 | tf_op jit(solution)/shard_map/ppermute | solution.py:312
  4.9 0.1 collective-permute-start.1
  4.9 0.9 %slice_bitcast_fusion.2 = bf16[128,512]{1,0:T(8,128)(2,1)S(1)} fusion(bf16[1,128,2048]{2,1,0:T(8,128)(2,1)} %param.9), kind=kLoop, calls=%fused_computation.2 | loop fusion | bytes 262144 | tf_op jit(solution)/shard_map/squeeze | solution.py:531
  5.8 0.1 collective-permute-start.3
  5.9 4.8 %local_scores.1 = (f32[16,128,256]{2,1,0:T(8,128)S(1)}, bf16[128,2048]{1,0:T(8,128)(2,1)S(1)}, bf16[128,2048]{1,0:T(8,128)(2,1)S(1)}, bf16[128,2048]{1,0:T(8,128...) custom-call(bf16[128,2048]{1,0:T(8,128)(2,1)} %bitcast.17, ...), custom_call_target="tpu_custom_call" | custom-call | tf_op jit(solution)/shard_map/local_scores/pallas_call | solution.py:248
  10.7 0.0 collective-permute-done.k_mem_ref.refs_8_
  10.7 0.9 %soft_weights.1.weights_ref = f32[16,128,256]{2,1,0:T(8,128)S(1)} custom-call(f32[16,128,256]{2,1,0:T(8,128)S(1)} %get-tuple-element.56.score_ref, bf16[128,2048]{1,0:T(8,128)(2,1)S(1)} %get-tuple-element.86.content_ref.refs_6_, bf16[128,2048]{1,0:T(8,128)(2,1)S(1)} %collective-permute-done.k_mem_ref.refs_8_), custom_call_target="tpu_custom_call" | custom-call | tf_op jit(solution)/shard_map/soft_weights/pallas_call | solution.py:464
  11.6 0.7 %collective-permute-done.2.v_mem_ref = bf16[128,768]{1,0:T(8,128)(2,1)S(1)} collective-permute-done((bf16[128,768]{1,0:T(8,128)(2,1)S(1)}, bf16[128,768]{1,0:T(8,128)(2,1)S(1)}, u32[]{:S(2)}, u32[]{:S(2)}) %collective-permute-start.2) | collective-permute-done | bytes 196640 | tf_op jit(solution)/shard_map/ppermute | solution.py:312
  12.3 1.0 %score_grads.4 = (bf16[6,128,256]{2,1,0:T(8,128)(2,1)S(1)}, bf16[6,128,256]{2,1,0:T(8,128)(2,1)S(1)}, f32[2,64,768]{2,1,0:T(8,128)S(1)}, bf16[136,768]{1,0:T(8,128)(2,1)S(1)}, f32[2,768]{1,0:T(2,128)S(1)}) custom-call(f32[16,128,256]{2,1,0:T(8,128)S(1)} %soft_weights.1.weights_ref, bf16[128,2048]{1,0:T(8,128)(2,1)S(1)} %get-tuple-element.58.flipped_ref, ...), custom_call_target="tpu_custom_call" | custom-call | tf_op jit(solution)/shard_map/score_grads/pallas_call | solution.py:464
  13.2 0.1 collective-permute-start.5
  13.3 1.1 %collective-permute-done.1.v_mem_ref = bf16[128,768]{1,0:T(8,128)(2,1)S(1)} collective-permute-done((bf16[128,768]{1,0:T(8,128)(2,1)S(1)}, bf16[128,768]{1,0:T(8,128)(2,1)S(1)}, u32[]{:S(2)}, u32[]{:S(2)}) %collective-permute-start.1) | collective-permute-done | bytes 196640 | tf_op jit(solution)/shard_map/ppermute | solution.py:312
  14.4 1.0 %score_grads.3 = (bf16[6,128,256]{2,1,0:T(8,128)(2,1)S(1)}, bf16[6,128,256]{2,1,0:T(8,128)(2,1)S(1)}, f32[2,64,768]{2,1,0:T(8,128)S(1)}, bf16[136,768]{1,0:T(8,128)(2,1)S(1)}, f32[2,768]{1,0:T(2,128)S(1)}) custom-call(f32[16,128,256]{2,1,0:T(8,128)S(1)} %soft_weights.1.weights_ref, bf16[128,2048]{1,0:T(8,128)(2,1)S(1)} %get-tuple-element.58.flipped_ref, ...), custom_call_target="tpu_custom_call" | custom-call | tf_op jit(solution)/shard_map/score_grads/pallas_call | solution.py:464
  15.4 0.1 collective-permute-start.4
  15.4 0.4 collective-permute-done.3.v_mem_ref
  15.8 0.7 %score_grads.5 = (bf16[4,128,256]{2,1,0:T(8,128)(2,1)S(1)}, bf16[4,128,256]{2,1,0:T(8,128)(2,1)S(1)}, f32[2,64,512]{2,1,0:T(8,128)S(1)}, bf16[136,512]{1,0:T(8,128)(2,1)S(1)}, f32[2,512]{1,0:T(2,128)S(1)}) custom-call(f32[16,128,256]{2,1,0:T(8,128)S(1)} %soft_weights.1.weights_ref, bf16[128,2048]{1,0:T(8,128)(2,1)S(1)} %get-tuple-element.58.flipped_ref, ...), custom_call_target="tpu_custom_call" | custom-call | tf_op jit(solution)/shard_map/score_grads/pallas_call | solution.py:464
  16.5 0.2 collective-permute-start.6
  16.7 1.2 %collective-permute-done.6.refs_5_ = bf16[136,512]{1,0:T(8,128)(2,1)S(1)} collective-permute-done((bf16[136,512]{1,0:T(8,128)(2,1)S(1)}, bf16[136,512]{1,0:T(8,128)(2,1)S(1)}, u32[]{:S(2)}, u32[]{:S(2)}) %collective-permute-start.6) | collective-permute-done | bytes 139296 | tf_op jit(solution)/shard_map/ppermute | solution.py:316
  17.9 0.0 collective-permute-done.5.refs_4_
  17.9 0.0 collective-permute-done.4.refs_3_
  17.9 0.2 plane_parts.1
  18.1 3.3 %collective-permute-start.7 = (bf16[272,256]{1,0:T(8,128)(2,1)S(1)}, bf16[272,256]{1,0:T(8,128)(2,1)S(1)}, u32[]{:S(2)}, u32[]{:S(2)}) collective-permute-start(bf16[272,256]{1,0:T(8,128)(2,1)S(1)} %get-tuple-element.96), channel_id=1, source_target_pairs={{0,17},{1,16},{2,19},{3,18},{4,21},{5,20},{6,23},{7,22},{8,25},{9,... | collective-permute-start | bytes 417800 | tf_op jit(solution)/shard_map/ppermute | solution.py:522
  21.4 0.5 %collective-permute-start.8 = (bf16[272,256]{1,0:T(8,128)(2,1)S(1)}, bf16[272,256]{1,0:T(8,128)(2,1)S(1)}, u32[]{:S(2)}, u32[]{:S(2)}) collective-permute-start(bf16[272,256]{1,0:T(8,128)(2,1)S(1)} %get-tuple-element.97), channel_id=1, source_target_pairs={{0,16},{1,17},{2,18},{3,19},{4,20},{5,21},{6,22},{7,23},{8,24},{9,... | collective-permute-start | bytes 417800 | tf_op jit(solution)/shard_map/ppermute | solution.py:522
  21.9 0.1 collective-permute-start.9
  22.1 2.3 %row_grads.1 = (bf16[128,2048]{1,0:T(8,128)(2,1)}, bf16[128,2048]{1,0:T(8,128)(2,1)}) custom-call(bf16[6,128,256]{2,1,0:T(8,128)(2,1)S(1)} %get-tuple-element.80.refs_0_, bf16[6,128,256]{2,1,0:T(8,128)(2,1)S(1)} %get-tuple-element.81.refs_1_, bf16[4,128,256]{2,1,0:T(8,128)(2,1)S(1)} %get-tuple-element.82.refs_2_, ...), custom_call_target="tpu_custom_call" | custom-call | tf_op jit(solution)/shard_map/row_grads/pallas_call | solution.py:464
  24.4 1.3 %collective-permute-done.7.refs_0_ = bf16[272,256]{1,0:T(8,128)(2,1)S(1)} collective-permute-done((bf16[272,256]{1,0:T(8,128)(2,1)S(1)}, bf16[272,256]{1,0:T(8,128)(2,1)S(1)}, u32[]{:S(2)}, u32[]{:S(2)}) %collective-permute-start.7) | collective-permute-done | bytes 139296 | tf_op jit(solution)/shard_map/ppermute | solution.py:522
  25.7 2.7 %collective-permute-done.8.refs_1_ = bf16[272,256]{1,0:T(8,128)(2,1)S(1)} collective-permute-done((bf16[272,256]{1,0:T(8,128)(2,1)S(1)}, bf16[272,256]{1,0:T(8,128)(2,1)S(1)}, u32[]{:S(2)}, u32[]{:S(2)}) %collective-permute-start.8) | collective-permute-done | bytes 139296 | tf_op jit(solution)/shard_map/ppermute | solution.py:522
  28.4 0.3 collective-permute-done.9.refs_2_
  28.7 0.1 line_parts.1
  28.8 2.7 %collective-permute-start.10 = (bf16[80,256]{1,0:T(8,128)(2,1)S(1)}, bf16[80,256]{1,0:T(8,128)(2,1)S(1)}, u32[]{:S(2)}, u32[]{:S(2)}) collective-permute-start(bf16[80,256]{1,0:T(8,128)(2,1)S(1)} %get-tuple-element.101), channel_id=1, source_target_pairs={{0,4},{1,5},{2,6},{3,7},{4,0},{5,1},{6,2},{7,3},{8,12},{9,13},{10,... | collective-permute-start | bytes 122888 | tf_op jit(solution)/shard_map/ppermute | solution.py:316
  31.4 1.3 %collective-permute-start.11 = (bf16[80,256]{1,0:T(8,128)(2,1)S(1)}, bf16[80,256]{1,0:T(8,128)(2,1)S(1)}, u32[]{:S(2)}, u32[]{:S(2)}) collective-permute-start(bf16[80,256]{1,0:T(8,128)(2,1)S(1)} %get-tuple-element.102), channel_id=1, source_target_pairs={{0,6},{1,7},{2,4},{3,5},{4,2},{5,3},{6,0},{7,1},{8,14},{9,15},{10,... | collective-permute-start | bytes 122888 | tf_op jit(solution)/shard_map/ppermute | solution.py:316
  32.8 0.2 collective-permute-start.12
  33.0 1.1 %collective-permute-done.10.refs_0_ = bf16[80,256]{1,0:T(8,128)(2,1)S(1)} collective-permute-done((bf16[80,256]{1,0:T(8,128)(2,1)S(1)}, bf16[80,256]{1,0:T(8,128)(2,1)S(1)}, u32[]{:S(2)}, u32[]{:S(2)}) %collective-permute-start.10) | collective-permute-done | bytes 40992 | tf_op jit(solution)/shard_map/ppermute | solution.py:316
  34.1 3.1 %collective-permute-done.11.refs_1_ = bf16[80,256]{1,0:T(8,128)(2,1)S(1)} collective-permute-done((bf16[80,256]{1,0:T(8,128)(2,1)S(1)}, bf16[80,256]{1,0:T(8,128)(2,1)S(1)}, u32[]{:S(2)}, u32[]{:S(2)}) %collective-permute-start.11) | collective-permute-done | bytes 40992 | tf_op jit(solution)/shard_map/ppermute | solution.py:316
  37.2 0.0 collective-permute-done.12.refs_2_
  37.2 0.7 %last_sums.1 = (f32[64,256]{1,0:T(8,128)}, f32[16,128]{1,0:T(8,128)}, f32[16,128]{1,0:T(8,128)}) custom-call(f32[64,256]{1,0:T(8,128)S(1)} %get-tuple-element.99.total_ref, f32[16,256]{1,0:T(8,128)S(1)} %get-tuple-element.100.rows_ref, bf16[80,256]{1,0:T(8,128)(2,1)S(1)} %collective-permute-done.10.refs_0_, ...), custom_call_target="tpu_custom_call" | custom-call | tf_op jit(solution)/shard_map/last_sums/pallas_call | solution.py:464
Async XLA Ops:
  0.6 10.1 %collective-permute-start = (bf16[128,2048]{1,0:T(8,128)(2,1)}, bf16[128,2048]{1,0:T(8,128)(2,1)S(1)}, u32[]{:S(2)}, u32[]{:S(2)}) collective-permute-start(bf16[128,2048]{1,0:T(8,128)(2,1)} %bitcast.19), channel_id=1, source_target_pairs={{0,8},{8,16},{16,24},{24,0},{1,9},{9,17},{17,25},{25,1},{2,10},{10... | collective-permute-start | bytes 1572872 | tf_op jit(solution)/shard_map/ppermute | solution.py:312
  2.2 10.1 %collective-permute-start.2 = (bf16[128,768]{1,0:T(8,128)(2,1)S(1)}, bf16[128,768]{1,0:T(8,128)(2,1)S(1)}, u32[]{:S(2)}, u32[]{:S(2)}) collective-permute-start(bf16[128,768]{1,0:T(8,128)(2,1)S(1)} %get-tuple-element.107), channel_id=1, source_target_pairs={{0,8},{8,16},{16,24},{24,0},{1,9},{9,17},{17,25},{25,1},{2,10},{10... | collective-permute-start | bytes 589832 | tf_op jit(solution)/shard_map/ppermute | solution.py:312
  4.9 9.5 %collective-permute-start.1 = (bf16[128,768]{1,0:T(8,128)(2,1)S(1)}, bf16[128,768]{1,0:T(8,128)(2,1)S(1)}, u32[]{:S(2)}, u32[]{:S(2)}) collective-permute-start(bf16[128,768]{1,0:T(8,128)(2,1)S(1)} %get-tuple-element.108), channel_id=1, source_target_pairs={{0,8},{8,16},{16,24},{24,0},{1,9},{9,17},{17,25},{25,1},{2,10},{10... | collective-permute-start | bytes 589832 | tf_op jit(solution)/shard_map/ppermute | solution.py:312
  5.8 9.9 %collective-permute-start.3 = (bf16[128,512]{1,0:T(8,128)(2,1)S(1)}, bf16[128,512]{1,0:T(8,128)(2,1)S(1)}, u32[]{:S(2)}, u32[]{:S(2)}) collective-permute-start(bf16[128,512]{1,0:T(8,128)(2,1)S(1)} %slice_bitcast_fusion.2), channel_id=1, source_target_pairs={{0,8},{8,16},{16,24},{24,0},{1,9},{9,17},{17,25},{25,1},{2,10},{10... | collective-permute-start | bytes 393224 | tf_op jit(solution)/shard_map/ppermute | solution.py:312
  13.2 4.7 %collective-permute-start.5 = (bf16[136,768]{1,0:T(8,128)(2,1)S(1)}, bf16[136,768]{1,0:T(8,128)(2,1)S(1)}, u32[]{:S(2)}, u32[]{:S(2)}) collective-permute-start(bf16[136,768]{1,0:T(8,128)(2,1)S(1)} %get-tuple-element.67), channel_id=1, source_target_pairs={{0,8},{8,0},{16,24},{24,16},{1,9},{9,1},{17,25},{25,17},{2,10},{10... | collective-permute-start | bytes 626696 | tf_op jit(solution)/shard_map/ppermute | solution.py:316
  15.4 2.6 %collective-permute-start.4 = (bf16[136,768]{1,0:T(8,128)(2,1)S(1)}, bf16[136,768]{1,0:T(8,128)(2,1)S(1)}, u32[]{:S(2)}, u32[]{:S(2)}) collective-permute-start(bf16[136,768]{1,0:T(8,128)(2,1)S(1)} %get-tuple-element.66), channel_id=1, source_target_pairs={{0,8},{8,0},{16,24},{24,16},{1,9},{9,1},{17,25},{25,17},{2,10},{10... | collective-permute-start | bytes 626696 | tf_op jit(solution)/shard_map/ppermute | solution.py:316
  16.5 1.4 %collective-permute-start.6 = (bf16[136,512]{1,0:T(8,128)(2,1)S(1)}, bf16[136,512]{1,0:T(8,128)(2,1)S(1)}, u32[]{:S(2)}, u32[]{:S(2)}) collective-permute-start(bf16[136,512]{1,0:T(8,128)(2,1)S(1)} %get-tuple-element.68), channel_id=1, source_target_pairs={{0,8},{8,0},{16,24},{24,16},{1,9},{9,1},{17,25},{25,17},{2,10},{10... | collective-permute-start | bytes 417800 | tf_op jit(solution)/shard_map/ppermute | solution.py:316
  18.1 7.6 %collective-permute-start.7 = (bf16[272,256]{1,0:T(8,128)(2,1)S(1)}, bf16[272,256]{1,0:T(8,128)(2,1)S(1)}, u32[]{:S(2)}, u32[]{:S(2)}) collective-permute-start(bf16[272,256]{1,0:T(8,128)(2,1)S(1)} %get-tuple-element.96), channel_id=1, source_target_pairs={{0,17},{1,16},{2,19},{3,18},{4,21},{5,20},{6,23},{7,22},{8,25},{9,... | collective-permute-start | bytes 417800 | tf_op jit(solution)/shard_map/ppermute | solution.py:522
  21.4 7.0 %collective-permute-start.8 = (bf16[272,256]{1,0:T(8,128)(2,1)S(1)}, bf16[272,256]{1,0:T(8,128)(2,1)S(1)}, u32[]{:S(2)}, u32[]{:S(2)}) collective-permute-start(bf16[272,256]{1,0:T(8,128)(2,1)S(1)} %get-tuple-element.97), channel_id=1, source_target_pairs={{0,16},{1,17},{2,18},{3,19},{4,20},{5,21},{6,22},{7,23},{8,24},{9,... | collective-permute-start | bytes 417800 | tf_op jit(solution)/shard_map/ppermute | solution.py:522
  21.9 6.8 %collective-permute-start.9 = (bf16[272,256]{1,0:T(8,128)(2,1)S(1)}, bf16[272,256]{1,0:T(8,128)(2,1)S(1)}, u32[]{:S(2)}, u32[]{:S(2)}) collective-permute-start(bf16[272,256]{1,0:T(8,128)(2,1)S(1)} %get-tuple-element.98), channel_id=1, source_target_pairs={{0,1},{1,0},{2,3},{3,2},{4,5},{5,4},{6,7},{7,6},{8,9},{9,8},{10,11... | collective-permute-start | bytes 417800 | tf_op jit(solution)/shard_map/ppermute | solution.py:522
  28.8 5.4 %collective-permute-start.10 = (bf16[80,256]{1,0:T(8,128)(2,1)S(1)}, bf16[80,256]{1,0:T(8,128)(2,1)S(1)}, u32[]{:S(2)}, u32[]{:S(2)}) collective-permute-start(bf16[80,256]{1,0:T(8,128)(2,1)S(1)} %get-tuple-element.101), channel_id=1, source_target_pairs={{0,4},{1,5},{2,6},{3,7},{4,0},{5,1},{6,2},{7,3},{8,12},{9,13},{10,... | collective-permute-start | bytes 122888 | tf_op jit(solution)/shard_map/ppermute | solution.py:316
  31.4 5.8 %collective-permute-start.11 = (bf16[80,256]{1,0:T(8,128)(2,1)S(1)}, bf16[80,256]{1,0:T(8,128)(2,1)S(1)}, u32[]{:S(2)}, u32[]{:S(2)}) collective-permute-start(bf16[80,256]{1,0:T(8,128)(2,1)S(1)} %get-tuple-element.102), channel_id=1, source_target_pairs={{0,6},{1,7},{2,4},{3,5},{4,2},{5,3},{6,0},{7,1},{8,14},{9,15},{10,... | collective-permute-start | bytes 122888 | tf_op jit(solution)/shard_map/ppermute | solution.py:316
  32.8 4.5 %collective-permute-start.12 = (bf16[80,256]{1,0:T(8,128)(2,1)S(1)}, bf16[80,256]{1,0:T(8,128)(2,1)S(1)}, u32[]{:S(2)}, u32[]{:S(2)}) collective-permute-start(bf16[80,256]{1,0:T(8,128)(2,1)S(1)} %get-tuple-element.103), channel_id=1, source_target_pairs={{0,2},{1,3},{2,0},{3,1},{4,6},{5,7},{6,4},{7,5},{8,10},{9,11},{10,... | collective-permute-start | bytes 122888 | tf_op jit(solution)/shard_map/ppermute | solution.py:316

commit v8 on v7

--- a/solution.py
+++ b/solution.py
@@ -504,7 +504,7 @@
         plane_sums,
         *got,
     )
-    got = [swap(sends[distance - 1], "dp", 2 * distance) for distance in (2, 3, 1)]
+    got = [swap(sends[distance - 1], "dp", 2 * distance) for distance in (3, 2, 1)]
     side = ((tail, cols // 2), jnp.float32)
     total, *sums = whole_call(
         last_kernel, "last_sums", [((part_rows, cols), jnp.float32), side, side], total, bias_rows, *got

time: 38.1 us -> 38.2 us (level)
  no operation moved by 1% of the time
where the time goes in v8:
time: 38.2 us; the launch traced here: 38 us
  starting transfers between devices  12.1 us (32%)
  waiting for transfers between devices  11.7 us (31%)
  Pallas kernels  11.6 us (30%)
  local copies, waits for them, and re-layouts  1.96 us (5%)
  between operations  0.71 us (2%)
    pallas_call x8, Pallas kernels, whole_call(): pl.pallas_call(kernel, name=name, out_shape=[jax.ShapeDtypeStruct(*shape)...  6.83 us
    ppermute x6, waiting for transfers between devices, swap(): lax.ppermute(block, axis, [(i, i ^ flip) for i in range(lax.axis_size(axi...  5.34 us
    ppermute x6, starting transfers between devices, swap(): lax.ppermute(block, axis, [(i, i ^ flip) for i in range(lax.axis_size(axi...  4.81 us
    pallas_call x1, Pallas kernels, local_scores(): pl.pallas_call(local_kernel, name='local_scores', in_specs=[stays] * 7, o...  4.76 us
    ppermute x3, waiting for transfers between devices, swap_both(): return lax.ppermute(block, ('seg', 'dp'), route)  4.28 us
    ppermute x3, starting transfers between devices, swap_both(): return lax.ppermute(block, ('seg', 'dp'), route)  3.93 us
    ppermute x4, starting transfers between devices, from_behind(): lax.ppermute(block, axis, [(i, (i + 1) % count) for i in range(count)])  3.32 us
    ppermute x4, waiting for transfers between devices, from_behind(): lax.ppermute(block, axis, [(i, (i + 1) % count) for i in range(count)])  2.07 us
  transfers between devices with their start and end apart: 13, of which 9 were waited for; matrix products, arithmetic and copies ran while one was open for 5% of the time, Pallas kernels for 28%

profile of v8, /device:TPU:0, one launch (start us, length us, event | category | flops | bytes accessed | tf_op | source)
XLA Modules:
  0.0 38.0 jit_solution(5953057108822057848)
XLA Ops:
  0.6 0.5 %collective-permute-start = (bf16[128,2048]{1,0:T(8,128)(2,1)}, bf16[128,2048]{1,0:T(8,128)(2,1)S(1)}, u32[]{:S(2)}, u32[]{:S(2)}) collective-permute-start(bf16[128,2048]{1,0:T(8,128)(2,1)} %bitcast.19), channel_id=1, source_target_pairs={{0,8},{8,16},{16,24},{24,0},{1,9},{9,17},{17,25},{25,1},{2,10},{10... | collective-permute-start | bytes 1572872 | tf_op jit(solution)/shard_map/ppermute | solution.py:312
  1.1 1.0 %slice_bitcast_fusion = (bf16[128,768]{1,0:T(8,128)(2,1)S(1)}, bf16[128,768]{1,0:T(8,128)(2,1)S(1)}) fusion(bf16[1,128,2048]{2,1,0:T(8,128)(2,1)} %param.9), kind=kLoop, calls=%fused_computation | loop fusion | bytes 786432 | tf_op jit(solution)/shard_map/squeeze | solution.py:531
  2.2 2.7 %collective-permute-start.2 = (bf16[128,768]{1,0:T(8,128)(2,1)S(1)}, bf16[128,768]{1,0:T(8,128)(2,1)S(1)}, u32[]{:S(2)}, u32[]{:S(2)}) collective-permute-start(bf16[128,768]{1,0:T(8,128)(2,1)S(1)} %get-tuple-element.107), channel_id=1, source_target_pairs={{0,8},{8,16},{16,24},{24,0},{1,9},{9,17},{17,25},{25,1},{2,10},{10... | collective-permute-start | bytes 589832 | tf_op jit(solution)/shard_map/ppermute | solution.py:312
  4.9 0.1 collective-permute-start.1
  4.9 0.9 %slice_bitcast_fusion.2 = bf16[128,512]{1,0:T(8,128)(2,1)S(1)} fusion(bf16[1,128,2048]{2,1,0:T(8,128)(2,1)} %param.9), kind=kLoop, calls=%fused_computation.2 | loop fusion | bytes 262144 | tf_op jit(solution)/shard_map/squeeze | solution.py:531
  5.8 0.1 collective-permute-start.3
  5.9 4.8 %local_scores.1 = (f32[16,128,256]{2,1,0:T(8,128)S(1)}, bf16[128,2048]{1,0:T(8,128)(2,1)S(1)}, bf16[128,2048]{1,0:T(8,128)(2,1)S(1)}, bf16[128,2048]{1,0:T(8,128...) custom-call(bf16[128,2048]{1,0:T(8,128)(2,1)} %bitcast.17, ...), custom_call_target="tpu_custom_call" | custom-call | tf_op jit(solution)/shard_map/local_scores/pallas_call | solution.py:248
  10.7 0.0 collective-permute-done.k_mem_ref.refs_8_
  10.7 0.9 %soft_weights.1.weights_ref = f32[16,128,256]{2,1,0:T(8,128)S(1)} custom-call(f32[16,128,256]{2,1,0:T(8,128)S(1)} %get-tuple-element.56.score_ref, bf16[128,2048]{1,0:T(8,128)(2,1)S(1)} %get-tuple-element.86.content_ref.refs_6_, bf16[128,2048]{1,0:T(8,128)(2,1)S(1)} %collective-permute-done.k_mem_ref.refs_8_), custom_call_target="tpu_custom_call" | custom-call | tf_op jit(solution)/shard_map/soft_weights/pallas_call | solution.py:464
  11.6 0.7 %collective-permute-done.2.v_mem_ref = bf16[128,768]{1,0:T(8,128)(2,1)S(1)} collective-permute-done((bf16[128,768]{1,0:T(8,128)(2,1)S(1)}, bf16[128,768]{1,0:T(8,128)(2,1)S(1)}, u32[]{:S(2)}, u32[]{:S(2)}) %collective-permute-start.2) | collective-permute-done | bytes 196640 | tf_op jit(solution)/shard_map/ppermute | solution.py:312
  12.3 1.0 %score_grads.4 = (bf16[6,128,256]{2,1,0:T(8,128)(2,1)S(1)}, bf16[6,128,256]{2,1,0:T(8,128)(2,1)S(1)}, f32[2,64,768]{2,1,0:T(8,128)S(1)}, bf16[136,768]{1,0:T(8,128)(2,1)S(1)}, f32[2,768]{1,0:T(2,128)S(1)}) custom-call(f32[16,128,256]{2,1,0:T(8,128)S(1)} %soft_weights.1.weights_ref, bf16[128,2048]{1,0:T(8,128)(2,1)S(1)} %get-tuple-element.58.flipped_ref, ...), custom_call_target="tpu_custom_call" | custom-call | tf_op jit(solution)/shard_map/score_grads/pallas_call | solution.py:464
  13.2 0.1 collective-permute-start.5
  13.3 1.1 %collective-permute-done.1.v_mem_ref = bf16[128,768]{1,0:T(8,128)(2,1)S(1)} collective-permute-done((bf16[128,768]{1,0:T(8,128)(2,1)S(1)}, bf16[128,768]{1,0:T(8,128)(2,1)S(1)}, u32[]{:S(2)}, u32[]{:S(2)}) %collective-permute-start.1) | collective-permute-done | bytes 196640 | tf_op jit(solution)/shard_map/ppermute | solution.py:312
  14.4 1.0 %score_grads.3 = (bf16[6,128,256]{2,1,0:T(8,128)(2,1)S(1)}, bf16[6,128,256]{2,1,0:T(8,128)(2,1)S(1)}, f32[2,64,768]{2,1,0:T(8,128)S(1)}, bf16[136,768]{1,0:T(8,128)(2,1)S(1)}, f32[2,768]{1,0:T(2,128)S(1)}) custom-call(f32[16,128,256]{2,1,0:T(8,128)S(1)} %soft_weights.1.weights_ref, bf16[128,2048]{1,0:T(8,128)(2,1)S(1)} %get-tuple-element.58.flipped_ref, ...), custom_call_target="tpu_custom_call" | custom-call | tf_op jit(solution)/shard_map/score_grads/pallas_call | solution.py:464
  15.4 0.1 collective-permute-start.4
  15.4 0.4 collective-permute-done.3.v_mem_ref
  15.8 0.7 %score_grads.5 = (bf16[4,128,256]{2,1,0:T(8,128)(2,1)S(1)}, bf16[4,128,256]{2,1,0:T(8,128)(2,1)S(1)}, f32[2,64,512]{2,1,0:T(8,128)S(1)}, bf16[136,512]{1,0:T(8,128)(2,1)S(1)}, f32[2,512]{1,0:T(2,128)S(1)}) custom-call(f32[16,128,256]{2,1,0:T(8,128)S(1)} %soft_weights.1.weights_ref, bf16[128,2048]{1,0:T(8,128)(2,1)S(1)} %get-tuple-element.58.flipped_ref, ...), custom_call_target="tpu_custom_call" | custom-call | tf_op jit(solution)/shard_map/score_grads/pallas_call | solution.py:464
  16.5 0.2 collective-permute-start.6
  16.7 1.2 %collective-permute-done.6.refs_5_ = bf16[136,512]{1,0:T(8,128)(2,1)S(1)} collective-permute-done((bf16[136,512]{1,0:T(8,128)(2,1)S(1)}, bf16[136,512]{1,0:T(8,128)(2,1)S(1)}, u32[]{:S(2)}, u32[]{:S(2)}) %collective-permute-start.6) | collective-permute-done | bytes 139296 | tf_op jit(solution)/shard_map/ppermute | solution.py:316
  17.9 0.0 collective-permute-done.5.refs_4_
  17.9 0.0 collective-permute-done.4.refs_3_
  17.9 0.2 plane_parts.1
  18.1 3.3 %collective-permute-start.7 = (bf16[272,256]{1,0:T(8,128)(2,1)S(1)}, bf16[272,256]{1,0:T(8,128)(2,1)S(1)}, u32[]{:S(2)}, u32[]{:S(2)}) collective-permute-start(bf16[272,256]{1,0:T(8,128)(2,1)S(1)} %get-tuple-element.96), channel_id=1, source_target_pairs={{0,17},{1,16},{2,19},{3,18},{4,21},{5,20},{6,23},{7,22},{8,25},{9,... | collective-permute-start | bytes 417800 | tf_op jit(solution)/shard_map/ppermute | solution.py:522
  21.4 0.5 %collective-permute-start.8 = (bf16[272,256]{1,0:T(8,128)(2,1)S(1)}, bf16[272,256]{1,0:T(8,128)(2,1)S(1)}, u32[]{:S(2)}, u32[]{:S(2)}) collective-permute-start(bf16[272,256]{1,0:T(8,128)(2,1)S(1)} %get-tuple-element.97), channel_id=1, source_target_pairs={{0,16},{1,17},{2,18},{3,19},{4,20},{5,21},{6,22},{7,23},{8,24},{9,... | collective-permute-start | bytes 417800 | tf_op jit(solution)/shard_map/ppermute | solution.py:522
  21.9 0.1 collective-permute-start.9
  22.1 2.3 %row_grads.1 = (bf16[128,2048]{1,0:T(8,128)(2,1)}, bf16[128,2048]{1,0:T(8,128)(2,1)}) custom-call(bf16[6,128,256]{2,1,0:T(8,128)(2,1)S(1)} %get-tuple-element.80.refs_0_, bf16[6,128,256]{2,1,0:T(8,128)(2,1)S(1)} %get-tuple-element.81.refs_1_, bf16[4,128,256]{2,1,0:T(8,128)(2,1)S(1)} %get-tuple-element.82.refs_2_, ...), custom_call_target="tpu_custom_call" | custom-call | tf_op jit(solution)/shard_map/row_grads/pallas_call | solution.py:464
  24.4 1.3 %collective-permute-done.7.refs_0_ = bf16[272,256]{1,0:T(8,128)(2,1)S(1)} collective-permute-done((bf16[272,256]{1,0:T(8,128)(2,1)S(1)}, bf16[272,256]{1,0:T(8,128)(2,1)S(1)}, u32[]{:S(2)}, u32[]{:S(2)}) %collective-permute-start.7) | collective-permute-done | bytes 139296 | tf_op jit(solution)/shard_map/ppermute | solution.py:522
  25.7 2.7 %collective-permute-done.8.refs_1_ = bf16[272,256]{1,0:T(8,128)(2,1)S(1)} collective-permute-done((bf16[272,256]{1,0:T(8,128)(2,1)S(1)}, bf16[272,256]{1,0:T(8,128)(2,1)S(1)}, u32[]{:S(2)}, u32[]{:S(2)}) %collective-permute-start.8) | collective-permute-done | bytes 139296 | tf_op jit(solution)/shard_map/ppermute | solution.py:522
  28.4 0.3 collective-permute-done.9.refs_2_
  28.7 0.1 line_parts.1
  28.8 3.7 %collective-permute-start.10 = (bf16[80,256]{1,0:T(8,128)(2,1)S(1)}, bf16[80,256]{1,0:T(8,128)(2,1)S(1)}, u32[]{:S(2)}, u32[]{:S(2)}) collective-permute-start(bf16[80,256]{1,0:T(8,128)(2,1)S(1)} %get-tuple-element.101), channel_id=1, source_target_pairs={{0,6},{1,7},{2,4},{3,5},{4,2},{5,3},{6,0},{7,1},{8,14},{9,15},{10,... | collective-permute-start | bytes 122888 | tf_op jit(solution)/shard_map/ppermute | solution.py:316
  32.5 0.0 collective-permute-start.11
  32.5 0.8 %collective-permute-start.12 = (bf16[80,256]{1,0:T(8,128)(2,1)S(1)}, bf16[80,256]{1,0:T(8,128)(2,1)S(1)}, u32[]{:S(2)}, u32[]{:S(2)}) collective-permute-start(bf16[80,256]{1,0:T(8,128)(2,1)S(1)} %get-tuple-element.103), channel_id=1, source_target_pairs={{0,2},{1,3},{2,0},{3,1},{4,6},{5,7},{6,4},{7,5},{8,10},{9,11},{10,... | collective-permute-start | bytes 122888 | tf_op jit(solution)/shard_map/ppermute | solution.py:316
  33.2 1.6 %collective-permute-done.10.refs_0_ = bf16[80,256]{1,0:T(8,128)(2,1)S(1)} collective-permute-done((bf16[80,256]{1,0:T(8,128)(2,1)S(1)}, bf16[80,256]{1,0:T(8,128)(2,1)S(1)}, u32[]{:S(2)}, u32[]{:S(2)}) %collective-permute-start.10) | collective-permute-done | bytes 40992 | tf_op jit(solution)/shard_map/ppermute | solution.py:316
  34.8 2.5 %collective-permute-done.11.refs_1_ = bf16[80,256]{1,0:T(8,128)(2,1)S(1)} collective-permute-done((bf16[80,256]{1,0:T(8,128)(2,1)S(1)}, bf16[80,256]{1,0:T(8,128)(2,1)S(1)}, u32[]{:S(2)}, u32[]{:S(2)}) %collective-permute-start.11) | collective-permute-done | bytes 40992 | tf_op jit(solution)/shard_map/ppermute | solution.py:316
  37.4 0.0 collective-permute-done.12.refs_2_
  37.4 0.7 %last_sums.1 = (f32[64,256]{1,0:T(8,128)}, f32[16,128]{1,0:T(8,128)}, f32[16,128]{1,0:T(8,128)}) custom-call(f32[64,256]{1,0:T(8,128)S(1)} %get-tuple-element.99.total_ref, f32[16,256]{1,0:T(8,128)S(1)} %get-tuple-element.100.rows_ref, bf16[80,256]{1,0:T(8,128)(2,1)S(1)} %collective-permute-done.10.refs_0_, ...), custom_call_target="tpu_custom_call" | custom-call | tf_op jit(solution)/shard_map/last_sums/pallas_call | solution.py:464
Async XLA Ops:
  0.6 10.1 %collective-permute-start = (bf16[128,2048]{1,0:T(8,128)(2,1)}, bf16[128,2048]{1,0:T(8,128)(2,1)S(1)}, u32[]{:S(2)}, u32[]{:S(2)}) collective-permute-start(bf16[128,2048]{1,0:T(8,128)(2,1)} %bitcast.19), channel_id=1, source_target_pairs={{0,8},{8,16},{16,24},{24,0},{1,9},{9,17},{17,25},{25,1},{2,10},{10... | collective-permute-start | bytes 1572872 | tf_op jit(solution)/shard_map/ppermute | solution.py:312
  2.2 10.1 %collective-permute-start.2 = (bf16[128,768]{1,0:T(8,128)(2,1)S(1)}, bf16[128,768]{1,0:T(8,128)(2,1)S(1)}, u32[]{:S(2)}, u32[]{:S(2)}) collective-permute-start(bf16[128,768]{1,0:T(8,128)(2,1)S(1)} %get-tuple-element.107), channel_id=1, source_target_pairs={{0,8},{8,16},{16,24},{24,0},{1,9},{9,17},{17,25},{25,1},{2,10},{10... | collective-permute-start | bytes 589832 | tf_op jit(solution)/shard_map/ppermute | solution.py:312
  4.9 9.5 %collective-permute-start.1 = (bf16[128,768]{1,0:T(8,128)(2,1)S(1)}, bf16[128,768]{1,0:T(8,128)(2,1)S(1)}, u32[]{:S(2)}, u32[]{:S(2)}) collective-permute-start(bf16[128,768]{1,0:T(8,128)(2,1)S(1)} %get-tuple-element.108), channel_id=1, source_target_pairs={{0,8},{8,16},{16,24},{24,0},{1,9},{9,17},{17,25},{25,1},{2,10},{10... | collective-permute-start | bytes 589832 | tf_op jit(solution)/shard_map/ppermute | solution.py:312
  5.8 9.9 %collective-permute-start.3 = (bf16[128,512]{1,0:T(8,128)(2,1)S(1)}, bf16[128,512]{1,0:T(8,128)(2,1)S(1)}, u32[]{:S(2)}, u32[]{:S(2)}) collective-permute-start(bf16[128,512]{1,0:T(8,128)(2,1)S(1)} %slice_bitcast_fusion.2), channel_id=1, source_target_pairs={{0,8},{8,16},{16,24},{24,0},{1,9},{9,17},{17,25},{25,1},{2,10},{10... | collective-permute-start | bytes 393224 | tf_op jit(solution)/shard_map/ppermute | solution.py:312
  13.2 4.7 %collective-permute-start.5 = (bf16[136,768]{1,0:T(8,128)(2,1)S(1)}, bf16[136,768]{1,0:T(8,128)(2,1)S(1)}, u32[]{:S(2)}, u32[]{:S(2)}) collective-permute-start(bf16[136,768]{1,0:T(8,128)(2,1)S(1)} %get-tuple-element.67), channel_id=1, source_target_pairs={{0,8},{8,0},{16,24},{24,16},{1,9},{9,1},{17,25},{25,17},{2,10},{10... | collective-permute-start | bytes 626696 | tf_op jit(solution)/shard_map/ppermute | solution.py:316
  15.4 2.6 %collective-permute-start.4 = (bf16[136,768]{1,0:T(8,128)(2,1)S(1)}, bf16[136,768]{1,0:T(8,128)(2,1)S(1)}, u32[]{:S(2)}, u32[]{:S(2)}) collective-permute-start(bf16[136,768]{1,0:T(8,128)(2,1)S(1)} %get-tuple-element.66), channel_id=1, source_target_pairs={{0,8},{8,0},{16,24},{24,16},{1,9},{9,1},{17,25},{25,17},{2,10},{10... | collective-permute-start | bytes 626696 | tf_op jit(solution)/shard_map/ppermute | solution.py:316
  16.5 1.4 %collective-permute-start.6 = (bf16[136,512]{1,0:T(8,128)(2,1)S(1)}, bf16[136,512]{1,0:T(8,128)(2,1)S(1)}, u32[]{:S(2)}, u32[]{:S(2)}) collective-permute-start(bf16[136,512]{1,0:T(8,128)(2,1)S(1)} %get-tuple-element.68), channel_id=1, source_target_pairs={{0,8},{8,0},{16,24},{24,16},{1,9},{9,1},{17,25},{25,17},{2,10},{10... | collective-permute-start | bytes 417800 | tf_op jit(solution)/shard_map/ppermute | solution.py:316
  18.1 7.6 %collective-permute-start.7 = (bf16[272,256]{1,0:T(8,128)(2,1)S(1)}, bf16[272,256]{1,0:T(8,128)(2,1)S(1)}, u32[]{:S(2)}, u32[]{:S(2)}) collective-permute-start(bf16[272,256]{1,0:T(8,128)(2,1)S(1)} %get-tuple-element.96), channel_id=1, source_target_pairs={{0,17},{1,16},{2,19},{3,18},{4,21},{5,20},{6,23},{7,22},{8,25},{9,... | collective-permute-start | bytes 417800 | tf_op jit(solution)/shard_map/ppermute | solution.py:522
  21.4 7.0 %collective-permute-start.8 = (bf16[272,256]{1,0:T(8,128)(2,1)S(1)}, bf16[272,256]{1,0:T(8,128)(2,1)S(1)}, u32[]{:S(2)}, u32[]{:S(2)}) collective-permute-start(bf16[272,256]{1,0:T(8,128)(2,1)S(1)} %get-tuple-element.97), channel_id=1, source_target_pairs={{0,16},{1,17},{2,18},{3,19},{4,20},{5,21},{6,22},{7,23},{8,24},{9,... | collective-permute-start | bytes 417800 | tf_op jit(solution)/shard_map/ppermute | solution.py:522
  21.9 6.8 %collective-permute-start.9 = (bf16[272,256]{1,0:T(8,128)(2,1)S(1)}, bf16[272,256]{1,0:T(8,128)(2,1)S(1)}, u32[]{:S(2)}, u32[]{:S(2)}) collective-permute-start(bf16[272,256]{1,0:T(8,128)(2,1)S(1)} %get-tuple-element.98), channel_id=1, source_target_pairs={{0,1},{1,0},{2,3},{3,2},{4,5},{5,4},{6,7},{7,6},{8,9},{9,8},{10,11... | collective-permute-start | bytes 417800 | tf_op jit(solution)/shard_map/ppermute | solution.py:522
  28.8 6.0 %collective-permute-start.10 = (bf16[80,256]{1,0:T(8,128)(2,1)S(1)}, bf16[80,256]{1,0:T(8,128)(2,1)S(1)}, u32[]{:S(2)}, u32[]{:S(2)}) collective-permute-start(bf16[80,256]{1,0:T(8,128)(2,1)S(1)} %get-tuple-element.101), channel_id=1, source_target_pairs={{0,6},{1,7},{2,4},{3,5},{4,2},{5,3},{6,0},{7,1},{8,14},{9,15},{10,... | collective-permute-start | bytes 122888 | tf_op jit(solution)/shard_map/ppermute | solution.py:316
  32.5 4.9 %collective-permute-start.11 = (bf16[80,256]{1,0:T(8,128)(2,1)S(1)}, bf16[80,256]{1,0:T(8,128)(2,1)S(1)}, u32[]{:S(2)}, u32[]{:S(2)}) collective-permute-start(bf16[80,256]{1,0:T(8,128)(2,1)S(1)} %get-tuple-element.102), channel_id=1, source_target_pairs={{0,4},{1,5},{2,6},{3,7},{4,0},{5,1},{6,2},{7,3},{8,12},{9,13},{10,... | collective-permute-start | bytes 122888 | tf_op jit(solution)/shard_map/ppermute | solution.py:316
  32.5 4.9 %collective-permute-start.12 = (bf16[80,256]{1,0:T(8,128)(2,1)S(1)}, bf16[80,256]{1,0:T(8,128)(2,1)S(1)}, u32[]{:S(2)}, u32[]{:S(2)}) collective-permute-start(bf16[80,256]{1,0:T(8,128)(2,1)S(1)} %get-tuple-element.103), channel_id=1, source_target_pairs={{0,2},{1,3},{2,0},{3,1},{4,6},{5,7},{6,4},{7,5},{8,10},{9,11},{10,... | collective-permute-start | bytes 122888 | tf_op jit(solution)/shard_map/ppermute | solution.py:316
